TPU v7x, 32 devices: a whole 2x2x4 slice. The times are simulated.
32 devices in a mesh: tile: 8 (over z, x), aux: 4 (over y, core).
Axes of the slice: x: 2, y: 2, z: 4, core: 2. Of those that a mesh axis runs over, the one named last changes fastest.
Arguments:
- density: float32 [1024, 1024], P('tile', 'aux'), may hold values from -6 to 6
- factors: float32 [192, 16, 128, 128], P(('tile', 'aux')), may hold values from -0.125 to 0.125
- orthogonalizers: float32 [1024, 128], replicated, may hold values from -0.5 to 0.5
- slot_pairs: int32 [1024, 2], P(('tile', 'aux')), may hold values from 0 to 5
- density_source: int32 [1024, 1], replicated, may hold values from 0 to 7; in each aligned block of 32 rows (0 to 31, 32 to 63, ...) at most 8 rows name the same one
- density_column: int32 [1024, 1], replicated, may hold values from 0 to 7
- target_row: int32 [1024, 1], replicated, may hold values from 0 to 7; in each aligned block of 32 rows (0 to 31, 32 to 63, ...) at most 8 rows name the same one
- target_column: int32 [1024, 1], replicated, may hold values from 0 to 7
Outputs:
- fock_exchange: float32 [1024, 1024], P('tile', 'aux')
Inputs may be any that keep to these rules, and one draw needn't show every extreme that they name: `density_source`: in each aligned block of 32 rows (the tasks of one device) no row tile is named more than 8 times, a bound that some block reaches. `target_row`: in each aligned block of 32 rows (the tasks of one device) no row tile is named more than 8 times, a bound that some block reaches.
All inputs are finite; a program needn't handle non-finite values.
Results may differ from a plain program's by a relative error of at most 0.0001.
Values sent between devices are 32-bit elements; how exact they have to be, the bound alone decides.
No kernel may reach another device: no remote copies, remote signals or barrier semaphores. Data moves between devices by JAX's collectives and lax.ppermute only.
A program may use at most 128 MiB of HBM per device.

v0:
```python
import jax
import jax.numpy as jnp
from jax import lax
from jax.sharding import PartitionSpec as P

highest = lax.Precision.HIGHEST


def ranks_of(key_rows):
    task_count = key_rows.shape[-1]
    position = jnp.arange(task_count)
    earlier = position[None, :] < position[:, None]
    matching = key_rows[..., :, None] == key_rows[..., None, :]
    return jnp.sum(matching & earlier, axis=-1)


def slot_table(key_rows, other_rows, wanted, capacity):
    ranking = ranks_of(key_rows)
    levels = jnp.arange(capacity)
    chosen = (key_rows == wanted)[..., None, :] & (ranking[..., None, :] == levels[:, None])
    picked = jnp.sum(jnp.where(chosen, other_rows[..., None, :], 0), axis=-1)
    filled = jnp.any(chosen, axis=-1)
    return (picked, filled)


def local(
    density,
    factors,
    orthogonalizers,
    slot_pairs,
    density_source,
    density_column,
    target_row,
    target_column,
):
    tiles_all = lax.axis_size("tile")
    aux_count = lax.axis_size("aux")
    tile_me = lax.axis_index("tile")
    aux_me = lax.axis_index("aux")
    tile_width = factors.shape[-1]
    task_count = slot_pairs.shape[0]
    capacity = max(2, 2 * task_count // tiles_all)
    quarter = tile_width // aux_count
    per_block = tiles_all // aux_count
    source_grid = density_source.reshape(tiles_all, aux_count, task_count)
    column_grid = density_column.reshape(tiles_all, aux_count, task_count)
    target_grid = target_row.reshape(tiles_all, aux_count, task_count)
    target_cols = target_column.reshape(tiles_all, aux_count, task_count)
    own_source = source_grid[tile_me, aux_me]
    own_target = target_grid[tile_me, aux_me]
    row_slab = lax.all_gather(density, "aux", axis=1, tiled=True)
    slab_tiles = row_slab.reshape(tile_width, tiles_all, tile_width)
    group_source = lax.dynamic_index_in_dim(source_grid, aux_me, 1, False)
    group_column = lax.dynamic_index_in_dim(column_grid, aux_me, 1, False)
    send_cols, send_filled = slot_table(group_source, group_column, tile_me, capacity)
    outgoing = jnp.take(slab_tiles, send_cols, axis=1)
    outgoing = jnp.where(send_filled[None, :, :, None], outgoing, 0.0)
    incoming = lax.all_to_all(outgoing, "tile", split_axis=1, concat_axis=1, tiled=True)
    own_rank = ranks_of(own_source)
    group = 8
    batches = task_count // group

    def one_batch(items):
        sources, rank_block, lefts, rights = items
        dens_block = incoming[:, sources, rank_block, :]
        halfway = jnp.einsum("gpik,kgl->gpil", factors[lefts], dens_block, precision=highest)
        return jnp.einsum("gpil,gplj->gij", halfway, factors[rights], precision=highest)

    partials = lax.map(
        one_batch,
        (
            own_source.reshape(batches, group),
            own_rank.reshape(batches, group),
            slot_pairs[:, 0].reshape(batches, group),
            slot_pairs[:, 1].reshape(batches, group),
        ),
    )
    partials = partials.reshape(task_count, tile_width, tile_width)
    task_ids = jnp.arange(task_count, dtype=jnp.int32)
    owners = jnp.arange(tiles_all, dtype=jnp.int32)[:, None]
    send_task, send_live = slot_table(own_target[None, :], task_ids[None, :], owners, capacity)
    outbound = jnp.where(send_live[:, :, None, None], partials[send_task], 0.0)
    arrived = lax.all_to_all(outbound, "tile", split_axis=0, concat_axis=0, tiled=True)
    group_target = lax.dynamic_index_in_dim(target_grid, aux_me, 1, False)
    group_cols = lax.dynamic_index_in_dim(target_cols, aux_me, 1, False)
    cols_b, cols_live = slot_table(group_target, group_cols, tile_me, capacity)
    spread = ((cols_b.reshape(-1)[None, :] == owners) & cols_live.reshape(-1)[None, :]).astype(
        jnp.float32
    )
    row_sums = jnp.einsum(
        "bs,sij->ibj", spread, arrived.reshape(-1, tile_width, tile_width), precision=highest
    )
    row_sums = row_sums.reshape(tile_width, tiles_all * tile_width)
    exchange_rows = lax.psum_scatter(row_sums, "aux", scatter_dimension=0, tiled=True)
    mirrored = lax.all_to_all(
        lax.all_to_all(
            exchange_rows.reshape(quarter, tiles_all, tile_width),
            "tile",
            split_axis=1,
            concat_axis=1,
            tiled=True,
        ),
        "aux",
        split_axis=1,
        concat_axis=0,
        tiled=True,
    )
    full_rows = lax.all_to_all(
        exchange_rows.reshape(quarter, aux_count, per_block * tile_width),
        "aux",
        split_axis=1,
        concat_axis=0,
        tiled=True,
    )
    direct_part = full_rows.reshape(tile_width, per_block, tile_width)
    symmetric = direct_part + jnp.transpose(mirrored, (2, 1, 0))
    blocks_x = orthogonalizers.reshape(tiles_all, tile_width, tile_width)
    left_x = blocks_x[tile_me]
    right_x = lax.dynamic_slice_in_dim(blocks_x, aux_me * per_block, per_block, 0)
    leftward = jnp.einsum("ki,kbl->ibl", left_x, symmetric, precision=highest)
    fock = jnp.einsum("ibl,blj->ibj", leftward, right_x, precision=highest)
    return fock.reshape(tile_width, per_block * tile_width)


def solution(mesh):
    return jax.shard_map(
        local,
        mesh=mesh,
        in_specs=(
            P("tile", "aux"),
            P(("tile", "aux"), None, None, None),
            P(),
            P(("tile", "aux"), None),
            P(),
            P(),
            P(),
            P(),
        ),
        out_specs=P("tile", "aux"),
        check_vma=False,
    )
```

profile of v0, /device:TPU:0, one launch (start us, length us, event | category | flops | bytes accessed | tf_op | source)
XLA Modules:
  0.0 460.6 jit_solution(16725498381495939168)
XLA Ops:
  6.5 0.5 broadcast.252
  7.1 1.3 reduce.27
  8.5 1.3 reduce.25
  10.0 1.3 reduce.26
  11.4 1.3 reduce.28
  12.8 0.5 convert_reduce_fusion
  13.3 0.2 select_reduce_fusion.1
  13.5 0.2 fusion.20
  13.9 1.0 copy.49
  14.9 8.7 %all_gather.3 = f32[128,1024]{0,1:T(8,128)S(1)} all-gather(f32[128,256]{0,1:T(8,128)S(1)} %copy.49), channel_id=1, replica_groups=mesh['tile'=8,'aux'=4] {'aux'}, dimensions={1}, use_global_device_ids=true | all-gather | bytes 655360 | tf_op jit(solution)/shard_map/all_gather | solution.py:51
  23.5 0.2 copy.50
  23.7 2.8 gather_fusion.3
  26.5 4.6 select_bitcast_fusion
  31.1 5.9 %all-to-all-start = ((f32[128,8,8,128]{3,0,2,1:T(8,128)}), f32[128,8,8,128]{3,0,2,1:T(8,128)}, u32[]{:S(2)}, u32[]{:S(2)}) async-start(f32[128,8,8,128]{3,0,2,1:T(8,128)} %select_bitcast_fusion), calls=%async_computation | async-start | bytes 8388608 | tf_op jit(solution)/shard_map/all_to_all | solution.py:58
  37.1 0.2 convert_reduce_fusion.2
  37.3 0.1 reshape.342
  37.5 0.1 reshape_squeeze.11
  37.6 0.2 convert_reduce_fusion.3
  37.8 0.2 fusion.18
  38.2 0.2 and_reduce_fusion
  38.4 92.5 %all-to-all-done = f32[128,8,8,128]{3,0,2,1:T(8,128)} async-done(((f32[128,8,8,128]{3,0,2,1:T(8,128)}), f32[128,8,8,128]{3,0,2,1:T(8,128)}, u32[]{:S(2)}, u32[]{:S(2)}) %all-to-all-start) | async-done | bytes 4194336 | tf_op jit(solution)/shard_map/all_to_all | solution.py:58
  130.9 159.3 %while.10 = (s32[]{:T(128)}, f32[4,8,128,128]{3,2,1,0:T(8,128)S(1)}, s32[4,8]{1,0:T(4,128)S(1)}, f32[6,16,128,128]{3,2,1,0:T(8,128)}, s32[4,8]{1,0:T(4,128)S(1)}...) while((s32[]{:T(128)}, f32[4,8,128,128]{3,2,1,0:T(8,128)S(1)}, ...), condition=%wide.region_7.8_spmd, body=%wide.region_6.7_spmd.sunk | while | flops 6442452992 | bytes 69214728 | solution.py:69
  130.9 7.1 %gather_fusion = f32[8,16,128,128]{3,2,1,0:T(8,128)} fusion(f32[6,16,128,128]{3,2,1,0:T(8,128)} %get-tuple-element.156, s32[1024]{0:T(1024)S(1)} %pad_clamp_fusion.6), kind=kCustom, calls=%fused_computation.clone.1 | custom fusion | bytes 16777248 | tf_op jit(solution)/shard_map/while/body/eval_jaxpr/gather | solution.py:66
  138.0 2.8 gather_fusion.1
  140.7 11.0 %fusion.50 = f32[8,16,128,128]{3,2,1,0:T(8,128)} fusion(f32[8,16,128,128]{3,2,1,0:T(8,128)} %gather_fusion, f32[8,128,128]{2,1,0:T(8,128)S(1)} %gather_fusion.1), kind=kOutput, calls=%fused_computation.7.clone.1 | convolution fusion | flops 3221225472 | bytes 17301504 | tf_op jit(solution)/shard_map/while/body/eval_jaxpr/gpik,kgl->gpil/dot_general | solution.py:66
  151.8 7.1 %gather_fusion.2 = f32[8,16,128,128]{3,2,1,0:T(8,128)} fusion(f32[6,16,128,128]{3,2,1,0:T(8,128)} %get-tuple-element.156, s32[1024]{0:T(1024)S(1)} %pad_clamp_fusion.7), kind=kCustom, calls=%fused_computation.2.clone.1 | custom fusion | bytes 16777248 | tf_op jit(solution)/shard_map/while/body/eval_jaxpr/gather | solution.py:67
  158.9 11.8 %fusion.52 = f32[4,8,128,128]{3,2,1,0:T(8,128)S(1)} fusion(f32[4,8,128,128]{3,2,1,0:T(8,128)S(1)} %get-tuple-element.145, s32[]{:T(128)} %get-tuple-element.144, f32[8,16,128,128]{3,2,1,0:T(8,128)} %fusion.50, f32[8,16,128,128]{3,2,1,0:T(8,128)} %gather_fusion.2), kind=kOutput, calls=%fused_computation.6.clone.1 | convolution fusion | flops 3221225472 | bytes 17301508 | tf_op jit(solution)/shard_map/while/body/eval_jaxpr/gpil,gplj->gij/dot_general | solution.py:67
  170.7 7.1 %gather_fusion = f32[8,16,128,128]{3,2,1,0:T(8,128)} fusion(f32[6,16,128,128]{3,2,1,0:T(8,128)} %get-tuple-element.156, s32[1024]{0:T(1024)S(1)} %pad_clamp_fusion.6), kind=kCustom, calls=%fused_computation.clone.1 | custom fusion | bytes 16777248 | tf_op jit(solution)/shard_map/while/body/eval_jaxpr/gather | solution.py:66
  177.8 2.8 gather_fusion.1
  180.6 11.0 %fusion.50 = f32[8,16,128,128]{3,2,1,0:T(8,128)} fusion(f32[8,16,128,128]{3,2,1,0:T(8,128)} %gather_fusion, f32[8,128,128]{2,1,0:T(8,128)S(1)} %gather_fusion.1), kind=kOutput, calls=%fused_computation.7.clone.1 | convolution fusion | flops 3221225472 | bytes 17301504 | tf_op jit(solution)/shard_map/while/body/eval_jaxpr/gpik,kgl->gpil/dot_general | solution.py:66
  191.6 7.1 %gather_fusion.2 = f32[8,16,128,128]{3,2,1,0:T(8,128)} fusion(f32[6,16,128,128]{3,2,1,0:T(8,128)} %get-tuple-element.156, s32[1024]{0:T(1024)S(1)} %pad_clamp_fusion.7), kind=kCustom, calls=%fused_computation.2.clone.1 | custom fusion | bytes 16777248 | tf_op jit(solution)/shard_map/while/body/eval_jaxpr/gather | solution.py:67
  198.7 11.8 %fusion.52 = f32[4,8,128,128]{3,2,1,0:T(8,128)S(1)} fusion(f32[4,8,128,128]{3,2,1,0:T(8,128)S(1)} %get-tuple-element.145, s32[]{:T(128)} %get-tuple-element.144, f32[8,16,128,128]{3,2,1,0:T(8,128)} %fusion.50, f32[8,16,128,128]{3,2,1,0:T(8,128)} %gather_fusion.2), kind=kOutput, calls=%fused_computation.6.clone.1 | convolution fusion | flops 3221225472 | bytes 17301508 | tf_op jit(solution)/shard_map/while/body/eval_jaxpr/gpil,gplj->gij/dot_general | solution.py:67
  210.5 7.1 %gather_fusion = f32[8,16,128,128]{3,2,1,0:T(8,128)} fusion(f32[6,16,128,128]{3,2,1,0:T(8,128)} %get-tuple-element.156, s32[1024]{0:T(1024)S(1)} %pad_clamp_fusion.6), kind=kCustom, calls=%fused_computation.clone.1 | custom fusion | bytes 16777248 | tf_op jit(solution)/shard_map/while/body/eval_jaxpr/gather | solution.py:66
  217.6 2.8 gather_fusion.1
  220.4 11.0 %fusion.50 = f32[8,16,128,128]{3,2,1,0:T(8,128)} fusion(f32[8,16,128,128]{3,2,1,0:T(8,128)} %gather_fusion, f32[8,128,128]{2,1,0:T(8,128)S(1)} %gather_fusion.1), kind=kOutput, calls=%fused_computation.7.clone.1 | convolution fusion | flops 3221225472 | bytes 17301504 | tf_op jit(solution)/shard_map/while/body/eval_jaxpr/gpik,kgl->gpil/dot_general | solution.py:66
  231.4 7.1 %gather_fusion.2 = f32[8,16,128,128]{3,2,1,0:T(8,128)} fusion(f32[6,16,128,128]{3,2,1,0:T(8,128)} %get-tuple-element.156, s32[1024]{0:T(1024)S(1)} %pad_clamp_fusion.7), kind=kCustom, calls=%fused_computation.2.clone.1 | custom fusion | bytes 16777248 | tf_op jit(solution)/shard_map/while/body/eval_jaxpr/gather | solution.py:67
  238.5 11.8 %fusion.52 = f32[4,8,128,128]{3,2,1,0:T(8,128)S(1)} fusion(f32[4,8,128,128]{3,2,1,0:T(8,128)S(1)} %get-tuple-element.145, s32[]{:T(128)} %get-tuple-element.144, f32[8,16,128,128]{3,2,1,0:T(8,128)} %fusion.50, f32[8,16,128,128]{3,2,1,0:T(8,128)} %gather_fusion.2), kind=kOutput, calls=%fused_computation.6.clone.1 | convolution fusion | flops 3221225472 | bytes 17301508 | tf_op jit(solution)/shard_map/while/body/eval_jaxpr/gpil,gplj->gij/dot_general | solution.py:67
  250.4 7.1 %gather_fusion = f32[8,16,128,128]{3,2,1,0:T(8,128)} fusion(f32[6,16,128,128]{3,2,1,0:T(8,128)} %get-tuple-element.156, s32[1024]{0:T(1024)S(1)} %pad_clamp_fusion.6), kind=kCustom, calls=%fused_computation.clone.1 | custom fusion | bytes 16777248 | tf_op jit(solution)/shard_map/while/body/eval_jaxpr/gather | solution.py:66
  257.5 2.8 gather_fusion.1
  260.2 11.0 %fusion.50 = f32[8,16,128,128]{3,2,1,0:T(8,128)} fusion(f32[8,16,128,128]{3,2,1,0:T(8,128)} %gather_fusion, f32[8,128,128]{2,1,0:T(8,128)S(1)} %gather_fusion.1), kind=kOutput, calls=%fused_computation.7.clone.1 | convolution fusion | flops 3221225472 | bytes 17301504 | tf_op jit(solution)/shard_map/while/body/eval_jaxpr/gpik,kgl->gpil/dot_general | solution.py:66
  271.3 7.1 %gather_fusion.2 = f32[8,16,128,128]{3,2,1,0:T(8,128)} fusion(f32[6,16,128,128]{3,2,1,0:T(8,128)} %get-tuple-element.156, s32[1024]{0:T(1024)S(1)} %pad_clamp_fusion.7), kind=kCustom, calls=%fused_computation.2.clone.1 | custom fusion | bytes 16777248 | tf_op jit(solution)/shard_map/while/body/eval_jaxpr/gather | solution.py:67
  278.3 11.8 %fusion.52 = f32[4,8,128,128]{3,2,1,0:T(8,128)S(1)} fusion(f32[4,8,128,128]{3,2,1,0:T(8,128)S(1)} %get-tuple-element.145, s32[]{:T(128)} %get-tuple-element.144, f32[8,16,128,128]{3,2,1,0:T(8,128)} %fusion.50, f32[8,16,128,128]{3,2,1,0:T(8,128)} %gather_fusion.2), kind=kOutput, calls=%fused_computation.6.clone.1 | convolution fusion | flops 3221225472 | bytes 17301508 | tf_op jit(solution)/shard_map/while/body/eval_jaxpr/gpil,gplj->gij/dot_general | solution.py:67
  290.2 2.8 gather_fusion.4
  292.9 4.5 broadcast_select_fusion
  297.4 4.5 all-to-all-start.1
  302.0 0.2 reduce-scatter.2.cloned.1.call-start
  302.2 0.2 select_reduce_fusion
  302.5 0.2 fusion.22
  302.7 0.1 and.97
  302.8 92.0 %all-to-all-done.1 = f32[8,8,128,128]{3,2,1,0:T(8,128)} async-done(((f32[8,8,128,128]{3,2,1,0:T(8,128)}), f32[8,8,128,128]{3,2,1,0:T(8,128)}, u32[]{:S(2)}, u32[]{:S(2)}) %all-to-all-start.1) | async-done | bytes 4194336 | tf_op jit(solution)/shard_map/all_to_all | solution.py:83
  394.8 5.8 %fusion.9 = f32[128,128,8]{1,2,0:T(8,128)S(1)} fusion(f32[8,8,128,128]{3,2,1,0:T(8,128)} %all-to-all-done.1, s32[64]{0:T(128)S(1)} %eq.187, pred[64]{0:T(512)(128)(4,1)S(1)} %and.97), kind=kOutput, calls=%fused_computation.26 | convolution fusion | flops 100664320 | bytes 4718912 | tf_op jit(solution)/shard_map/bs,sij->ibj/dot_general | solution.py:90
  400.6 0.9 copy.77
  401.5 20.4 %reduce-scatter.2.cloned.1.call-done = f32[32,1024]{1,0:T(8,128)} async-done(((f32[128,1024]{1,0:T(8,128)}), f32[32,1024]{1,0:T(8,128)}) %reduce-scatter.2.cloned.1.call-update) | async-done | bytes 131088 | tf_op jit(solution)/shard_map/reduce_scatter | solution.py:94
  421.9 1.6 copy.78
  423.5 3.3 all-to-all-start.2
  426.8 0.9 copy_bitcast_fusion.1
  427.7 3.6 all-to-all-done.2
  431.4 12.8 %all_to_all.48 = f32[32,8,128]{2,0,1:T(8,128)} all-to-all(f32[32,8,128]{2,0,1:T(8,128)S(1)} %copy_bitcast_fusion.1), channel_id=1, replica_groups=mesh['tile'=8,'aux'=4] {'tile'}, dimensions={1} | all-to-all | bytes 262144 | tf_op jit(solution)/shard_map/all_to_all | solution.py:96
  444.1 3.3 all-to-all-start.4
  447.6 4.5 all-to-all-done.4
  452.1 0.1 copy.55
  452.3 0.3 fusion.12
  452.6 0.4 fusion.14
  453.0 0.8 copy.57
  (48 shorter events, 1.2 us)
Async XLA Ops:
  6.5 445.7 %copy-start = (f32[1024,128]{1,0:T(8,128)S(1)}, f32[1024,128]{1,0:T(8,128)}, u32[]{:S(2)}) copy-start(f32[1024,128]{1,0:T(8,128)} %param.12) | copy-start | bytes 1572868
  31.1 6.3 %copy-start.1 = (s32[32,2]{0,1:T(2,128)S(1)}, s32[32,2]{0,1:T(2,128)}, u32[]{:S(2)}) copy-start(s32[32,2]{0,1:T(2,128)} %param.13) | copy-start | bytes 772
  31.1 99.7 %all-to-all-start = ((f32[128,8,8,128]{3,0,2,1:T(8,128)}), f32[128,8,8,128]{3,0,2,1:T(8,128)}, u32[]{:S(2)}, u32[]{:S(2)}) async-start(f32[128,8,8,128]{3,0,2,1:T(8,128)} %select_bitcast_fusion), calls=%async_computation | async-start | bytes 8388608 | tf_op jit(solution)/shard_map/all_to_all | solution.py:58
  297.4 97.4 %all-to-all-start.1 = ((f32[8,8,128,128]{3,2,1,0:T(8,128)}), f32[8,8,128,128]{3,2,1,0:T(8,128)}, u32[]{:S(2)}, u32[]{:S(2)}) async-start(f32[8,8,128,128]{3,2,1,0:T(8,128)} %broadcast_select_fusion), calls=%async_computation.1 | async-start | bytes 8388608 | tf_op jit(solution)/shard_map/all_to_all | solution.py:83
  302.0 120.0 %reduce-scatter.2.cloned.1.call-start = ((), (), s32[]{:S(2)}) async-start(), calls=%async_computation.6 | async-start | bytes 655360 | tf_op jit(solution)/shard_map/reduce_scatter | solution.py:94
  423.5 7.9 %all-to-all-start.2 = ((f32[32,4,256]{2,0,1:T(8,128)}), f32[32,4,256]{2,0,1:T(8,128)S(1)}, u32[]{:S(2)}, u32[]{:S(2)}) async-start(f32[32,4,256]{2,0,1:T(8,128)} %bitcast.118), calls=%async_computation.3 | async-start | bytes 262144 | tf_op jit(solution)/shard_map/all_to_all | solution.py:108
  444.1 7.9 %all-to-all-start.4 = ((f32[32,8,128]{2,0,1:T(8,128)}), f32[32,8,128]{2,0,1:T(8,128)S(1)}, u32[]{:S(2)}, u32[]{:S(2)}) async-start(f32[32,8,128]{2,0,1:T(8,128)} %all_to_all.48), calls=%async_computation.5 | async-start | bytes 262144 | tf_op jit(solution)/shard_map/all_to_all | solution.py:95
Sparse Core Ops, SparseCore 0:
  401.6 20.2 reduce-scatter.1
where the time goes:
time: 462 us; the launch traced here: 461 us
  waiting for transfers between devices  213 us (46%)
  matrix products  97.8 us (21%)
  local copies, waits for them, and re-layouts  80.4 us (17%)
  blocking collectives  21.4 us (5%)
  starting transfers between devices  17.4 us (4%)
  other arithmetic  16.9 us (4%)
  between operations  13.6 us (3%)
    all_to_all x1, waiting for transfers between devices, local(): lax.all_to_all(outgoing, 'tile', split_axis=1, concat_axis=1, tiled=True)  92.5 us
    all_to_all x1, waiting for transfers between devices, local(): lax.all_to_all(outbound, 'tile', split_axis=0, concat_axis=0, tiled=True)  92 us
    dot_general x4, matrix products, one_batch(): jnp.einsum('gpil,gplj->gij', halfway, factors[rights], precision=highest)  47.2 us
    dot_general x4, matrix products, one_batch(): jnp.einsum('gpik,kgl->gpil', factors[lefts], dens_block, precision=highest)  44 us
    gather x4, local copies, waits for them, and re-layouts, one_batch(): factors[lefts]  28.3 us
    gather x4, local copies, waits for them, and re-layouts, one_batch(): factors[rights]  28.3 us
    reduce_scatter x1, waiting for transfers between devices, local(): lax.psum_scatter(row_sums, 'aux', scatter_dimension=0, tiled=True)  20.4 us
    all_to_all x1, blocking collectives, local(): lax.all_to_all(exchange_rows.reshape(quarter, tiles_all, tile_width), 'ti...  12.8 us
  transfers between devices with their start and end apart: 5, of which 5 were waited for; matrix products, arithmetic and copies ran while one was open for 1% of the time, Pallas kernels for 0%

commit v1 on v0

--- a/solution.py
+++ b/solution.py
@@ -1,9 +1,16 @@
+import functools
+
 import jax
 import jax.numpy as jnp
 from jax import lax
+from jax.experimental import pallas as pl
+from jax.experimental.pallas import tpu as pltpu
 from jax.sharding import PartitionSpec as P
 
+
 highest = lax.Precision.HIGHEST
+AXES = ("tile", "aux")
+GATHER_LIMIT = 16 << 20
 
 
 def ranks_of(key_rows):
@@ -23,7 +30,7 @@
     return (picked, filled)
 
 
-def local(
+def routed(
     density,
     factors,
     orthogonalizers,
@@ -122,6 +129,290 @@
     return fock.reshape(tile_width, per_block * tile_width)
 
 
+MIB = 1 << 20
+UNROLL = 4
+ROW_STAGE, ROW_LEFT, ROW_RIGHT, ROW_SHARD, ROW_PART, ROW_A, ROW_AC, ROW_B, ROW_BC = range(9)
+
+
+def split(x):
+    hi = x.astype(jnp.bfloat16)
+    lo = (x - hi.astype(jnp.float32)).astype(jnp.bfloat16)
+    return hi, lo
+
+
+def prep_kernel(f_hbm, o_ref, buf, sem):
+    slots, rows, w = f_hbm.shape
+    copies = [pltpu.make_async_copy(f_hbm.at[s], buf.at[s], sem.at[s]) for s in range(slots)]
+    for copy in copies:
+        copy.start()
+    step = 256
+    for s, copy in enumerate(copies):
+        copy.wait()
+
+        @pl.loop(0, rows // step)
+        def _(i, s=s):
+            at = pl.ds(pl.multiple_of(i * step, step), step)
+            hi, lo = split(buf[s, at, :])
+            o_ref[s, at, :w] = hi
+            o_ref[s, at, w:] = lo
+
+
+def prep(factors):
+    s, p, w, _ = factors.shape
+    rows = p * w
+    return pl.pallas_call(
+        prep_kernel,
+        in_specs=[pl.BlockSpec(memory_space=pl.ANY)],
+        out_specs=pl.BlockSpec(memory_space=pltpu.VMEM),
+        out_shape=jax.ShapeDtypeStruct((s, rows, 2 * w), jnp.bfloat16),
+        scratch_shapes=[pltpu.VMEM((s, rows, w), jnp.float32), pltpu.SemaphoreType.DMA((s,))],
+        compiler_params=pltpu.CompilerParams(vmem_limit_bytes=16 * MIB),
+        cost_estimate=pl.CostEstimate(flops=2 * factors.size, bytes_accessed=8 * factors.size, transcendentals=0),
+    )(factors.reshape(s, rows, w))
+
+
+def task_kernel(stage, first, firsts, cuts, tab, *refs):
+    f2, *refs = refs
+    if not first:
+        sums_in, *refs = refs
+    stacks, refs = refs[: len(firsts)], refs[len(firsts) :]
+    outs, (sums, order, tiles, sem) = refs[: len(refs) - 4], refs[len(refs) - 4 :]
+    w = f2.shape[2] // 2
+    tasks = tab.shape[1]
+    pairs = f2.shape[1] // (2 * w)
+    f32 = jnp.float32
+
+    def pick(q, count):
+        mine = tab[ROW_STAGE, q] == stage
+
+        @pl.when(mine)
+        def _():
+            order[count] = q
+            shard, part = tab[ROW_SHARD, q], pl.multiple_of(tab[ROW_PART, q] * w, w)
+            for start, stack in zip(firsts, stacks):
+                @pl.when((shard >= start) & (shard < start + stack.shape[0]))
+                def _(start=start, stack=stack):
+                    pltpu.make_async_copy(
+                        stack.at[shard - start, :, pl.ds(part, w)], tiles.at[count], sem.at[count]
+                    ).start()
+
+        return count + mine.astype(jnp.int32)
+
+    count = lax.fori_loop(0, tasks, pick, 0)
+    sums[...] = jnp.zeros_like(sums) if first else sums_in[...]
+
+    def rows(p):
+        return slice(p * 2 * w, (p + 1) * 2 * w)
+
+    def one(i):
+        q = order[i]
+        left, right = tab[ROW_LEFT, q], tab[ROW_RIGHT, q]
+        hi, lo = split(tiles[i])
+        half = jnp.concatenate([hi, lo], axis=1)
+        wt = jnp.concatenate([half, half], axis=0)
+        acc = None
+        for p in range(pairs):
+            h = jnp.dot(f2[left, rows(p), :], wt, preferred_element_type=f32)
+            hi, lo = split(h[:, :w] + h[:, w:])
+            lhs = jnp.concatenate(
+                [jnp.concatenate([hi[:w], hi[w:]], axis=1), jnp.concatenate([lo[:w], lo[w:]], axis=1)], axis=0
+            )
+            d = jnp.dot(lhs, f2[right, rows(p), :], preferred_element_type=f32)
+            acc = d if acc is None else acc + d
+        part = acc[:w] + acc[w:]
+        part = part[:, :w] + part[:, w:]
+        c = pl.ds(pl.multiple_of(tab[ROW_AC, q] * w, w), w)
+        sums[tab[ROW_A, q], :, c] = sums[tab[ROW_A, q], :, c] + part
+        c = pl.ds(pl.multiple_of(tab[ROW_BC, q] * w, w), w)
+        sums[tab[ROW_B, q], :, c] = sums[tab[ROW_B, q], :, c] + part.T
+
+    def several(start, n):
+        for k in range(n):
+            pltpu.make_async_copy(stacks[0].at[0, :, pl.ds(0, w)], tiles.at[start + k], sem.at[start + k]).wait()
+        for k in range(n):
+            one(start + k)
+
+    def many(i, carry):
+        several(i * UNROLL, UNROLL)
+        return carry
+
+    def single(i, carry):
+        several(i, 1)
+        return carry
+
+    lax.fori_loop(0, count // UNROLL, many, 0)
+    lax.fori_loop(count // UNROLL * UNROLL, count, single, 0)
+    if cuts:
+        for start, out in zip(cuts, outs):
+            out[...] = sums[start : start + out.shape[0]]
+
+
+def run_stage(table, stage, f2, stacks, firsts, sums, shape, cuts=()):
+    tasks = table.shape[1]
+    w = f2.shape[2] // 2
+    first = sums is None
+    vmem = pl.BlockSpec(memory_space=pltpu.VMEM)
+    ends = list(cuts[1:]) + [shape[0]]
+    shapes = [(end - start,) + shape[1:] for start, end in zip(cuts, ends)] if cuts else [shape]
+    outs = [jax.ShapeDtypeStruct(s, jnp.float32) for s in shapes]
+    kept = [pltpu.VMEM(shape, jnp.float32)] if cuts else []
+    body = functools.partial(task_kernel, stage, first, tuple(firsts), tuple(cuts))
+    return pl.pallas_call(
+        body,
+        in_specs=[pl.BlockSpec(memory_space=pltpu.SMEM)] + [vmem] * (1 if first else 2)
+        + [pl.BlockSpec(memory_space=pl.ANY)] * len(stacks),
+        out_specs=[vmem] * len(outs),
+        out_shape=outs,
+        scratch_shapes=kept + [
+            pltpu.SMEM((tasks,), jnp.int32),
+            pltpu.VMEM((tasks, w, w), jnp.float32),
+            pltpu.SemaphoreType.DMA((tasks,)),
+        ],
+        compiler_params=pltpu.CompilerParams(vmem_limit_bytes=20 * MIB),
+        cost_estimate=pl.CostEstimate(flops=tasks * f2.shape[1] * w * w * 4, bytes_accessed=2 * f2.size, transcendentals=0),
+    )(table, f2, *([] if first else [sums]), *stacks)
+
+
+def shift(value, sizes, move):
+    depth, wide, tall, cores = sizes
+    pairs = []
+    for source in range(depth * wide * tall * cores):
+        rest, c = divmod(source, cores)
+        rest, y = divmod(rest, tall)
+        z, x = divmod(rest, wide)
+        tz, tx, ty, tc = move(z, x, y, c)
+        pairs.append((source, (((tz % depth) * wide + tx) * tall + ty) * cores + tc))
+    return lax.ppermute(value, AXES, pairs)
+
+
+def across_x(z, x, y, c):
+    return z, 1 - x, y, c
+
+
+def across_y(z, x, y, c):
+    return z, x, 1 - y, c
+
+
+def across_core(z, x, y, c):
+    return z, x, y, 1 - c
+
+
+def across_diagonal(z, x, y, c):
+    return (z, x, 1 - y, c) if c == 0 else (z, 1 - x, y, c)
+
+
+def across_z(step):
+    return lambda z, x, y, c: (z + step, x, y, c)
+
+
+def gathered(
+    density,
+    factors,
+    orthogonalizers,
+    slot_pairs,
+    density_source,
+    density_column,
+    target_row,
+    target_column,
+):
+    tiles_all = lax.axis_size("tile")
+    aux_count = lax.axis_size("aux")
+    tile_me = lax.axis_index("tile")
+    aux_me = lax.axis_index("aux")
+    tile_width = factors.shape[-1]
+    task_count = slot_pairs.shape[0]
+    per_block = tiles_all // aux_count
+    depth = tiles_all // 2
+    far = depth - 1
+    sizes = (depth, 2, aux_count // 2, 2)
+    z_me, x_me = tile_me // 2, tile_me % 2
+    y_me, core_me = aux_me // 2, aux_me % 2
+    on_first = core_me == 0
+
+    def move(value, how):
+        return shift(value, sizes, how)
+
+    start = (tile_me * aux_count + aux_me) * task_count
+
+    def own(table):
+        return lax.dynamic_slice_in_dim(table[:, 0], start, task_count)
+
+    def place(row, column, sign):
+        aux = column // per_block
+        dz = (sign * (z_me - row // 2)) & (depth - 1) if depth & far == 0 else (sign * (z_me - row // 2)) % depth
+        side = ((aux // 2) ^ y_me) * 2 + ((row & 1) ^ x_me)
+        shard = ((aux & 1) ^ core_me) * 4 * depth + jnp.where(dz == 0, side, 3 + side * far + dz)
+        stage = jnp.where((dz == 0) | (side == 0), 0, jnp.where(side == 3, 2, 1))
+        return stage, shard, column % per_block
+
+    row_a, col_b = own(target_row), own(target_column)
+    stage, source, part = place(own(density_source), own(density_column), 1)
+    _, shard_a, part_a = place(row_a, col_b, 1)
+    _, shard_b, part_b = place(col_b, row_a, 1)
+    table = jnp.stack([stage, slot_pairs[:, 0], slot_pairs[:, 1], source, part, shard_a, part_a, shard_b, part_b])
+
+    column = [move(density, across_z(step)) for step in range(1, depth)]
+    near_x, near_y = move(density, across_x), move(density, across_y)
+    near_d = move(jnp.where(on_first, near_x, near_y), across_diagonal)
+    near = jnp.stack([density, near_x, near_y, near_d])
+    near_c = move(near, across_core)
+    split_factors = prep(factors)
+    column, split_factors, table = lax.optimization_barrier((jnp.stack(column), split_factors, table))
+    column_c = move(column, across_core)
+    side_x = move(column, across_x)
+    side_y = move(column, across_y)
+    corner = move(jnp.where(on_first, side_x, side_y), across_diagonal)
+    side_xc, side_yc, corner_c = (move(value, across_core) for value in (side_x, side_y, corner))
+
+    firsts = [0, 4, 4 + far, 4 + 2 * far, 4 + 3 * far]
+    other = [first + 4 * depth for first in firsts]
+    shape = (8 * depth,) + density.shape
+    (sums,) = run_stage(
+        table, 0, split_factors, [near, near_c, column, column_c], [firsts[0], other[0], firsts[1], other[1]], None, shape
+    )
+    (sums,) = run_stage(
+        table, 1, split_factors, [side_x, side_y, side_xc, side_yc], firsts[2:4] + other[2:4], sums, shape
+    )
+    mine_and_others = run_stage(
+        table, 2, split_factors, [corner, corner_c], [firsts[4], other[4]], sums, shape, firsts + other
+    )
+    mine, others = mine_and_others[:5], mine_and_others[5:]
+
+    corner = mine[4] + move(others[4], across_core)
+    near = mine[0] + move(others[0], across_core)
+    corner_in = move(corner, across_diagonal)
+    near_in = move(near[3], across_diagonal)
+    side_x = mine[2] + move(others[2], across_core)
+    side_y = mine[3] + move(others[3], across_core)
+    column = mine[1] + move(others[1], across_core)
+    side_x = side_x + jnp.where(on_first, corner_in, 0.0)
+    side_y = side_y + jnp.where(on_first, 0.0, corner_in)
+    near_x = near[1] + jnp.where(on_first, near_in, 0.0)
+    near_y = near[2] + jnp.where(on_first, 0.0, near_in)
+    column = column + move(side_x, across_x) + move(side_y, across_y)
+    total = near[0] + move(near_x, across_x) + move(near_y, across_y)
+    for step in range(1, depth):
+        total = total + move(column[step - 1], across_z(-step))
+
+    blocks_x = orthogonalizers.reshape(tiles_all, tile_width, tile_width)
+    left_x = blocks_x[tile_me]
+    right_x = lax.dynamic_slice_in_dim(blocks_x, aux_me * per_block, per_block, 0)
+    leftward = jnp.einsum("ki,kn->in", left_x, total, precision=highest)
+    leftward = leftward.reshape(tile_width, per_block, tile_width)
+    fock = jnp.einsum("ibl,blj->ibj", leftward, right_x, precision=highest)
+    return fock.reshape(tile_width, per_block * tile_width)
+
+
+def local(density, *rest):
+    tiles_all = lax.axis_size("tile")
+    aux_count = lax.axis_size("aux")
+    whole = density.size * density.dtype.itemsize * tiles_all * aux_count
+    pairs = tiles_all % 2 == 0 and aux_count == 4 and tiles_all % aux_count == 0
+    if pairs and whole <= GATHER_LIMIT:
+        return gathered(density, *rest)
+    return routed(density, *rest)
+
+
 def solution(mesh):
     return jax.shard_map(
         local,

time: 462 us -> 102 us (0.22)
  waiting for transfers between devices: 213 us -> 34.2 us
  matrix products: 97.8 us -> 0.71 us
  local copies, waits for them, and re-layouts: 80.4 us -> 4.39 us
  Pallas kernels: 0 us -> 29.6 us
  blocking collectives: 21.4 us -> 0 us
  other arithmetic: 16.9 us -> 2.1 us
  between operations: 13.6 us -> 0.2 us
  starting transfers between devices: 17.4 us -> 29.7 us
    all_to_all x4 -> x0, waiting for transfers between devices: 193 us -> none  [the longest x1 92.5 us: local(): lax.all_to_all(outgoing, 'tile', split_axis=1, concat_axis=1, tiled=True)]
    dot_general x11 -> x2, matrix products: 97.8 us -> 0.71 us  [the longest x1 0.4 us: gathered(): fock = jnp.einsum('ibl,blj->ibj', leftward, right_x, precision=highest)]
    gather x14 -> x0, local copies, waits for them, and re-layouts: 73.3 us -> none  [the longest x4 28.3 us: one_batch(): factors[lefts]]
    ppermute x0 -> x28, waiting for transfers between devices: none -> 34.2 us  [shift(): return lax.ppermute(value, AXES, pairs)]
    ppermute x0 -> x28, starting transfers between devices: none -> 29.7 us  [shift(): return lax.ppermute(value, AXES, pairs)]
    pallas_call x0 -> x4, Pallas kernels: none -> 29.6 us  [the longest x3 28 us: run_stage(): pl.pallas_call(body, in_specs=[pl.BlockSpec(memory_space=pltpu.SMEM)] + [...]
    reduce_scatter x1 -> x0, waiting for transfers between devices: 20.4 us -> none  [local(): lax.psum_scatter(row_sums, 'aux', scatter_dimension=0, tiled=True)]
    all_to_all x4 -> x0, starting transfers between devices: 17.1 us -> none  [the longest x1 5.94 us: local(): lax.all_to_all(outgoing, 'tile', split_axis=1, concat_axis=1, tiled=True)]
  transfers between devices with their start and end apart: 5 -> 28, of which waited for: 5 -> 10; matrix products, arithmetic and copies ran while one was open for 1% -> 3% of each run, Pallas kernels for 0% -> 24%
where the time goes in v1:
time: 102 us; the launch traced here: 101 us
  waiting for transfers between devices  34.2 us (34%)
  starting transfers between devices  29.7 us (29%)
  Pallas kernels  29.6 us (29%)
  local copies, waits for them, and re-layouts  4.39 us (4%)
  other arithmetic  2.1 us (2%)
    ppermute x28, waiting for transfers between devices, shift(): return lax.ppermute(value, AXES, pairs)  34.2 us
    ppermute x28, starting transfers between devices, shift(): return lax.ppermute(value, AXES, pairs)  29.7 us
    pallas_call x3, Pallas kernels, run_stage(): pl.pallas_call(body, in_specs=[pl.BlockSpec(memory_space=pltpu.SMEM)] + [...  28 us
    unnamed x6, local copies, waits for them, and re-layouts  2.79 us
  transfers between devices with their start and end apart: 28, of which 10 were waited for; matrix products, arithmetic and copies ran while one was open for 3% of the time, Pallas kernels for 24%

profile of v1, /device:TPU:0, one launch (start us, length us, event | category | flops | bytes accessed | tf_op | source)
XLA Modules:
  0.0 101.0 jit_solution(6052687605908993613)
XLA Ops:
  0.0 5.1 %collective-permute-start.2 = (f32[128,256]{1,0:T(8,128)}, f32[128,256]{1,0:T(8,128)S(1)}, u32[]{:S(2)}, u32[]{:S(2)}) collective-permute-start(f32[128,256]{1,0:T(8,128)} %param.8), channel_id=1, source_target_pairs={{0,24},{1,25},{2,26},{3,27},{4,28},{5,29},{6,30},{7,31},{8,0},{9,1... | collective-permute-start | bytes 393224 | tf_op jit(solution)/shard_map/ppermute | solution.py:285
  5.1 0.0 collective-permute-start.1
  5.1 1.0 %collective-permute-start = (f32[128,256]{1,0:T(8,128)}, f32[128,256]{1,0:T(8,128)S(1)}, u32[]{:S(2)}, u32[]{:S(2)}) collective-permute-start(f32[128,256]{1,0:T(8,128)} %param.8), channel_id=1, source_target_pairs={{0,8},{1,9},{2,10},{3,11},{4,12},{5,13},{6,14},{7,15},{8,16},{9,17... | collective-permute-start | bytes 393224 | tf_op jit(solution)/shard_map/ppermute | solution.py:285
  6.1 1.5 %collective-permute-start.3 = (f32[128,256]{1,0:T(8,128)}, f32[128,256]{1,0:T(8,128)S(1)}, u32[]{:S(2)}, u32[]{:S(2)}) collective-permute-start(f32[128,256]{1,0:T(8,128)} %param.8), channel_id=1, source_target_pairs={{0,4},{1,5},{2,6},{3,7},{4,0},{5,1},{6,2},{7,3},{8,12},{9,13},{10,... | collective-permute-start | bytes 393224 | tf_op jit(solution)/shard_map/ppermute | solution.py:285
  7.6 1.5 %collective-permute-start.4 = (f32[128,256]{1,0:T(8,128)}, f32[128,256]{1,0:T(8,128)S(1)}, u32[]{:S(2)}, u32[]{:S(2)}) collective-permute-start(f32[128,256]{1,0:T(8,128)} %param.8), channel_id=1, source_target_pairs={{0,2},{1,3},{2,0},{3,1},{4,6},{5,7},{6,4},{7,5},{8,10},{9,11},{10,... | collective-permute-start | bytes 393224 | tf_op jit(solution)/shard_map/ppermute | solution.py:285
  9.1 0.7 and_select_fusion.6
  9.8 0.8 fusion.17
  10.6 0.8 slice_bitcast_fusion.7
  11.4 0.0 collective-permute-done.3
  11.4 1.4 %collective-permute-done.4 = f32[128,256]{1,0:T(8,128)S(1)} collective-permute-done((f32[128,256]{1,0:T(8,128)}, f32[128,256]{1,0:T(8,128)S(1)}, u32[]{:S(2)}, u32[]{:S(2)}) %collective-permute-start.4) | collective-permute-done | bytes 131104 | tf_op jit(solution)/shard_map/ppermute | solution.py:285
  12.8 1.6 %collective-permute-start.5 = (f32[128,256]{1,0:T(8,128)S(1)}, f32[128,256]{1,0:T(8,128)S(1)}, u32[]{:S(2)}, u32[]{:S(2)}) collective-permute-start(f32[128,256]{1,0:T(8,128)S(1)} %broadcast_select_fusion.1), channel_id=1, source_target_pairs={{0,2},{1,5},{2,0},{3,7},{4,6},{5,1},{6,4},{7,3},{8,10},{9,13},{10,... | collective-permute-start | bytes 393224 | tf_op jit(solution)/shard_map/ppermute | solution.py:285
  14.4 2.8 %copy-done.1 = f32[6,16,128,128]{3,2,1,0:T(8,128)S(1)} copy-done((f32[6,16,128,128]{3,2,1,0:T(8,128)S(1)}, f32[6,16,128,128]{3,2,1,0:T(8,128)}, u32[]{:S(2)}) %copy-start.1) | copy-done | bytes 6291480
  17.2 1.6 %shard_map.82.refs_0_ = bf16[6,2048,256]{2,1,0:T(8,128)(2,1)S(1)} custom-call(f32[6,2048,128]{2,1,0:T(8,128)S(1)} %bitcast.114), custom_call_target="tpu_custom_call" | custom-call | flops 3145728 | bytes 12582912 | tf_op jit(solution)/shard_map/pallas_call | solution.py:163
  18.8 0.0 collective-permute-done.2
  18.8 0.0 collective-permute-done.1
  18.9 0.0 collective-permute-done
  18.9 0.6 collective-permute-start.8
  19.5 0.5 collective-permute-start.9
  20.0 0.0 collective-permute-done.5
  20.1 0.1 collective-permute-start.6
  20.1 0.5 collective-permute-start.7
  20.6 6.4 %collective-permute-done.8.refs_2_ = f32[3,128,256]{2,1,0:T(8,128)S(1)} collective-permute-done((f32[3,128,256]{2,1,0:T(8,128)S(1)}, f32[3,128,256]{2,1,0:T(8,128)S(1)}, u32[]{:S(2)}, u32[]{:S(2)}) %collective-permute-start.8) | collective-permute-done | bytes 393248 | tf_op jit(solution)/shard_map/ppermute | solution.py:285
  27.0 1.2 %collective-permute-done.9.refs_3_ = f32[3,128,256]{2,1,0:T(8,128)S(1)} collective-permute-done((f32[3,128,256]{2,1,0:T(8,128)S(1)}, f32[3,128,256]{2,1,0:T(8,128)S(1)}, u32[]{:S(2)}, u32[]{:S(2)}) %collective-permute-start.9) | collective-permute-done | bytes 393248 | tf_op jit(solution)/shard_map/ppermute | solution.py:285
  28.2 0.1 broadcast_select_fusion
  28.3 1.6 %collective-permute-start.12 = (f32[3,128,256]{2,1,0:T(8,128)S(1)}, f32[3,128,256]{2,1,0:T(8,128)S(1)}, u32[]{:S(2)}, u32[]{:S(2)}) collective-permute-start(f32[3,128,256]{2,1,0:T(8,128)S(1)} %broadcast_select_fusion), channel_id=1, source_target_pairs={{0,2},{1,5},{2,0},{3,7},{4,6},{5,1},{6,4},{7,3},{8,10},{9,13},{10,... | collective-permute-start | bytes 1179656 | tf_op jit(solution)/shard_map/ppermute | solution.py:285
  29.9 0.0 collective-permute-start.10
  29.9 0.5 collective-permute-start.11
  30.4 0.0 collective-permute-done.7.refs_4_
  30.4 13.0 %shard_map.83.refs_1_ = f32[32,128,256]{2,1,0:T(8,128)S(1)} custom-call(s32[9,32]{1,0:T(8,128)S(1)} %stack.41.tab, bf16[6,2048,256]{2,1,0:T(8,128)(2,1)S(1)} %shard_map.82.refs_0_, f32[4,128,256]{2,1,0:T(8,128)S(1)} %pad_maximum_fusion.refs_1_, f32[4,128,256]{2,1,0:T(8,128)S(1)} %collective-permute-done.6.refs_2_, ...), custom_call_target="tpu_custom_call" | custom-call | flops 4294967296 | bytes 6291456 | tf_op jit(solution)/shard_map/pallas_call | solution.py:260
  43.4 0.3 collective-permute-start.13
  43.7 10.1 %shard_map.84.refs_1_ = f32[32,128,256]{2,1,0:T(8,128)S(1)} custom-call(s32[9,32]{1,0:T(8,128)S(1)} %stack.41.tab, bf16[6,2048,256]{2,1,0:T(8,128)(2,1)S(1)} %shard_map.82.refs_0_, f32[32,128,256]{2,1,0:T(8,128)S(1)} %shard_map.83.refs_1_, f32[3,128,256]{2,1,0:T(8,128)S(1)} %collective-permute-done.8.refs_2_, ...), custom_call_target="tpu_custom_call" | custom-call | flops 4294967296 | bytes 6291456 | tf_op jit(solution)/shard_map/pallas_call | solution.py:260
  53.9 0.0 collective-permute-done.13.refs_3_
  53.9 4.9 %shard_map.85 = (f32[4,128,256]{2,1,0:T(8,128)S(1)}, f32[3,128,256]{2,1,0:T(8,128)S(1)}, f32[3,128,256]{2,1,0:T(8,128)S(1)}, f32[3,128,256]{2,1,0:T(8,128)S(1)},...) custom-call(s32[9,32]{1,0:T(8,128)S(1)} %stack.41.tab, ...), custom_call_target="tpu_custom_call" | custom-call | flops 4294967296 | bytes 6291456 | tf_op jit(solution)/shard_map/pallas_call | solution.py:260
  58.8 2.6 %collective-permute-start.20 = (f32[3,128,256]{2,1,0:T(8,128)S(1)}, f32[3,128,256]{2,1,0:T(8,128)S(1)}, u32[]{:S(2)}, u32[]{:S(2)}) collective-permute-start(f32[3,128,256]{2,1,0:T(8,128)S(1)} %get-tuple-element.28), channel_id=1, source_target_pairs={{0,1},{1,0},{2,3},{3,2},{4,5},{5,4},{6,7},{7,6},{8,9},{9,8},{10,11... | collective-permute-start | bytes 1179656 | tf_op jit(solution)/shard_map/ppermute | solution.py:285
  61.4 0.1 collective-permute-start.14
  61.5 0.4 collective-permute-start.19
  61.9 0.1 collective-permute-start.23
  62.0 0.8 collective-permute-done.20
  62.7 0.1 add.335
  62.8 3.7 %collective-permute-start.21 = (f32[3,128,256]{2,1,0:T(8,128)S(1)}, f32[3,128,256]{2,1,0:T(8,128)S(1)}, u32[]{:S(2)}, u32[]{:S(2)}) collective-permute-start(f32[3,128,256]{2,1,0:T(8,128)S(1)} %add.335), channel_id=1, source_target_pairs={{0,2},{1,5},{2,0},{3,7},{4,6},{5,1},{6,4},{7,3},{8,10},{9,13},{10,... | collective-permute-start | bytes 1179656 | tf_op jit(solution)/shard_map/ppermute | solution.py:285
  66.5 0.1 add.328
  66.6 0.0 collective-permute-done.23
  66.6 5.7 %collective-permute-done.21 = f32[3,128,256]{2,1,0:T(8,128)S(1)} collective-permute-done((f32[3,128,256]{2,1,0:T(8,128)S(1)}, f32[3,128,256]{2,1,0:T(8,128)S(1)}, u32[]{:S(2)}, u32[]{:S(2)}) %collective-permute-start.21) | collective-permute-done | bytes 393248 | tf_op jit(solution)/shard_map/ppermute | solution.py:285
  72.2 0.2 select_add_fusion.1
  72.4 2.1 %collective-permute-start.24 = (f32[3,128,256]{2,1,0:T(8,128)S(1)}, f32[3,128,256]{2,1,0:T(8,128)S(1)}, u32[]{:S(2)}, u32[]{:S(2)}) collective-permute-start(f32[3,128,256]{2,1,0:T(8,128)S(1)} %get-tuple-element.42), channel_id=1, source_target_pairs={{0,2},{1,3},{2,0},{3,1},{4,6},{5,7},{6,4},{7,5},{8,10},{9,11},{10,... | collective-permute-start | bytes 1179656 | tf_op jit(solution)/shard_map/ppermute | solution.py:285
  74.5 0.0 collective-permute-start.22
  74.5 0.2 collective-permute-start.15
  74.6 10.0 %collective-permute-done.15 = f32[128,256]{1,0:T(8,128)S(1)} collective-permute-done((f32[128,256]{1,0:T(8,128)S(1)}, f32[128,256]{1,0:T(8,128)S(1)}, u32[]{:S(2)}, u32[]{:S(2)}) %collective-permute-start.15) | collective-permute-done | bytes 131104 | tf_op jit(solution)/shard_map/ppermute | solution.py:285
  84.7 1.8 %collective-permute-start.17 = (f32[128,256]{1,0:T(8,128)S(1)}, f32[128,256]{1,0:T(8,128)S(1)}, u32[]{:S(2)}, u32[]{:S(2)}) collective-permute-start(f32[128,256]{1,0:T(8,128)S(1)} %get-tuple-element.37), channel_id=1, source_target_pairs={{0,2},{1,3},{2,0},{3,1},{4,6},{5,7},{6,4},{7,5},{8,10},{9,11},{10,... | collective-permute-start | bytes 393224 | tf_op jit(solution)/shard_map/ppermute | solution.py:285
  86.5 0.0 collective-permute-start.16
  86.5 0.0 collective-permute-done.18
  86.5 0.0 collective-permute-done.24
  86.5 0.1 add_add_fusion
  86.7 1.6 %collective-permute-start.27 = (f32[128,256]{1,0:T(8,128)S(1)}, f32[128,256]{1,0:T(8,128)S(1)}, u32[]{:S(2)}, u32[]{:S(2)}) collective-permute-start(f32[128,256]{1,0:T(8,128)S(1)} %get-tuple-element.39), channel_id=1, source_target_pairs={{0,8},{1,9},{2,10},{3,11},{4,12},{5,13},{6,14},{7,15},{8,16},{9,17... | collective-permute-start | bytes 393224 | tf_op jit(solution)/shard_map/ppermute | solution.py:285
  88.3 1.8 %collective-permute-start.26 = (f32[128,256]{1,0:T(8,128)S(1)}, f32[128,256]{1,0:T(8,128)S(1)}, u32[]{:S(2)}, u32[]{:S(2)}) collective-permute-start(f32[128,256]{1,0:T(8,128)S(1)} %get-tuple-element.40), channel_id=1, source_target_pairs={{0,16},{1,17},{2,18},{3,19},{4,20},{5,21},{6,22},{7,23},{8,24},{9,... | collective-permute-start | bytes 393224 | tf_op jit(solution)/shard_map/ppermute | solution.py:285
  90.1 0.6 collective-permute-start.25
  90.7 0.2 collective-permute-done.17
  90.9 0.9 collective-permute-done.16
  91.8 3.2 %collective-permute-done.27 = f32[128,256]{1,0:T(8,128)S(1)} collective-permute-done((f32[128,256]{1,0:T(8,128)S(1)}, f32[128,256]{1,0:T(8,128)S(1)}, u32[]{:S(2)}, u32[]{:S(2)}) %collective-permute-start.27) | collective-permute-done | bytes 131104 | tf_op jit(solution)/shard_map/ppermute | solution.py:285
  95.0 4.5 %collective-permute-done.26 = f32[128,256]{1,0:T(8,128)S(1)} collective-permute-done((f32[128,256]{1,0:T(8,128)S(1)}, f32[128,256]{1,0:T(8,128)S(1)}, u32[]{:S(2)}, u32[]{:S(2)}) %collective-permute-start.26) | collective-permute-done | bytes 131104 | tf_op jit(solution)/shard_map/ppermute | solution.py:285
  99.5 0.0 collective-permute-done.25
  99.5 0.3 fusion
  99.8 0.4 fusion.11
  100.2 0.8 copy.11
  (21 shorter events, 0.2 us)
Async XLA Ops:
  0.0 99.5 %copy-start = (f32[1024,128]{1,0:T(8,128)S(1)}, f32[1024,128]{1,0:T(8,128)}, u32[]{:S(2)}) copy-start(f32[1024,128]{1,0:T(8,128)} %param.10) | copy-start | bytes 1572868
  0.0 18.8 %collective-permute-start.2 = (f32[128,256]{1,0:T(8,128)}, f32[128,256]{1,0:T(8,128)S(1)}, u32[]{:S(2)}, u32[]{:S(2)}) collective-permute-start(f32[128,256]{1,0:T(8,128)} %param.8), channel_id=1, source_target_pairs={{0,24},{1,25},{2,26},{3,27},{4,28},{5,29},{6,30},{7,31},{8,0},{9,1... | collective-permute-start | bytes 393224 | tf_op jit(solution)/shard_map/ppermute | solution.py:285
  5.1 13.8 %collective-permute-start.1 = (f32[128,256]{1,0:T(8,128)}, f32[128,256]{1,0:T(8,128)S(1)}, u32[]{:S(2)}, u32[]{:S(2)}) collective-permute-start(f32[128,256]{1,0:T(8,128)} %param.8), channel_id=1, source_target_pairs={{0,16},{1,17},{2,18},{3,19},{4,20},{5,21},{6,22},{7,23},{8,24},{9,... | collective-permute-start | bytes 393224 | tf_op jit(solution)/shard_map/ppermute | solution.py:285
  5.1 13.8 %collective-permute-start = (f32[128,256]{1,0:T(8,128)}, f32[128,256]{1,0:T(8,128)S(1)}, u32[]{:S(2)}, u32[]{:S(2)}) collective-permute-start(f32[128,256]{1,0:T(8,128)} %param.8), channel_id=1, source_target_pairs={{0,8},{1,9},{2,10},{3,11},{4,12},{5,13},{6,14},{7,15},{8,16},{9,17... | collective-permute-start | bytes 393224 | tf_op jit(solution)/shard_map/ppermute | solution.py:285
  6.1 5.3 %collective-permute-start.3 = (f32[128,256]{1,0:T(8,128)}, f32[128,256]{1,0:T(8,128)S(1)}, u32[]{:S(2)}, u32[]{:S(2)}) collective-permute-start(f32[128,256]{1,0:T(8,128)} %param.8), channel_id=1, source_target_pairs={{0,4},{1,5},{2,6},{3,7},{4,0},{5,1},{6,2},{7,3},{8,12},{9,13},{10,... | collective-permute-start | bytes 393224 | tf_op jit(solution)/shard_map/ppermute | solution.py:285
  7.6 5.2 %collective-permute-start.4 = (f32[128,256]{1,0:T(8,128)}, f32[128,256]{1,0:T(8,128)S(1)}, u32[]{:S(2)}, u32[]{:S(2)}) collective-permute-start(f32[128,256]{1,0:T(8,128)} %param.8), channel_id=1, source_target_pairs={{0,2},{1,3},{2,0},{3,1},{4,6},{5,7},{6,4},{7,5},{8,10},{9,11},{10,... | collective-permute-start | bytes 393224 | tf_op jit(solution)/shard_map/ppermute | solution.py:285
  12.8 7.2 %collective-permute-start.5 = (f32[128,256]{1,0:T(8,128)S(1)}, f32[128,256]{1,0:T(8,128)S(1)}, u32[]{:S(2)}, u32[]{:S(2)}) collective-permute-start(f32[128,256]{1,0:T(8,128)S(1)} %broadcast_select_fusion.1), channel_id=1, source_target_pairs={{0,2},{1,5},{2,0},{3,7},{4,6},{5,1},{6,4},{7,3},{8,10},{9,13},{10,... | collective-permute-start | bytes 393224 | tf_op jit(solution)/shard_map/ppermute | solution.py:285
  14.4 2.8 %copy-start.1 = (f32[6,16,128,128]{3,2,1,0:T(8,128)S(1)}, f32[6,16,128,128]{3,2,1,0:T(8,128)}, u32[]{:S(2)}) copy-start(f32[6,16,128,128]{3,2,1,0:T(8,128)} %param.9) | copy-start | bytes 18874372
  17.2 2.8 %copy-start.2 = (f32[128,256]{1,0:T(8,128)S(1)}, f32[128,256]{1,0:T(8,128)}, u32[]{:S(2)}) copy-start(f32[128,256]{1,0:T(8,128)} %param.8) | copy-start | bytes 393220
  18.9 8.1 %collective-permute-start.8 = (f32[3,128,256]{2,1,0:T(8,128)S(1)}, f32[3,128,256]{2,1,0:T(8,128)S(1)}, u32[]{:S(2)}, u32[]{:S(2)}) collective-permute-start(f32[3,128,256]{2,1,0:T(8,128)S(1)} %pad_maximum_fusion.1.refs_3_), channel_id=1, source_target_pairs={{0,4},{1,5},{2,6},{3,7},{4,0},{5,1},{6,2},{7,3},{8,12},{9,13},{10,... | collective-permute-start | bytes 1179656 | tf_op jit(solution)/shard_map/ppermute | solution.py:285
  19.5 8.7 %collective-permute-start.9 = (f32[3,128,256]{2,1,0:T(8,128)S(1)}, f32[3,128,256]{2,1,0:T(8,128)S(1)}, u32[]{:S(2)}, u32[]{:S(2)}) collective-permute-start(f32[3,128,256]{2,1,0:T(8,128)S(1)} %pad_maximum_fusion.1.refs_3_), channel_id=1, source_target_pairs={{0,2},{1,3},{2,0},{3,1},{4,6},{5,7},{6,4},{7,5},{8,10},{9,11},{10,... | collective-permute-start | bytes 1179656 | tf_op jit(solution)/shard_map/ppermute | solution.py:285
  20.1 10.4 %collective-permute-start.6 = (f32[4,128,256]{2,1,0:T(8,128)S(1)}, f32[4,128,256]{2,1,0:T(8,128)S(1)}, u32[]{:S(2)}, u32[]{:S(2)}) collective-permute-start(f32[4,128,256]{2,1,0:T(8,128)S(1)} %pad_maximum_fusion.refs_1_), channel_id=1, source_target_pairs={{0,1},{1,0},{2,3},{3,2},{4,5},{5,4},{6,7},{7,6},{8,9},{9,8},{10,11... | collective-permute-start | bytes 1572872 | tf_op jit(solution)/shard_map/ppermute | solution.py:285
  20.1 10.3 %collective-permute-start.7 = (f32[3,128,256]{2,1,0:T(8,128)S(1)}, f32[3,128,256]{2,1,0:T(8,128)S(1)}, u32[]{:S(2)}, u32[]{:S(2)}) collective-permute-start(f32[3,128,256]{2,1,0:T(8,128)S(1)} %pad_maximum_fusion.1.refs_3_), channel_id=1, source_target_pairs={{0,1},{1,0},{2,3},{3,2},{4,5},{5,4},{6,7},{7,6},{8,9},{9,8},{10,11... | collective-permute-start | bytes 1179656 | tf_op jit(solution)/shard_map/ppermute | solution.py:285
  28.3 15.1 %collective-permute-start.12 = (f32[3,128,256]{2,1,0:T(8,128)S(1)}, f32[3,128,256]{2,1,0:T(8,128)S(1)}, u32[]{:S(2)}, u32[]{:S(2)}) collective-permute-start(f32[3,128,256]{2,1,0:T(8,128)S(1)} %broadcast_select_fusion), channel_id=1, source_target_pairs={{0,2},{1,5},{2,0},{3,7},{4,6},{5,1},{6,4},{7,3},{8,10},{9,13},{10,... | collective-permute-start | bytes 1179656 | tf_op jit(solution)/shard_map/ppermute | solution.py:285
  29.9 13.8 %collective-permute-start.10 = (f32[3,128,256]{2,1,0:T(8,128)S(1)}, f32[3,128,256]{2,1,0:T(8,128)S(1)}, u32[]{:S(2)}, u32[]{:S(2)}) collective-permute-start(f32[3,128,256]{2,1,0:T(8,128)S(1)} %collective-permute-done.8.refs_2_), channel_id=1, source_target_pairs={{0,1},{1,0},{2,3},{3,2},{4,5},{5,4},{6,7},{7,6},{8,9},{9,8},{10,11... | collective-permute-start | bytes 1179656 | tf_op jit(solution)/shard_map/ppermute | solution.py:285
  29.9 13.8 %collective-permute-start.11 = (f32[3,128,256]{2,1,0:T(8,128)S(1)}, f32[3,128,256]{2,1,0:T(8,128)S(1)}, u32[]{:S(2)}, u32[]{:S(2)}) collective-permute-start(f32[3,128,256]{2,1,0:T(8,128)S(1)} %collective-permute-done.9.refs_3_), channel_id=1, source_target_pairs={{0,1},{1,0},{2,3},{3,2},{4,5},{5,4},{6,7},{7,6},{8,9},{9,8},{10,11... | collective-permute-start | bytes 1179656 | tf_op jit(solution)/shard_map/ppermute | solution.py:285
  43.4 10.5 %collective-permute-start.13 = (f32[3,128,256]{2,1,0:T(8,128)S(1)}, f32[3,128,256]{2,1,0:T(8,128)S(1)}, u32[]{:S(2)}, u32[]{:S(2)}) collective-permute-start(f32[3,128,256]{2,1,0:T(8,128)S(1)} %collective-permute-done.12.refs_2_), channel_id=1, source_target_pairs={{0,1},{1,0},{2,3},{3,2},{4,5},{5,4},{6,7},{7,6},{8,9},{9,8},{10,11... | collective-permute-start | bytes 1179656 | tf_op jit(solution)/shard_map/ppermute | solution.py:285
  58.8 3.9 %collective-permute-start.20 = (f32[3,128,256]{2,1,0:T(8,128)S(1)}, f32[3,128,256]{2,1,0:T(8,128)S(1)}, u32[]{:S(2)}, u32[]{:S(2)}) collective-permute-start(f32[3,128,256]{2,1,0:T(8,128)S(1)} %get-tuple-element.28), channel_id=1, source_target_pairs={{0,1},{1,0},{2,3},{3,2},{4,5},{5,4},{6,7},{7,6},{8,9},{9,8},{10,11... | collective-permute-start | bytes 1179656 | tf_op jit(solution)/shard_map/ppermute | solution.py:285
  61.4 5.1 %collective-permute-start.14 = (f32[4,128,256]{2,1,0:T(8,128)S(1)}, f32[4,128,256]{2,1,0:T(8,128)S(1)}, u32[]{:S(2)}, u32[]{:S(2)}) collective-permute-start(f32[4,128,256]{2,1,0:T(8,128)S(1)} %get-tuple-element.22), channel_id=1, source_target_pairs={{0,1},{1,0},{2,3},{3,2},{4,5},{5,4},{6,7},{7,6},{8,9},{9,8},{10,11... | collective-permute-start | bytes 1572872 | tf_op jit(solution)/shard_map/ppermute | solution.py:285
  61.5 5.1 %collective-permute-start.19 = (f32[3,128,256]{2,1,0:T(8,128)S(1)}, f32[3,128,256]{2,1,0:T(8,128)S(1)}, u32[]{:S(2)}, u32[]{:S(2)}) collective-permute-start(f32[3,128,256]{2,1,0:T(8,128)S(1)} %get-tuple-element.26), channel_id=1, source_target_pairs={{0,1},{1,0},{2,3},{3,2},{4,5},{5,4},{6,7},{7,6},{8,9},{9,8},{10,11... | collective-permute-start | bytes 1179656 | tf_op jit(solution)/shard_map/ppermute | solution.py:285
  61.9 4.7 %collective-permute-start.23 = (f32[3,128,256]{2,1,0:T(8,128)S(1)}, f32[3,128,256]{2,1,0:T(8,128)S(1)}, u32[]{:S(2)}, u32[]{:S(2)}) collective-permute-start(f32[3,128,256]{2,1,0:T(8,128)S(1)} %get-tuple-element.30), channel_id=1, source_target_pairs={{0,1},{1,0},{2,3},{3,2},{4,5},{5,4},{6,7},{7,6},{8,9},{9,8},{10,11... | collective-permute-start | bytes 1179656 | tf_op jit(solution)/shard_map/ppermute | solution.py:285
  62.8 9.4 %collective-permute-start.21 = (f32[3,128,256]{2,1,0:T(8,128)S(1)}, f32[3,128,256]{2,1,0:T(8,128)S(1)}, u32[]{:S(2)}, u32[]{:S(2)}) collective-permute-start(f32[3,128,256]{2,1,0:T(8,128)S(1)} %add.335), channel_id=1, source_target_pairs={{0,2},{1,5},{2,0},{3,7},{4,6},{5,1},{6,4},{7,3},{8,10},{9,13},{10,... | collective-permute-start | bytes 1179656 | tf_op jit(solution)/shard_map/ppermute | solution.py:285
  66.5 20.0 %collective-permute-start.18 = (f32[3,128,256]{2,1,0:T(8,128)S(1)}, f32[3,128,256]{2,1,0:T(8,128)S(1)}, u32[]{:S(2)}, u32[]{:S(2)}) collective-permute-start(f32[3,128,256]{2,1,0:T(8,128)S(1)} %get-tuple-element.24), channel_id=1, source_target_pairs={{0,1},{1,0},{2,3},{3,2},{4,5},{5,4},{6,7},{7,6},{8,9},{9,8},{10,11... | collective-permute-start | bytes 1179656 | tf_op jit(solution)/shard_map/ppermute | solution.py:285
  72.4 14.1 %collective-permute-start.24 = (f32[3,128,256]{2,1,0:T(8,128)S(1)}, f32[3,128,256]{2,1,0:T(8,128)S(1)}, u32[]{:S(2)}, u32[]{:S(2)}) collective-permute-start(f32[3,128,256]{2,1,0:T(8,128)S(1)} %get-tuple-element.42), channel_id=1, source_target_pairs={{0,2},{1,3},{2,0},{3,1},{4,6},{5,7},{6,4},{7,5},{8,10},{9,11},{10,... | collective-permute-start | bytes 1179656 | tf_op jit(solution)/shard_map/ppermute | solution.py:285
  74.5 12.1 %collective-permute-start.22 = (f32[3,128,256]{2,1,0:T(8,128)S(1)}, f32[3,128,256]{2,1,0:T(8,128)S(1)}, u32[]{:S(2)}, u32[]{:S(2)}) collective-permute-start(f32[3,128,256]{2,1,0:T(8,128)S(1)} %get-tuple-element.41), channel_id=1, source_target_pairs={{0,4},{1,5},{2,6},{3,7},{4,0},{5,1},{6,2},{7,3},{8,12},{9,13},{10,... | collective-permute-start | bytes 1179656 | tf_op jit(solution)/shard_map/ppermute | solution.py:285
  74.5 10.2 %collective-permute-start.15 = (f32[128,256]{1,0:T(8,128)S(1)}, f32[128,256]{1,0:T(8,128)S(1)}, u32[]{:S(2)}, u32[]{:S(2)}) collective-permute-start(f32[128,256]{1,0:T(8,128)S(1)} %slice_bitcast_fusion.4), channel_id=1, source_target_pairs={{0,2},{1,5},{2,0},{3,7},{4,6},{5,1},{6,4},{7,3},{8,10},{9,13},{10,... | collective-permute-start | bytes 393224 | tf_op jit(solution)/shard_map/ppermute | solution.py:285
  84.7 6.2 %collective-permute-start.17 = (f32[128,256]{1,0:T(8,128)S(1)}, f32[128,256]{1,0:T(8,128)S(1)}, u32[]{:S(2)}, u32[]{:S(2)}) collective-permute-start(f32[128,256]{1,0:T(8,128)S(1)} %get-tuple-element.37), channel_id=1, source_target_pairs={{0,2},{1,3},{2,0},{3,1},{4,6},{5,7},{6,4},{7,5},{8,10},{9,11},{10,... | collective-permute-start | bytes 393224 | tf_op jit(solution)/shard_map/ppermute | solution.py:285
  86.5 5.3 %collective-permute-start.16 = (f32[128,256]{1,0:T(8,128)S(1)}, f32[128,256]{1,0:T(8,128)S(1)}, u32[]{:S(2)}, u32[]{:S(2)}) collective-permute-start(f32[128,256]{1,0:T(8,128)S(1)} %get-tuple-element.36), channel_id=1, source_target_pairs={{0,4},{1,5},{2,6},{3,7},{4,0},{5,1},{6,2},{7,3},{8,12},{9,13},{10,... | collective-permute-start | bytes 393224 | tf_op jit(solution)/shard_map/ppermute | solution.py:285
  86.7 8.3 %collective-permute-start.27 = (f32[128,256]{1,0:T(8,128)S(1)}, f32[128,256]{1,0:T(8,128)S(1)}, u32[]{:S(2)}, u32[]{:S(2)}) collective-permute-start(f32[128,256]{1,0:T(8,128)S(1)} %get-tuple-element.39), channel_id=1, source_target_pairs={{0,8},{1,9},{2,10},{3,11},{4,12},{5,13},{6,14},{7,15},{8,16},{9,17... | collective-permute-start | bytes 393224 | tf_op jit(solution)/shard_map/ppermute | solution.py:285
  88.3 11.2 %collective-permute-start.26 = (f32[128,256]{1,0:T(8,128)S(1)}, f32[128,256]{1,0:T(8,128)S(1)}, u32[]{:S(2)}, u32[]{:S(2)}) collective-permute-start(f32[128,256]{1,0:T(8,128)S(1)} %get-tuple-element.40), channel_id=1, source_target_pairs={{0,16},{1,17},{2,18},{3,19},{4,20},{5,21},{6,22},{7,23},{8,24},{9,... | collective-permute-start | bytes 393224 | tf_op jit(solution)/shard_map/ppermute | solution.py:285
  90.1 9.4 %collective-permute-start.25 = (f32[128,256]{1,0:T(8,128)S(1)}, f32[128,256]{1,0:T(8,128)S(1)}, u32[]{:S(2)}, u32[]{:S(2)}) collective-permute-start(f32[128,256]{1,0:T(8,128)S(1)} %get-tuple-element.38), channel_id=1, source_target_pairs={{0,24},{1,25},{2,26},{3,27},{4,28},{5,29},{6,30},{7,31},{8,0},{9,1... | collective-permute-start | bytes 393224 | tf_op jit(solution)/shard_map/ppermute | solution.py:285

commit v2 on v1

--- a/solution.py
+++ b/solution.py
@@ -131,7 +131,7 @@
 
 MIB = 1 << 20
 UNROLL = 4
-ROW_STAGE, ROW_LEFT, ROW_RIGHT, ROW_SHARD, ROW_PART, ROW_A, ROW_AC, ROW_B, ROW_BC = range(9)
+ROW_STAGE, ROW_SHARD, ROW_PART, ROW_LEFT, ROW_RIGHT, ROW_A, ROW_AC, ROW_B, ROW_BC = range(9)
 
 
 def split(x):
@@ -162,13 +162,13 @@
     rows = p * w
     return pl.pallas_call(
         prep_kernel,
-        in_specs=[pl.BlockSpec(memory_space=pl.ANY)],
+        in_specs=[pl.BlockSpec(memory_space=pltpu.HBM)],
         out_specs=pl.BlockSpec(memory_space=pltpu.VMEM),
         out_shape=jax.ShapeDtypeStruct((s, rows, 2 * w), jnp.bfloat16),
         scratch_shapes=[pltpu.VMEM((s, rows, w), jnp.float32), pltpu.SemaphoreType.DMA((s,))],
-        compiler_params=pltpu.CompilerParams(vmem_limit_bytes=16 * MIB),
+        compiler_params=pltpu.CompilerParams(vmem_limit_bytes=8 * MIB),
         cost_estimate=pl.CostEstimate(flops=2 * factors.size, bytes_accessed=8 * factors.size, transcendentals=0),
-    )(factors.reshape(s, rows, w))
+    )(pltpu.with_memory_space_constraint(factors.reshape(s, rows, w), pltpu.HBM))
 
 
 def task_kernel(stage, first, firsts, cuts, tab, *refs):
@@ -241,7 +241,13 @@
         return carry
 
     lax.fori_loop(0, count // UNROLL, many, 0)
-    lax.fori_loop(count // UNROLL * UNROLL, count, single, 0)
+    done = count // UNROLL * UNROLL
+
+    @pl.when(count - done >= 2)
+    def _():
+        several(done, 2)
+
+    lax.fori_loop(count // 2 * 2, count, single, 0)
     if cuts:
         for start, out in zip(cuts, outs):
             out[...] = sums[start : start + out.shape[0]]
@@ -268,7 +274,7 @@
             pltpu.VMEM((tasks, w, w), jnp.float32),
             pltpu.SemaphoreType.DMA((tasks,)),
         ],
-        compiler_params=pltpu.CompilerParams(vmem_limit_bytes=20 * MIB),
+        compiler_params=pltpu.CompilerParams(vmem_limit_bytes=12 * MIB),
         cost_estimate=pl.CostEstimate(flops=tasks * f2.shape[1] * w * w * 4, bytes_accessed=2 * f2.size, transcendentals=0),
     )(table, f2, *([] if first else [sums]), *stacks)
 
@@ -302,7 +308,7 @@
 
 
 def across_z(step):
-    return lambda z, x, y, c: (z + step, x, y, c)
+    return lambda z, x, y, c: (z ^ step, x, y, c)
 
 
 def gathered(
@@ -323,10 +329,10 @@
     task_count = slot_pairs.shape[0]
     per_block = tiles_all // aux_count
     depth = tiles_all // 2
-    far = depth - 1
+    chunks = depth // 2
     sizes = (depth, 2, aux_count // 2, 2)
-    z_me, x_me = tile_me // 2, tile_me % 2
-    y_me, core_me = aux_me // 2, aux_me % 2
+    z_me, x_me = tile_me >> 1, tile_me & 1
+    y_me, core_me = aux_me >> 1, aux_me & 1
     on_first = core_me == 0
 
     def move(value, how):
@@ -337,62 +343,77 @@
     def own(table):
         return lax.dynamic_slice_in_dim(table[:, 0], start, task_count)
 
-    def place(row, column, sign):
+    def place(row, column):
         aux = column // per_block
-        dz = (sign * (z_me - row // 2)) & (depth - 1) if depth & far == 0 else (sign * (z_me - row // 2)) % depth
-        side = ((aux // 2) ^ y_me) * 2 + ((row & 1) ^ x_me)
-        shard = ((aux & 1) ^ core_me) * 4 * depth + jnp.where(dz == 0, side, 3 + side * far + dz)
-        stage = jnp.where((dz == 0) | (side == 0), 0, jnp.where(side == 3, 2, 1))
-        return stage, shard, column % per_block
+        side = ((aux >> 1) ^ y_me) * 2 + ((row & 1) ^ x_me)
+        return (aux & 1) ^ core_me, (row >> 1) ^ z_me, side, column % per_block
+
+    def source_of(row, column):
+        dc, dz, side, part = place(row, column)
+        stage = jnp.where(side > 0, 1, 0) + jnp.where(side == 3, 1, 0) + jnp.where(dz > 1, 1, 0)
+        return stage, ((dc * chunks + (dz >> 1)) * 4 + side) * 2 + (dz & 1), part
+
+    def target_of(row, column):
+        dc, dz, side, part = place(row, column)
+        turn = (chunks - 1 - (dz >> 1)) * 2
+        straight = jnp.where(side == 0, 3 * depth, 0) + turn + (dz & 1)
+        sideways = depth + turn * 2 + (side - 1) * 2 + (dz & 1)
+        at = jnp.where((side == 1) | (side == 2), sideways, straight)
+        return dc * 4 * depth + at, part
 
     row_a, col_b = own(target_row), own(target_column)
-    stage, source, part = place(own(density_source), own(density_column), 1)
-    _, shard_a, part_a = place(row_a, col_b, 1)
-    _, shard_b, part_b = place(col_b, row_a, 1)
-    table = jnp.stack([stage, slot_pairs[:, 0], slot_pairs[:, 1], source, part, shard_a, part_a, shard_b, part_b])
-
-    column = [move(density, across_z(step)) for step in range(1, depth)]
-    near_x, near_y = move(density, across_x), move(density, across_y)
-    near_d = move(jnp.where(on_first, near_x, near_y), across_diagonal)
-    near = jnp.stack([density, near_x, near_y, near_d])
-    near_c = move(near, across_core)
+    rows = [
+        *source_of(own(density_source), own(density_column)),
+        slot_pairs[:, 0],
+        slot_pairs[:, 1],
+        *target_of(row_a, col_b),
+        *target_of(col_b, row_a),
+    ]
+    which = lax.broadcasted_iota(jnp.int32, (len(rows), task_count), 0)
+    table = sum(jnp.where(which == at, row[None, :], 0) for at, row in enumerate(rows))
+
+    column = [density] + [move(density, across_z(step)) for step in range(1, depth)]
     split_factors = prep(factors)
-    column, split_factors, table = lax.optimization_barrier((jnp.stack(column), split_factors, table))
-    column_c = move(column, across_core)
-    side_x = move(column, across_x)
-    side_y = move(column, across_y)
-    corner = move(jnp.where(on_first, side_x, side_y), across_diagonal)
-    side_xc, side_yc, corner_c = (move(value, across_core) for value in (side_x, side_y, corner))
-
-    firsts = [0, 4, 4 + far, 4 + 2 * far, 4 + 3 * far]
-    other = [first + 4 * depth for first in firsts]
+    by_stage = [([], []) for _ in range(4)]
+    for k in range(chunks):
+        here = jnp.stack(column[2 * k : 2 * k + 2])
+        if k == 0:
+            here, split_factors, on_first = lax.optimization_barrier((here, split_factors, on_first))
+        side_x = move(here, across_x)
+        side_y = move(here, across_y)
+        corner = move(jnp.where(on_first, side_x, side_y), across_diagonal)
+        for side, value in enumerate((here, side_x, side_y, corner)):
+            stage = min(side, 1) + (side == 3) + (k > 0)
+            first = (k * 4 + side) * 2
+            for at, stack in ((first, value), (first + 4 * depth, move(value, across_core))):
+                by_stage[stage][0].append(stack)
+                by_stage[stage][1].append(at)
+
     shape = (8 * depth,) + density.shape
-    (sums,) = run_stage(
-        table, 0, split_factors, [near, near_c, column, column_c], [firsts[0], other[0], firsts[1], other[1]], None, shape
-    )
-    (sums,) = run_stage(
-        table, 1, split_factors, [side_x, side_y, side_xc, side_yc], firsts[2:4] + other[2:4], sums, shape
-    )
-    mine_and_others = run_stage(
-        table, 2, split_factors, [corner, corner_c], [firsts[4], other[4]], sums, shape, firsts + other
-    )
-    mine, others = mine_and_others[:5], mine_and_others[5:]
-
-    corner = mine[4] + move(others[4], across_core)
-    near = mine[0] + move(others[0], across_core)
-    corner_in = move(corner, across_diagonal)
-    near_in = move(near[3], across_diagonal)
-    side_x = mine[2] + move(others[2], across_core)
-    side_y = mine[3] + move(others[3], across_core)
-    column = mine[1] + move(others[1], across_core)
-    side_x = side_x + jnp.where(on_first, corner_in, 0.0)
-    side_y = side_y + jnp.where(on_first, 0.0, corner_in)
-    near_x = near[1] + jnp.where(on_first, near_in, 0.0)
-    near_y = near[2] + jnp.where(on_first, 0.0, near_in)
-    column = column + move(side_x, across_x) + move(side_y, across_y)
-    total = near[0] + move(near_x, across_x) + move(near_y, across_y)
-    for step in range(1, depth):
-        total = total + move(column[step - 1], across_z(-step))
+    groups = [0, depth] + [depth + 4 * k for k in range(1, chunks)] + [3 * depth]
+    sums = None
+    for stage, (values, firsts) in enumerate(by_stage):
+        cuts = groups + [4 * depth + at for at in groups] if stage == 3 else ()
+        results = run_stage(table, stage, split_factors, values, firsts, sums, shape, cuts)
+        sums = results[0]
+    mine, others = results[: len(groups)], results[len(groups) :]
+
+    merged = [a + move(b, across_core) for a, b in zip(mine, others)]
+    column = merged[-1]
+    total = None
+    corners = []
+    for turn in range(chunks):
+        corners.append(move(merged[0][2 * turn : 2 * turn + 2], across_diagonal))
+    for turn in range(chunks):
+        sides = merged[1 + turn]
+        side_x = sides[:2] + jnp.where(on_first, corners[turn], 0.0)
+        side_y = sides[2:] + jnp.where(on_first, 0.0, corners[turn])
+        here = column[2 * turn : 2 * turn + 2]
+        here = here + move(side_x, across_x) + move(side_y, across_y)
+        for bit in range(2):
+            step = (chunks - 1 - turn) * 2 + bit
+            value = move(here[bit], across_z(step)) if step else here[bit]
+            total = value if total is None else total + value
 
     blocks_x = orthogonalizers.reshape(tiles_all, tile_width, tile_width)
     left_x = blocks_x[tile_me]
@@ -407,8 +428,8 @@
     tiles_all = lax.axis_size("tile")
     aux_count = lax.axis_size("aux")
     whole = density.size * density.dtype.itemsize * tiles_all * aux_count
-    pairs = tiles_all % 2 == 0 and aux_count == 4 and tiles_all % aux_count == 0
-    if pairs and whole <= GATHER_LIMIT:
+    cube = aux_count == 4 and tiles_all >= aux_count and tiles_all & (tiles_all - 1) == 0
+    if cube and whole <= GATHER_LIMIT:
         return gathered(density, *rest)
     return routed(density, *rest)
 

time: 102 us -> 98.6 us (0.967)
  Pallas kernels: 29.6 us -> 34.3 us
  waiting for transfers between devices: 34.2 us -> 31.1 us
  local copies, waits for them, and re-layouts: 4.39 us -> 1.59 us
  starting transfers between devices: 29.7 us -> 28.2 us
    pallas_call x3 -> x4, Pallas kernels: 28 us -> 31.2 us  [run_stage(): pl.pallas_call(body, in_specs=[pl.BlockSpec(memory_space=pltpu.SMEM)] + [...]
    ppermute x28 -> x30, waiting for transfers between devices: 34.2 us -> 31.1 us  [shift(): return lax.ppermute(value, AXES, pairs)]
    unnamed x6 -> x4, local copies, waits for them, and re-layouts: 2.79 us -> 0.01 us
    ppermute x28 -> x30, starting transfers between devices: 29.7 us -> 28.2 us  [shift(): return lax.ppermute(value, AXES, pairs)]
    pallas_call x1, Pallas kernels: 1.62 us -> 3.07 us  [prep(): pl.pallas_call(prep_kernel, in_specs=[pl.BlockSpec(memory_space=pltpu.HBM...]
    add x6 -> x10, other arithmetic: 1.21 us -> 2.11 us  [the longest x1 0.81 us: source_of(): jnp.where(side > 0, 1, 0) + jnp.where(side == 3, 1, 0)]
  transfers between devices with their start and end apart: 28 -> 30, of which waited for: 10 -> 14; matrix products, arithmetic and copies ran while one was open for 3% -> 3% of each run, Pallas kernels for 24% -> 30%
where the time goes in v2:
time: 98.6 us; the launch traced here: 98.4 us
  Pallas kernels  34.3 us (35%)
  waiting for transfers between devices  31.1 us (32%)
  starting transfers between devices  28.2 us (29%)
  other arithmetic  2.26 us (2%)
  local copies, waits for them, and re-layouts  1.59 us (2%)
    pallas_call x4, Pallas kernels, run_stage(): pl.pallas_call(body, in_specs=[pl.BlockSpec(memory_space=pltpu.SMEM)] + [...  31.2 us
    ppermute x30, waiting for transfers between devices, shift(): return lax.ppermute(value, AXES, pairs)  31.1 us
    ppermute x30, starting transfers between devices, shift(): return lax.ppermute(value, AXES, pairs)  28.2 us
    pallas_call x1, Pallas kernels, prep(): pl.pallas_call(prep_kernel, in_specs=[pl.BlockSpec(memory_space=pltpu.HBM...  3.07 us
  transfers between devices with their start and end apart: 30, of which 14 were waited for; matrix products, arithmetic and copies ran while one was open for 3% of the time, Pallas kernels for 30%

profile of v2, /device:TPU:0, one launch (start us, length us, event | category | flops | bytes accessed | tf_op | source)
XLA Modules:
  0.0 98.4 jit_solution(6735634269513908302)
XLA Ops:
  0.0 3.1 %collective-permute-start = (f32[128,256]{1,0:T(8,128)}, f32[128,256]{1,0:T(8,128)S(1)}, u32[]{:S(2)}, u32[]{:S(2)}) collective-permute-start(f32[128,256]{1,0:T(8,128)} %param.8), channel_id=1, source_target_pairs={{0,8},{1,9},{2,10},{3,11},{4,12},{5,13},{6,14},{7,15},{8,0},{9,1},... | collective-permute-start | bytes 393224 | tf_op jit(solution)/shard_map/ppermute | solution.py:291
  3.1 2.6 %collective-permute-start.6 = (f32[128,256]{1,0:T(8,128)}, f32[128,256]{1,0:T(8,128)S(1)}, u32[]{:S(2)}, u32[]{:S(2)}) collective-permute-start(f32[128,256]{1,0:T(8,128)} %param.8), channel_id=1, source_target_pairs={{0,16},{1,17},{2,18},{3,19},{4,20},{5,21},{6,22},{7,23},{8,24},{9,... | collective-permute-start | bytes 393224 | tf_op jit(solution)/shard_map/ppermute | solution.py:291
  5.6 0.0 collective-permute-start.7
  5.7 0.8 fusion.18
  6.5 0.8 slice_bitcast_fusion.5
  7.3 0.7 bitcast_add_fusion
  8.0 0.0 copy-start.1
  8.0 3.1 %shard_map.82.refs_0_ = bf16[6,2048,256]{2,1,0:T(8,128)(2,1)S(1)} custom-call(f32[6,2048,128]{2,1,0:T(8,128)} %bitcast.93), custom_call_target="tpu_custom_call" | custom-call | flops 3145728 | bytes 12582912 | tf_op jit(solution)/shard_map/pallas_call | solution.py:163
  11.1 0.0 collective-permute-done
  11.2 1.8 %collective-permute-start.2 = (f32[2,128,256]{2,1,0:T(8,128)S(1)}, f32[2,128,256]{2,1,0:T(8,128)S(1)}, u32[]{:S(2)}, u32[]{:S(2)}) collective-permute-start(f32[2,128,256]{2,1,0:T(8,128)S(1)} %pad_maximum_fusion.refs_1_), channel_id=1, source_target_pairs={{0,4},{1,5},{2,6},{3,7},{4,0},{5,1},{6,2},{7,3},{8,12},{9,13},{10,... | collective-permute-start | bytes 786440 | tf_op jit(solution)/shard_map/ppermute | solution.py:291
  12.9 1.5 %collective-permute-start.4 = (f32[2,128,256]{2,1,0:T(8,128)S(1)}, f32[2,128,256]{2,1,0:T(8,128)S(1)}, u32[]{:S(2)}, u32[]{:S(2)}) collective-permute-start(f32[2,128,256]{2,1,0:T(8,128)S(1)} %pad_maximum_fusion.refs_1_), channel_id=1, source_target_pairs={{0,2},{1,3},{2,0},{3,1},{4,6},{5,7},{6,4},{7,5},{8,10},{9,11},{10,... | collective-permute-start | bytes 786440 | tf_op jit(solution)/shard_map/ppermute | solution.py:291
  14.5 1.7 %collective-permute-done.6 = f32[128,256]{1,0:T(8,128)S(1)} collective-permute-done((f32[128,256]{1,0:T(8,128)}, f32[128,256]{1,0:T(8,128)S(1)}, u32[]{:S(2)}, u32[]{:S(2)}) %collective-permute-start.6) | collective-permute-done | bytes 131104 | tf_op jit(solution)/shard_map/ppermute | solution.py:291
  16.2 0.0 collective-permute-done.7
  16.2 1.6 %collective-permute-start.11 = (f32[2,128,256]{2,1,0:T(8,128)S(1)}, f32[2,128,256]{2,1,0:T(8,128)S(1)}, u32[]{:S(2)}, u32[]{:S(2)}) collective-permute-start(f32[2,128,256]{2,1,0:T(8,128)S(1)} %pad_maximum_fusion.1.refs_6_), channel_id=1, source_target_pairs={{0,4},{1,5},{2,6},{3,7},{4,0},{5,1},{6,2},{7,3},{8,12},{9,13},{10,... | collective-permute-start | bytes 786440 | tf_op jit(solution)/shard_map/ppermute | solution.py:291
  17.7 1.5 %collective-permute-start.13 = (f32[2,128,256]{2,1,0:T(8,128)S(1)}, f32[2,128,256]{2,1,0:T(8,128)S(1)}, u32[]{:S(2)}, u32[]{:S(2)}) collective-permute-start(f32[2,128,256]{2,1,0:T(8,128)S(1)} %pad_maximum_fusion.1.refs_6_), channel_id=1, source_target_pairs={{0,2},{1,3},{2,0},{3,1},{4,6},{5,7},{6,4},{7,5},{8,10},{9,11},{10,... | collective-permute-start | bytes 786440 | tf_op jit(solution)/shard_map/ppermute | solution.py:291
  19.3 0.1 select_add_fusion.tab
  19.3 0.1 collective-permute-start.1
  19.4 1.0 collective-permute-done.2.refs_2_
  20.4 0.0 collective-permute-start.8
  20.4 1.7 %collective-permute-done.4.refs_4_ = f32[2,128,256]{2,1,0:T(8,128)S(1)} collective-permute-done((f32[2,128,256]{2,1,0:T(8,128)S(1)}, f32[2,128,256]{2,1,0:T(8,128)S(1)}, u32[]{:S(2)}, u32[]{:S(2)}) %collective-permute-start.4) | collective-permute-done | bytes 262176 | tf_op jit(solution)/shard_map/ppermute | solution.py:291
  22.1 1.6 %collective-permute-start.9 = (f32[2,128,256]{2,1,0:T(8,128)S(1)}, f32[2,128,256]{2,1,0:T(8,128)S(1)}, u32[]{:S(2)}, u32[]{:S(2)}) collective-permute-start(f32[2,128,256]{2,1,0:T(8,128)S(1)} %broadcast_select_fusion.1), channel_id=1, source_target_pairs={{0,2},{1,5},{2,0},{3,7},{4,6},{5,1},{6,4},{7,3},{8,10},{9,13},{10,... | collective-permute-start | bytes 786440 | tf_op jit(solution)/shard_map/ppermute | solution.py:291
  23.7 1.3 %collective-permute-done.11.refs_4_ = f32[2,128,256]{2,1,0:T(8,128)S(1)} collective-permute-done((f32[2,128,256]{2,1,0:T(8,128)S(1)}, f32[2,128,256]{2,1,0:T(8,128)S(1)}, u32[]{:S(2)}, u32[]{:S(2)}) %collective-permute-start.11) | collective-permute-done | bytes 262176 | tf_op jit(solution)/shard_map/ppermute | solution.py:291
  25.0 0.5 collective-permute-done.13.refs_6_
  25.6 1.6 %collective-permute-start.15 = (f32[2,128,256]{2,1,0:T(8,128)S(1)}, f32[2,128,256]{2,1,0:T(8,128)S(1)}, u32[]{:S(2)}, u32[]{:S(2)}) collective-permute-start(f32[2,128,256]{2,1,0:T(8,128)S(1)} %broadcast_select_fusion), channel_id=1, source_target_pairs={{0,2},{1,5},{2,0},{3,7},{4,6},{5,1},{6,4},{7,3},{8,10},{9,13},{10,... | collective-permute-start | bytes 786440 | tf_op jit(solution)/shard_map/ppermute | solution.py:291
  27.2 0.5 collective-permute-start.5
  27.7 4.4 %shard_map.83.refs_1_ = f32[32,128,256]{2,1,0:T(8,128)S(1)} custom-call(s32[9,32]{1,0:T(8,128)S(1)} %select_add_fusion.tab, bf16[6,2048,256]{2,1,0:T(8,128)(2,1)S(1)} %shard_map.82.refs_0_, f32[2,128,256]{2,1,0:T(8,128)S(1)} %pad_maximum_fusion.refs_1_, f32[2,128,256]{2,1,0:T(8,128)S(1)} %collective-permute-done.1.refs_2_), custom_call_target="tpu_custom_call" | custom-call | flops 4294967296 | bytes 6291456 | tf_op jit(solution)/shard_map/pallas_call | solution.py:266
  32.1 1.7 %collective-permute-start.12 = (f32[2,128,256]{2,1,0:T(8,128)S(1)}, f32[2,128,256]{2,1,0:T(8,128)S(1)}, u32[]{:S(2)}, u32[]{:S(2)}) collective-permute-start(f32[2,128,256]{2,1,0:T(8,128)S(1)} %collective-permute-done.11.refs_4_), channel_id=1, source_target_pairs={{0,1},{1,0},{2,3},{3,2},{4,5},{5,4},{6,7},{7,6},{8,9},{9,8},{10,11... | collective-permute-start | bytes 786440 | tf_op jit(solution)/shard_map/ppermute | solution.py:291
  33.8 0.1 collective-permute-start.14
  33.9 0.4 collective-permute-start.10
  34.3 0.1 collective-permute-start.16
  34.4 11.9 %shard_map.84.refs_1_ = f32[32,128,256]{2,1,0:T(8,128)S(1)} custom-call(s32[9,32]{1,0:T(8,128)S(1)} %select_add_fusion.tab, bf16[6,2048,256]{2,1,0:T(8,128)(2,1)S(1)} %shard_map.82.refs_0_, f32[32,128,256]{2,1,0:T(8,128)S(1)} %shard_map.83.refs_1_, f32[2,128,256]{2,1,0:T(8,128)S(1)} %collective-permute-done.2.refs_2_, ...), custom_call_target="tpu_custom_call" | custom-call | flops 4294967296 | bytes 6291456 | tf_op jit(solution)/shard_map/pallas_call | solution.py:266
  46.4 10.3 %shard_map.85.refs_1_ = f32[32,128,256]{2,1,0:T(8,128)S(1)} custom-call(s32[9,32]{1,0:T(8,128)S(1)} %select_add_fusion.tab, bf16[6,2048,256]{2,1,0:T(8,128)(2,1)S(1)} %shard_map.82.refs_0_, f32[32,128,256]{2,1,0:T(8,128)S(1)} %shard_map.84.refs_1_, f32[2,128,256]{2,1,0:T(8,128)S(1)} %collective-permute-done.9.refs_2_, ...), custom_call_target="tpu_custom_call" | custom-call | flops 4294967296 | bytes 6291456 | tf_op jit(solution)/shard_map/pallas_call | solution.py:266
  56.7 4.6 %shard_map.86 = (f32[4,128,256]{2,1,0:T(8,128)S(1)}, f32[4,128,256]{2,1,0:T(8,128)S(1)}, f32[4,128,256]{2,1,0:T(8,128)S(1)}, f32[4,128,256]{2,1,0:T(8,128)S(1)},...) custom-call(s32[9,32]{1,0:T(8,128)S(1)} %select_add_fusion.tab, ...), custom_call_target="tpu_custom_call" | custom-call | flops 4294967296 | bytes 6291456 | tf_op jit(solution)/shard_map/pallas_call | solution.py:266
  61.3 0.1 collective-permute-start.19
  61.3 0.5 collective-permute-start.25
  61.8 0.1 collective-permute-start.18
  61.9 1.3 %collective-permute-done.19 = f32[4,128,256]{2,1,0:T(8,128)S(1)} collective-permute-done((f32[4,128,256]{2,1,0:T(8,128)S(1)}, f32[4,128,256]{2,1,0:T(8,128)S(1)}, u32[]{:S(2)}, u32[]{:S(2)}) %collective-permute-start.19) | collective-permute-done | bytes 524320 | tf_op jit(solution)/shard_map/ppermute | solution.py:291
  63.2 0.1 add.318
  63.3 0.3 collective-permute-start.26
  63.7 1.8 %collective-permute-start.20 = (f32[2,128,256]{2,1,0:T(8,128)S(1)}, f32[2,128,256]{2,1,0:T(8,128)S(1)}, u32[]{:S(2)}, u32[]{:S(2)}) collective-permute-start(f32[2,128,256]{2,1,0:T(8,128)S(1)} %get-tuple-element.37), channel_id=1, source_target_pairs={{0,2},{1,5},{2,0},{3,7},{4,6},{5,1},{6,4},{7,3},{8,10},{9,13},{10,... | collective-permute-start | bytes 786440 | tf_op jit(solution)/shard_map/ppermute | solution.py:291
  65.4 0.1 add.324
  65.5 0.1 add.317
  65.6 4.2 %collective-permute-done.26 = f32[2,128,256]{2,1,0:T(8,128)S(1)} collective-permute-done((f32[2,128,256]{2,1,0:T(8,128)S(1)}, f32[2,128,256]{2,1,0:T(8,128)S(1)}, u32[]{:S(2)}, u32[]{:S(2)}) %collective-permute-start.26) | collective-permute-done | bytes 262176 | tf_op jit(solution)/shard_map/ppermute | solution.py:291
  69.8 0.1 slice_add_fusion.1
  69.8 0.1 collective-permute-start.27
  69.9 1.0 %collective-permute-start.28 = (f32[2,128,256]{2,1,0:T(8,128)S(1)}, f32[2,128,256]{2,1,0:T(8,128)S(1)}, u32[]{:S(2)}, u32[]{:S(2)}) collective-permute-start(f32[2,128,256]{2,1,0:T(8,128)S(1)} %get-tuple-element.34), channel_id=1, source_target_pairs={{0,2},{1,3},{2,0},{3,1},{4,6},{5,7},{6,4},{7,5},{8,10},{9,11},{10,... | collective-permute-start | bytes 786440 | tf_op jit(solution)/shard_map/ppermute | solution.py:291
  71.0 2.4 %collective-permute-done.20 = f32[2,128,256]{2,1,0:T(8,128)S(1)} collective-permute-done((f32[2,128,256]{2,1,0:T(8,128)S(1)}, f32[2,128,256]{2,1,0:T(8,128)S(1)}, u32[]{:S(2)}, u32[]{:S(2)}) %collective-permute-start.20) | collective-permute-done | bytes 262176 | tf_op jit(solution)/shard_map/ppermute | solution.py:291
  73.3 0.1 slice_add_fusion.4
  73.4 0.1 collective-permute-start.21
  73.5 0.6 collective-permute-start.22
  74.1 0.1 add.316
  74.2 4.9 %collective-permute-done.27 = f32[2,128,256]{2,1,0:T(8,128)S(1)} collective-permute-done((f32[2,128,256]{2,1,0:T(8,128)S(1)}, f32[2,128,256]{2,1,0:T(8,128)S(1)}, u32[]{:S(2)}, u32[]{:S(2)}) %collective-permute-start.27) | collective-permute-done | bytes 262176 | tf_op jit(solution)/shard_map/ppermute | solution.py:291
  79.1 0.1 collective-permute-done.28
  79.2 3.9 %collective-permute-done.21 = f32[2,128,256]{2,1,0:T(8,128)S(1)} collective-permute-done((f32[2,128,256]{2,1,0:T(8,128)S(1)}, f32[2,128,256]{2,1,0:T(8,128)S(1)}, u32[]{:S(2)}, u32[]{:S(2)}) %collective-permute-start.21) | collective-permute-done | bytes 262176 | tf_op jit(solution)/shard_map/ppermute | solution.py:291
  83.0 0.8 collective-permute-done.22
  83.8 0.1 fusion.1
  84.0 2.2 %collective-permute-start.23 = (f32[128,256]{1,0:T(8,128)S(1)}, f32[128,256]{1,0:T(8,128)S(1)}, u32[]{:S(2)}, u32[]{:S(2)}) collective-permute-start(f32[128,256]{1,0:T(8,128)S(1)} %get-tuple-element.40), channel_id=1, source_target_pairs={{0,16},{1,17},{2,18},{3,19},{4,20},{5,21},{6,22},{7,23},{8,24},{9,... | collective-permute-start | bytes 393224 | tf_op jit(solution)/shard_map/ppermute | solution.py:291
  86.2 2.8 %collective-permute-start.24 = (f32[128,256]{1,0:T(8,128)S(1)}, f32[128,256]{1,0:T(8,128)S(1)}, u32[]{:S(2)}, u32[]{:S(2)}) collective-permute-start(f32[128,256]{1,0:T(8,128)S(1)} %get-tuple-element.39), channel_id=1, source_target_pairs={{0,24},{1,25},{2,26},{3,27},{4,28},{5,29},{6,30},{7,31},{8,16},{9,... | collective-permute-start | bytes 393224 | tf_op jit(solution)/shard_map/ppermute | solution.py:291
  89.0 0.6 collective-permute-start.29
  89.6 6.8 %collective-permute-done.23 = f32[128,256]{1,0:T(8,128)S(1)} collective-permute-done((f32[128,256]{1,0:T(8,128)S(1)}, f32[128,256]{1,0:T(8,128)S(1)}, u32[]{:S(2)}, u32[]{:S(2)}) %collective-permute-start.23) | collective-permute-done | bytes 131104 | tf_op jit(solution)/shard_map/ppermute | solution.py:291
  96.4 0.5 collective-permute-done.29
  96.9 0.3 fusion.2
  97.3 0.4 fusion.8
  97.7 0.8 copy.11
  (32 shorter events, 0.3 us)
Async XLA Ops:
  0.0 96.9 %copy-start = (f32[1024,128]{1,0:T(8,128)S(1)}, f32[1024,128]{1,0:T(8,128)}, u32[]{:S(2)}) copy-start(f32[1024,128]{1,0:T(8,128)} %param.10) | copy-start | bytes 1572868
  0.0 11.1 %collective-permute-start = (f32[128,256]{1,0:T(8,128)}, f32[128,256]{1,0:T(8,128)S(1)}, u32[]{:S(2)}, u32[]{:S(2)}) collective-permute-start(f32[128,256]{1,0:T(8,128)} %param.8), channel_id=1, source_target_pairs={{0,8},{1,9},{2,10},{3,11},{4,12},{5,13},{6,14},{7,15},{8,0},{9,1},... | collective-permute-start | bytes 393224 | tf_op jit(solution)/shard_map/ppermute | solution.py:291
  3.1 13.1 %collective-permute-start.6 = (f32[128,256]{1,0:T(8,128)}, f32[128,256]{1,0:T(8,128)S(1)}, u32[]{:S(2)}, u32[]{:S(2)}) collective-permute-start(f32[128,256]{1,0:T(8,128)} %param.8), channel_id=1, source_target_pairs={{0,16},{1,17},{2,18},{3,19},{4,20},{5,21},{6,22},{7,23},{8,24},{9,... | collective-permute-start | bytes 393224 | tf_op jit(solution)/shard_map/ppermute | solution.py:291
  5.6 10.5 %collective-permute-start.7 = (f32[128,256]{1,0:T(8,128)}, f32[128,256]{1,0:T(8,128)S(1)}, u32[]{:S(2)}, u32[]{:S(2)}) collective-permute-start(f32[128,256]{1,0:T(8,128)} %param.8), channel_id=1, source_target_pairs={{0,24},{1,25},{2,26},{3,27},{4,28},{5,29},{6,30},{7,31},{8,16},{9,... | collective-permute-start | bytes 393224 | tf_op jit(solution)/shard_map/ppermute | solution.py:291
  8.0 3.1 %copy-start.1 = (f32[128,256]{1,0:T(8,128)S(1)}, f32[128,256]{1,0:T(8,128)}, u32[]{:S(2)}) copy-start(f32[128,256]{1,0:T(8,128)} %param.8) | copy-start | bytes 393220
  11.2 9.2 %collective-permute-start.2 = (f32[2,128,256]{2,1,0:T(8,128)S(1)}, f32[2,128,256]{2,1,0:T(8,128)S(1)}, u32[]{:S(2)}, u32[]{:S(2)}) collective-permute-start(f32[2,128,256]{2,1,0:T(8,128)S(1)} %pad_maximum_fusion.refs_1_), channel_id=1, source_target_pairs={{0,4},{1,5},{2,6},{3,7},{4,0},{5,1},{6,2},{7,3},{8,12},{9,13},{10,... | collective-permute-start | bytes 786440 | tf_op jit(solution)/shard_map/ppermute | solution.py:291
  12.9 9.2 %collective-permute-start.4 = (f32[2,128,256]{2,1,0:T(8,128)S(1)}, f32[2,128,256]{2,1,0:T(8,128)S(1)}, u32[]{:S(2)}, u32[]{:S(2)}) collective-permute-start(f32[2,128,256]{2,1,0:T(8,128)S(1)} %pad_maximum_fusion.refs_1_), channel_id=1, source_target_pairs={{0,2},{1,3},{2,0},{3,1},{4,6},{5,7},{6,4},{7,5},{8,10},{9,11},{10,... | collective-permute-start | bytes 786440 | tf_op jit(solution)/shard_map/ppermute | solution.py:291
  16.2 8.9 %collective-permute-start.11 = (f32[2,128,256]{2,1,0:T(8,128)S(1)}, f32[2,128,256]{2,1,0:T(8,128)S(1)}, u32[]{:S(2)}, u32[]{:S(2)}) collective-permute-start(f32[2,128,256]{2,1,0:T(8,128)S(1)} %pad_maximum_fusion.1.refs_6_), channel_id=1, source_target_pairs={{0,4},{1,5},{2,6},{3,7},{4,0},{5,1},{6,2},{7,3},{8,12},{9,13},{10,... | collective-permute-start | bytes 786440 | tf_op jit(solution)/shard_map/ppermute | solution.py:291
  17.7 7.8 %collective-permute-start.13 = (f32[2,128,256]{2,1,0:T(8,128)S(1)}, f32[2,128,256]{2,1,0:T(8,128)S(1)}, u32[]{:S(2)}, u32[]{:S(2)}) collective-permute-start(f32[2,128,256]{2,1,0:T(8,128)S(1)} %pad_maximum_fusion.1.refs_6_), channel_id=1, source_target_pairs={{0,2},{1,3},{2,0},{3,1},{4,6},{5,7},{6,4},{7,5},{8,10},{9,11},{10,... | collective-permute-start | bytes 786440 | tf_op jit(solution)/shard_map/ppermute | solution.py:291
  19.3 7.8 %collective-permute-start.1 = (f32[2,128,256]{2,1,0:T(8,128)S(1)}, f32[2,128,256]{2,1,0:T(8,128)S(1)}, u32[]{:S(2)}, u32[]{:S(2)}) collective-permute-start(f32[2,128,256]{2,1,0:T(8,128)S(1)} %pad_maximum_fusion.refs_1_), channel_id=1, source_target_pairs={{0,1},{1,0},{2,3},{3,2},{4,5},{5,4},{6,7},{7,6},{8,9},{9,8},{10,11... | collective-permute-start | bytes 786440 | tf_op jit(solution)/shard_map/ppermute | solution.py:291
  20.4 11.7 %collective-permute-start.8 = (f32[2,128,256]{2,1,0:T(8,128)S(1)}, f32[2,128,256]{2,1,0:T(8,128)S(1)}, u32[]{:S(2)}, u32[]{:S(2)}) collective-permute-start(f32[2,128,256]{2,1,0:T(8,128)S(1)} %pad_maximum_fusion.1.refs_6_), channel_id=1, source_target_pairs={{0,1},{1,0},{2,3},{3,2},{4,5},{5,4},{6,7},{7,6},{8,9},{9,8},{10,11... | collective-permute-start | bytes 786440 | tf_op jit(solution)/shard_map/ppermute | solution.py:291
  22.1 11.8 %collective-permute-start.9 = (f32[2,128,256]{2,1,0:T(8,128)S(1)}, f32[2,128,256]{2,1,0:T(8,128)S(1)}, u32[]{:S(2)}, u32[]{:S(2)}) collective-permute-start(f32[2,128,256]{2,1,0:T(8,128)S(1)} %broadcast_select_fusion.1), channel_id=1, source_target_pairs={{0,2},{1,5},{2,0},{3,7},{4,6},{5,1},{6,4},{7,3},{8,10},{9,13},{10,... | collective-permute-start | bytes 786440 | tf_op jit(solution)/shard_map/ppermute | solution.py:291
  25.6 8.8 %collective-permute-start.15 = (f32[2,128,256]{2,1,0:T(8,128)S(1)}, f32[2,128,256]{2,1,0:T(8,128)S(1)}, u32[]{:S(2)}, u32[]{:S(2)}) collective-permute-start(f32[2,128,256]{2,1,0:T(8,128)S(1)} %broadcast_select_fusion), channel_id=1, source_target_pairs={{0,2},{1,5},{2,0},{3,7},{4,6},{5,1},{6,4},{7,3},{8,10},{9,13},{10,... | collective-permute-start | bytes 786440 | tf_op jit(solution)/shard_map/ppermute | solution.py:291
  27.2 6.6 %collective-permute-start.3 = (f32[2,128,256]{2,1,0:T(8,128)S(1)}, f32[2,128,256]{2,1,0:T(8,128)S(1)}, u32[]{:S(2)}, u32[]{:S(2)}) collective-permute-start(f32[2,128,256]{2,1,0:T(8,128)S(1)} %collective-permute-done.2.refs_2_), channel_id=1, source_target_pairs={{0,1},{1,0},{2,3},{3,2},{4,5},{5,4},{6,7},{7,6},{8,9},{9,8},{10,11... | collective-permute-start | bytes 786440 | tf_op jit(solution)/shard_map/ppermute | solution.py:291
  27.2 7.2 %collective-permute-start.5 = (f32[2,128,256]{2,1,0:T(8,128)S(1)}, f32[2,128,256]{2,1,0:T(8,128)S(1)}, u32[]{:S(2)}, u32[]{:S(2)}) collective-permute-start(f32[2,128,256]{2,1,0:T(8,128)S(1)} %collective-permute-done.4.refs_4_), channel_id=1, source_target_pairs={{0,1},{1,0},{2,3},{3,2},{4,5},{5,4},{6,7},{7,6},{8,9},{9,8},{10,11... | collective-permute-start | bytes 786440 | tf_op jit(solution)/shard_map/ppermute | solution.py:291
  32.1 14.2 %collective-permute-start.12 = (f32[2,128,256]{2,1,0:T(8,128)S(1)}, f32[2,128,256]{2,1,0:T(8,128)S(1)}, u32[]{:S(2)}, u32[]{:S(2)}) collective-permute-start(f32[2,128,256]{2,1,0:T(8,128)S(1)} %collective-permute-done.11.refs_4_), channel_id=1, source_target_pairs={{0,1},{1,0},{2,3},{3,2},{4,5},{5,4},{6,7},{7,6},{8,9},{9,8},{10,11... | collective-permute-start | bytes 786440 | tf_op jit(solution)/shard_map/ppermute | solution.py:291
  33.8 12.6 %collective-permute-start.14 = (f32[2,128,256]{2,1,0:T(8,128)S(1)}, f32[2,128,256]{2,1,0:T(8,128)S(1)}, u32[]{:S(2)}, u32[]{:S(2)}) collective-permute-start(f32[2,128,256]{2,1,0:T(8,128)S(1)} %collective-permute-done.13.refs_6_), channel_id=1, source_target_pairs={{0,1},{1,0},{2,3},{3,2},{4,5},{5,4},{6,7},{7,6},{8,9},{9,8},{10,11... | collective-permute-start | bytes 786440 | tf_op jit(solution)/shard_map/ppermute | solution.py:291
  33.9 12.5 %collective-permute-start.10 = (f32[2,128,256]{2,1,0:T(8,128)S(1)}, f32[2,128,256]{2,1,0:T(8,128)S(1)}, u32[]{:S(2)}, u32[]{:S(2)}) collective-permute-start(f32[2,128,256]{2,1,0:T(8,128)S(1)} %collective-permute-done.9.refs_2_), channel_id=1, source_target_pairs={{0,1},{1,0},{2,3},{3,2},{4,5},{5,4},{6,7},{7,6},{8,9},{9,8},{10,11... | collective-permute-start | bytes 786440 | tf_op jit(solution)/shard_map/ppermute | solution.py:291
  34.3 22.3 %collective-permute-start.16 = (f32[2,128,256]{2,1,0:T(8,128)S(1)}, f32[2,128,256]{2,1,0:T(8,128)S(1)}, u32[]{:S(2)}, u32[]{:S(2)}) collective-permute-start(f32[2,128,256]{2,1,0:T(8,128)S(1)} %collective-permute-done.15.refs_2_), channel_id=1, source_target_pairs={{0,1},{1,0},{2,3},{3,2},{4,5},{5,4},{6,7},{7,6},{8,9},{9,8},{10,11... | collective-permute-start | bytes 786440 | tf_op jit(solution)/shard_map/ppermute | solution.py:291
  61.3 2.0 %collective-permute-start.19 = (f32[4,128,256]{2,1,0:T(8,128)S(1)}, f32[4,128,256]{2,1,0:T(8,128)S(1)}, u32[]{:S(2)}, u32[]{:S(2)}) collective-permute-start(f32[4,128,256]{2,1,0:T(8,128)S(1)} %get-tuple-element.24), channel_id=1, source_target_pairs={{0,1},{1,0},{2,3},{3,2},{4,5},{5,4},{6,7},{7,6},{8,9},{9,8},{10,11... | collective-permute-start | bytes 1572872 | tf_op jit(solution)/shard_map/ppermute | solution.py:291
  61.3 4.1 %collective-permute-start.25 = (f32[4,128,256]{2,1,0:T(8,128)S(1)}, f32[4,128,256]{2,1,0:T(8,128)S(1)}, u32[]{:S(2)}, u32[]{:S(2)}) collective-permute-start(f32[4,128,256]{2,1,0:T(8,128)S(1)} %get-tuple-element.26), channel_id=1, source_target_pairs={{0,1},{1,0},{2,3},{3,2},{4,5},{5,4},{6,7},{7,6},{8,9},{9,8},{10,11... | collective-permute-start | bytes 1572872 | tf_op jit(solution)/shard_map/ppermute | solution.py:291
  61.8 3.7 %collective-permute-start.18 = (f32[4,128,256]{2,1,0:T(8,128)S(1)}, f32[4,128,256]{2,1,0:T(8,128)S(1)}, u32[]{:S(2)}, u32[]{:S(2)}) collective-permute-start(f32[4,128,256]{2,1,0:T(8,128)S(1)} %get-tuple-element.22), channel_id=1, source_target_pairs={{0,1},{1,0},{2,3},{3,2},{4,5},{5,4},{6,7},{7,6},{8,9},{9,8},{10,11... | collective-permute-start | bytes 1572872 | tf_op jit(solution)/shard_map/ppermute | solution.py:291
  63.3 6.4 %collective-permute-start.26 = (f32[2,128,256]{2,1,0:T(8,128)S(1)}, f32[2,128,256]{2,1,0:T(8,128)S(1)}, u32[]{:S(2)}, u32[]{:S(2)}) collective-permute-start(f32[2,128,256]{2,1,0:T(8,128)S(1)} %get-tuple-element.38), channel_id=1, source_target_pairs={{0,2},{1,5},{2,0},{3,7},{4,6},{5,1},{6,4},{7,3},{8,10},{9,13},{10,... | collective-permute-start | bytes 786440 | tf_op jit(solution)/shard_map/ppermute | solution.py:291
  63.7 9.7 %collective-permute-start.20 = (f32[2,128,256]{2,1,0:T(8,128)S(1)}, f32[2,128,256]{2,1,0:T(8,128)S(1)}, u32[]{:S(2)}, u32[]{:S(2)}) collective-permute-start(f32[2,128,256]{2,1,0:T(8,128)S(1)} %get-tuple-element.37), channel_id=1, source_target_pairs={{0,2},{1,5},{2,0},{3,7},{4,6},{5,1},{6,4},{7,3},{8,10},{9,13},{10,... | collective-permute-start | bytes 786440 | tf_op jit(solution)/shard_map/ppermute | solution.py:291
  65.4 8.6 %collective-permute-start.17 = (f32[4,128,256]{2,1,0:T(8,128)S(1)}, f32[4,128,256]{2,1,0:T(8,128)S(1)}, u32[]{:S(2)}, u32[]{:S(2)}) collective-permute-start(f32[4,128,256]{2,1,0:T(8,128)S(1)} %get-tuple-element.20), channel_id=1, source_target_pairs={{0,1},{1,0},{2,3},{3,2},{4,5},{5,4},{6,7},{7,6},{8,9},{9,8},{10,11... | collective-permute-start | bytes 1572872 | tf_op jit(solution)/shard_map/ppermute | solution.py:291
  69.8 9.2 %collective-permute-start.27 = (f32[2,128,256]{2,1,0:T(8,128)S(1)}, f32[2,128,256]{2,1,0:T(8,128)S(1)}, u32[]{:S(2)}, u32[]{:S(2)}) collective-permute-start(f32[2,128,256]{2,1,0:T(8,128)S(1)} %get-tuple-element.33), channel_id=1, source_target_pairs={{0,4},{1,5},{2,6},{3,7},{4,0},{5,1},{6,2},{7,3},{8,12},{9,13},{10,... | collective-permute-start | bytes 786440 | tf_op jit(solution)/shard_map/ppermute | solution.py:291
  69.9 9.2 %collective-permute-start.28 = (f32[2,128,256]{2,1,0:T(8,128)S(1)}, f32[2,128,256]{2,1,0:T(8,128)S(1)}, u32[]{:S(2)}, u32[]{:S(2)}) collective-permute-start(f32[2,128,256]{2,1,0:T(8,128)S(1)} %get-tuple-element.34), channel_id=1, source_target_pairs={{0,2},{1,3},{2,0},{3,1},{4,6},{5,7},{6,4},{7,5},{8,10},{9,11},{10,... | collective-permute-start | bytes 786440 | tf_op jit(solution)/shard_map/ppermute | solution.py:291
  73.4 9.6 %collective-permute-start.21 = (f32[2,128,256]{2,1,0:T(8,128)S(1)}, f32[2,128,256]{2,1,0:T(8,128)S(1)}, u32[]{:S(2)}, u32[]{:S(2)}) collective-permute-start(f32[2,128,256]{2,1,0:T(8,128)S(1)} %get-tuple-element.31), channel_id=1, source_target_pairs={{0,4},{1,5},{2,6},{3,7},{4,0},{5,1},{6,2},{7,3},{8,12},{9,13},{10,... | collective-permute-start | bytes 786440 | tf_op jit(solution)/shard_map/ppermute | solution.py:291
  73.5 10.4 %collective-permute-start.22 = (f32[2,128,256]{2,1,0:T(8,128)S(1)}, f32[2,128,256]{2,1,0:T(8,128)S(1)}, u32[]{:S(2)}, u32[]{:S(2)}) collective-permute-start(f32[2,128,256]{2,1,0:T(8,128)S(1)} %get-tuple-element.32), channel_id=1, source_target_pairs={{0,2},{1,3},{2,0},{3,1},{4,6},{5,7},{6,4},{7,5},{8,10},{9,11},{10,... | collective-permute-start | bytes 786440 | tf_op jit(solution)/shard_map/ppermute | solution.py:291
  84.0 12.4 %collective-permute-start.23 = (f32[128,256]{1,0:T(8,128)S(1)}, f32[128,256]{1,0:T(8,128)S(1)}, u32[]{:S(2)}, u32[]{:S(2)}) collective-permute-start(f32[128,256]{1,0:T(8,128)S(1)} %get-tuple-element.40), channel_id=1, source_target_pairs={{0,16},{1,17},{2,18},{3,19},{4,20},{5,21},{6,22},{7,23},{8,24},{9,... | collective-permute-start | bytes 393224 | tf_op jit(solution)/shard_map/ppermute | solution.py:291
  86.2 10.2 %collective-permute-start.24 = (f32[128,256]{1,0:T(8,128)S(1)}, f32[128,256]{1,0:T(8,128)S(1)}, u32[]{:S(2)}, u32[]{:S(2)}) collective-permute-start(f32[128,256]{1,0:T(8,128)S(1)} %get-tuple-element.39), channel_id=1, source_target_pairs={{0,24},{1,25},{2,26},{3,27},{4,28},{5,29},{6,30},{7,31},{8,16},{9,... | collective-permute-start | bytes 393224 | tf_op jit(solution)/shard_map/ppermute | solution.py:291
  89.0 7.9 %collective-permute-start.29 = (f32[128,256]{1,0:T(8,128)S(1)}, f32[128,256]{1,0:T(8,128)S(1)}, u32[]{:S(2)}, u32[]{:S(2)}) collective-permute-start(f32[128,256]{1,0:T(8,128)S(1)} %slice_bitcast_fusion), channel_id=1, source_target_pairs={{0,8},{1,9},{2,10},{3,11},{4,12},{5,13},{6,14},{7,15},{8,0},{9,1},... | collective-permute-start | bytes 393224 | tf_op jit(solution)/shard_map/ppermute | solution.py:291

commit v3 on v2

--- a/solution.py
+++ b/solution.py
@@ -171,12 +171,17 @@
     )(pltpu.with_memory_space_constraint(factors.reshape(s, rows, w), pltpu.HBM))
 
 
-def task_kernel(stage, first, firsts, cuts, tab, *refs):
+def task_kernel(stage, first, keep, firsts, cuts, tab, *refs):
     f2, *refs = refs
     if not first:
         sums_in, *refs = refs
     stacks, refs = refs[: len(firsts)], refs[len(firsts) :]
-    outs, (sums, order, tiles, sem) = refs[: len(refs) - 4], refs[len(refs) - 4 :]
+    if keep:
+        sums, *refs = refs
+    outs, refs = refs[: len(cuts)], refs[len(cuts) :]
+    if not keep:
+        sums, *refs = refs
+    order, tiles, sem = refs
     w = f2.shape[2] // 2
     tasks = tab.shape[1]
     pairs = f2.shape[1] // (2 * w)
@@ -248,28 +253,25 @@
         several(done, 2)
 
     lax.fori_loop(count // 2 * 2, count, single, 0)
-    if cuts:
-        for start, out in zip(cuts, outs):
-            out[...] = sums[start : start + out.shape[0]]
-
-
-def run_stage(table, stage, f2, stacks, firsts, sums, shape, cuts=()):
+    for (start, size), out in zip(cuts, outs):
+        out[...] = sums[start : start + size]
+
+
+def run_stage(table, stage, f2, stacks, firsts, sums, shape, cuts, keep):
     tasks = table.shape[1]
     w = f2.shape[2] // 2
     first = sums is None
     vmem = pl.BlockSpec(memory_space=pltpu.VMEM)
-    ends = list(cuts[1:]) + [shape[0]]
-    shapes = [(end - start,) + shape[1:] for start, end in zip(cuts, ends)] if cuts else [shape]
+    shapes = ([shape] if keep else []) + [(size,) + shape[1:] for _, size in cuts]
     outs = [jax.ShapeDtypeStruct(s, jnp.float32) for s in shapes]
-    kept = [pltpu.VMEM(shape, jnp.float32)] if cuts else []
-    body = functools.partial(task_kernel, stage, first, tuple(firsts), tuple(cuts))
+    body = functools.partial(task_kernel, stage, first, keep, tuple(firsts), tuple(cuts))
     return pl.pallas_call(
         body,
         in_specs=[pl.BlockSpec(memory_space=pltpu.SMEM)] + [vmem] * (1 if first else 2)
         + [pl.BlockSpec(memory_space=pl.ANY)] * len(stacks),
         out_specs=[vmem] * len(outs),
         out_shape=outs,
-        scratch_shapes=kept + [
+        scratch_shapes=([] if keep else [pltpu.VMEM(shape, jnp.float32)]) + [
             pltpu.SMEM((tasks,), jnp.int32),
             pltpu.VMEM((tasks, w, w), jnp.float32),
             pltpu.SemaphoreType.DMA((tasks,)),
@@ -359,16 +361,14 @@
         straight = jnp.where(side == 0, 3 * depth, 0) + turn + (dz & 1)
         sideways = depth + turn * 2 + (side - 1) * 2 + (dz & 1)
         at = jnp.where((side == 1) | (side == 2), sideways, straight)
-        return dc * 4 * depth + at, part
+        return side == 3, dc * 4 * depth + at, part
 
     row_a, col_b = own(target_row), own(target_column)
-    rows = [
-        *source_of(own(density_source), own(density_column)),
-        slot_pairs[:, 0],
-        slot_pairs[:, 1],
-        *target_of(row_a, col_b),
-        *target_of(col_b, row_a),
-    ]
+    corner_a, *target_a = target_of(row_a, col_b)
+    corner_b, *target_b = target_of(col_b, row_a)
+    stage, *source = source_of(own(density_source), own(density_column))
+    stage = jnp.where((stage > 1) & ~(corner_a | corner_b), 4, stage)
+    rows = [stage, *source, slot_pairs[:, 0], slot_pairs[:, 1], *target_a, *target_b]
     which = lax.broadcasted_iota(jnp.int32, (len(rows), task_count), 0)
     table = sum(jnp.where(which == at, row[None, :], 0) for at, row in enumerate(rows))
 
@@ -389,29 +389,31 @@
                 by_stage[stage][0].append(stack)
                 by_stage[stage][1].append(at)
 
+    by_stage.append(tuple(one + other for one, other in zip(by_stage[2], by_stage[3])))
     shape = (8 * depth,) + density.shape
-    groups = [0, depth] + [depth + 4 * k for k in range(1, chunks)] + [3 * depth]
+    corner_cuts = [(at, depth) for at in (0, 4 * depth)]
+    groups = [(depth + 4 * k, 4) for k in range(chunks)] + [(3 * depth + 2 * k, 2) for k in range(chunks)]
+    cuts = groups + [(4 * depth + at, size) for at, size in groups]
     sums = None
     for stage, (values, firsts) in enumerate(by_stage):
-        cuts = groups + [4 * depth + at for at in groups] if stage == 3 else ()
-        results = run_stage(table, stage, split_factors, values, firsts, sums, shape, cuts)
+        cut = {3: corner_cuts, 4: cuts}.get(stage, ())
+        results = run_stage(table, stage, split_factors, values, firsts, sums, shape, cut, stage < 4)
         sums = results[0]
+        if stage == 3:
+            corner_mine, corner_other = results[1:]
     mine, others = results[: len(groups)], results[len(groups) :]
 
+    corner = corner_mine + move(corner_other, across_core)
     merged = [a + move(b, across_core) for a, b in zip(mine, others)]
-    column = merged[-1]
+    corners = [move(corner[2 * k : 2 * k + 2], across_diagonal) for k in range(chunks)]
     total = None
-    corners = []
-    for turn in range(chunks):
-        corners.append(move(merged[0][2 * turn : 2 * turn + 2], across_diagonal))
-    for turn in range(chunks):
-        sides = merged[1 + turn]
-        side_x = sides[:2] + jnp.where(on_first, corners[turn], 0.0)
-        side_y = sides[2:] + jnp.where(on_first, 0.0, corners[turn])
-        here = column[2 * turn : 2 * turn + 2]
+    for k in range(chunks):
+        sides, here = merged[k], merged[chunks + k]
+        side_x = sides[:2] + jnp.where(on_first, corners[k], 0.0)
+        side_y = sides[2:] + jnp.where(on_first, 0.0, corners[k])
         here = here + move(side_x, across_x) + move(side_y, across_y)
         for bit in range(2):
-            step = (chunks - 1 - turn) * 2 + bit
+            step = (chunks - 1 - k) * 2 + bit
             value = move(here[bit], across_z(step)) if step else here[bit]
             total = value if total is None else total + value
 

time: 98.6 us -> 96.7 us (0.981)
  waiting for transfers between devices: 31.1 us -> 20.2 us
  starting transfers between devices: 28.2 us -> 35.2 us
  Pallas kernels: 34.3 us -> 36.3 us
    ppermute x30 -> x31, waiting for transfers between devices: 31.1 us -> 20.2 us  [shift(): return lax.ppermute(value, AXES, pairs)]
    ppermute x30 -> x31, starting transfers between devices: 28.2 us -> 35.2 us  [shift(): return lax.ppermute(value, AXES, pairs)]
    pallas_call x4 -> x5, Pallas kernels: 31.2 us -> 33.3 us  [run_stage(): pl.pallas_call(body, in_specs=[pl.BlockSpec(memory_space=pltpu.SMEM)] + [...]
    add x4 -> x3, other arithmetic: 1.65 us -> 0.18 us  [the longest x2 0.11 us: gathered(): side_x = sides[:2] + jnp.where(on_first, corners[k], 0.0)]
  transfers between devices with their start and end apart: 30 -> 31, of which waited for: 14 -> 12; matrix products, arithmetic and copies ran while one was open for 3% -> 3% of each run, Pallas kernels for 30% -> 34%
where the time goes in v3:
time: 96.7 us; the launch traced here: 96.6 us
  Pallas kernels  36.3 us (38%)
  starting transfers between devices  35.2 us (36%)
  waiting for transfers between devices  20.2 us (21%)
  other arithmetic  2.27 us (2%)
  local copies, waits for them, and re-layouts  1.59 us (2%)
    ppermute x31, starting transfers between devices, shift(): return lax.ppermute(value, AXES, pairs)  35.2 us
    pallas_call x5, Pallas kernels, run_stage(): pl.pallas_call(body, in_specs=[pl.BlockSpec(memory_space=pltpu.SMEM)] + [...  33.3 us
    ppermute x31, waiting for transfers between devices, shift(): return lax.ppermute(value, AXES, pairs)  20.2 us
    pallas_call x1, Pallas kernels, prep(): pl.pallas_call(prep_kernel, in_specs=[pl.BlockSpec(memory_space=pltpu.HBM...  3.07 us
  transfers between devices with their start and end apart: 31, of which 12 were waited for; matrix products, arithmetic and copies ran while one was open for 3% of the time, Pallas kernels for 34%

profile of v3, /device:TPU:0, one launch (start us, length us, event | category | flops | bytes accessed | tf_op | source)
XLA Modules:
  0.0 96.6 jit_solution(14610147632887185111)
XLA Ops:
  0.0 3.1 %collective-permute-start = (f32[128,256]{1,0:T(8,128)}, f32[128,256]{1,0:T(8,128)S(1)}, u32[]{:S(2)}, u32[]{:S(2)}) collective-permute-start(f32[128,256]{1,0:T(8,128)} %param.8), channel_id=1, source_target_pairs={{0,8},{1,9},{2,10},{3,11},{4,12},{5,13},{6,14},{7,15},{8,0},{9,1},... | collective-permute-start | bytes 393224 | tf_op jit(solution)/shard_map/ppermute | solution.py:293
  3.1 2.6 %collective-permute-start.6 = (f32[128,256]{1,0:T(8,128)}, f32[128,256]{1,0:T(8,128)S(1)}, u32[]{:S(2)}, u32[]{:S(2)}) collective-permute-start(f32[128,256]{1,0:T(8,128)} %param.8), channel_id=1, source_target_pairs={{0,16},{1,17},{2,18},{3,19},{4,20},{5,21},{6,22},{7,23},{8,24},{9,... | collective-permute-start | bytes 393224 | tf_op jit(solution)/shard_map/ppermute | solution.py:293
  5.6 0.0 collective-permute-start.7
  5.7 0.8 slice_bitcast_fusion.5
  6.4 0.8 and_select_fusion.3
  7.2 0.7 and_select_fusion.2
  8.0 0.0 copy-start.1
  8.0 3.1 %shard_map.82.refs_0_ = bf16[6,2048,256]{2,1,0:T(8,128)(2,1)S(1)} custom-call(f32[6,2048,128]{2,1,0:T(8,128)} %bitcast.75), custom_call_target="tpu_custom_call" | custom-call | flops 3145728 | bytes 12582912 | tf_op jit(solution)/shard_map/pallas_call | solution.py:163
  11.1 0.0 collective-permute-done
  11.2 1.8 %collective-permute-start.2 = (f32[2,128,256]{2,1,0:T(8,128)S(1)}, f32[2,128,256]{2,1,0:T(8,128)S(1)}, u32[]{:S(2)}, u32[]{:S(2)}) collective-permute-start(f32[2,128,256]{2,1,0:T(8,128)S(1)} %pad_maximum_fusion.refs_1_), channel_id=1, source_target_pairs={{0,4},{1,5},{2,6},{3,7},{4,0},{5,1},{6,2},{7,3},{8,12},{9,13},{10,... | collective-permute-start | bytes 786440 | tf_op jit(solution)/shard_map/ppermute | solution.py:293
  12.9 1.5 %collective-permute-start.4 = (f32[2,128,256]{2,1,0:T(8,128)S(1)}, f32[2,128,256]{2,1,0:T(8,128)S(1)}, u32[]{:S(2)}, u32[]{:S(2)}) collective-permute-start(f32[2,128,256]{2,1,0:T(8,128)S(1)} %pad_maximum_fusion.refs_1_), channel_id=1, source_target_pairs={{0,2},{1,3},{2,0},{3,1},{4,6},{5,7},{6,4},{7,5},{8,10},{9,11},{10,... | collective-permute-start | bytes 786440 | tf_op jit(solution)/shard_map/ppermute | solution.py:293
  14.5 1.7 %collective-permute-done.6 = f32[128,256]{1,0:T(8,128)S(1)} collective-permute-done((f32[128,256]{1,0:T(8,128)}, f32[128,256]{1,0:T(8,128)S(1)}, u32[]{:S(2)}, u32[]{:S(2)}) %collective-permute-start.6) | collective-permute-done | bytes 131104 | tf_op jit(solution)/shard_map/ppermute | solution.py:293
  16.2 0.0 collective-permute-done.7
  16.2 1.6 %collective-permute-start.11 = (f32[2,128,256]{2,1,0:T(8,128)S(1)}, f32[2,128,256]{2,1,0:T(8,128)S(1)}, u32[]{:S(2)}, u32[]{:S(2)}) collective-permute-start(f32[2,128,256]{2,1,0:T(8,128)S(1)} %pad_maximum_fusion.1.refs_6_), channel_id=1, source_target_pairs={{0,4},{1,5},{2,6},{3,7},{4,0},{5,1},{6,2},{7,3},{8,12},{9,13},{10,... | collective-permute-start | bytes 786440 | tf_op jit(solution)/shard_map/ppermute | solution.py:293
  17.7 1.5 %collective-permute-start.13 = (f32[2,128,256]{2,1,0:T(8,128)S(1)}, f32[2,128,256]{2,1,0:T(8,128)S(1)}, u32[]{:S(2)}, u32[]{:S(2)}) collective-permute-start(f32[2,128,256]{2,1,0:T(8,128)S(1)} %pad_maximum_fusion.1.refs_6_), channel_id=1, source_target_pairs={{0,2},{1,3},{2,0},{3,1},{4,6},{5,7},{6,4},{7,5},{8,10},{9,11},{10,... | collective-permute-start | bytes 786440 | tf_op jit(solution)/shard_map/ppermute | solution.py:293
  19.3 0.1 select_add_fusion.tab
  19.3 0.1 collective-permute-start.1
  19.4 1.0 %collective-permute-done.2.refs_2_ = f32[2,128,256]{2,1,0:T(8,128)S(1)} collective-permute-done((f32[2,128,256]{2,1,0:T(8,128)S(1)}, f32[2,128,256]{2,1,0:T(8,128)S(1)}, u32[]{:S(2)}, u32[]{:S(2)}) %collective-permute-start.2) | collective-permute-done | bytes 262176 | tf_op jit(solution)/shard_map/ppermute | solution.py:293
  20.4 0.0 collective-permute-start.8
  20.4 1.7 %collective-permute-done.4.refs_4_ = f32[2,128,256]{2,1,0:T(8,128)S(1)} collective-permute-done((f32[2,128,256]{2,1,0:T(8,128)S(1)}, f32[2,128,256]{2,1,0:T(8,128)S(1)}, u32[]{:S(2)}, u32[]{:S(2)}) %collective-permute-start.4) | collective-permute-done | bytes 262176 | tf_op jit(solution)/shard_map/ppermute | solution.py:293
  22.2 1.6 %collective-permute-start.9 = (f32[2,128,256]{2,1,0:T(8,128)S(1)}, f32[2,128,256]{2,1,0:T(8,128)S(1)}, u32[]{:S(2)}, u32[]{:S(2)}) collective-permute-start(f32[2,128,256]{2,1,0:T(8,128)S(1)} %broadcast_select_fusion.1), channel_id=1, source_target_pairs={{0,2},{1,5},{2,0},{3,7},{4,6},{5,1},{6,4},{7,3},{8,10},{9,13},{10,... | collective-permute-start | bytes 786440 | tf_op jit(solution)/shard_map/ppermute | solution.py:293
  23.7 1.3 %collective-permute-done.11.refs_4_ = f32[2,128,256]{2,1,0:T(8,128)S(1)} collective-permute-done((f32[2,128,256]{2,1,0:T(8,128)S(1)}, f32[2,128,256]{2,1,0:T(8,128)S(1)}, u32[]{:S(2)}, u32[]{:S(2)}) %collective-permute-start.11) | collective-permute-done | bytes 262176 | tf_op jit(solution)/shard_map/ppermute | solution.py:293
  25.0 0.5 collective-permute-done.13.refs_6_
  25.6 1.6 %collective-permute-start.15 = (f32[2,128,256]{2,1,0:T(8,128)S(1)}, f32[2,128,256]{2,1,0:T(8,128)S(1)}, u32[]{:S(2)}, u32[]{:S(2)}) collective-permute-start(f32[2,128,256]{2,1,0:T(8,128)S(1)} %broadcast_select_fusion), channel_id=1, source_target_pairs={{0,2},{1,5},{2,0},{3,7},{4,6},{5,1},{6,4},{7,3},{8,10},{9,13},{10,... | collective-permute-start | bytes 786440 | tf_op jit(solution)/shard_map/ppermute | solution.py:293
  27.2 0.0 collective-permute-start.3
  27.2 0.5 collective-permute-start.5
  27.7 4.4 %shard_map.83.refs_1_ = f32[32,128,256]{2,1,0:T(8,128)S(1)} custom-call(s32[9,32]{1,0:T(8,128)S(1)} %select_add_fusion.tab, bf16[6,2048,256]{2,1,0:T(8,128)(2,1)S(1)} %shard_map.82.refs_0_, f32[2,128,256]{2,1,0:T(8,128)S(1)} %pad_maximum_fusion.refs_1_, f32[2,128,256]{2,1,0:T(8,128)S(1)} %collective-permute-done.1.refs_2_), custom_call_target="tpu_custom_call" | custom-call | flops 4294967296 | bytes 6291456 | tf_op jit(solution)/shard_map/pallas_call | solution.py:268
  32.2 1.7 %collective-permute-start.12 = (f32[2,128,256]{2,1,0:T(8,128)S(1)}, f32[2,128,256]{2,1,0:T(8,128)S(1)}, u32[]{:S(2)}, u32[]{:S(2)}) collective-permute-start(f32[2,128,256]{2,1,0:T(8,128)S(1)} %collective-permute-done.11.refs_4_), channel_id=1, source_target_pairs={{0,1},{1,0},{2,3},{3,2},{4,5},{5,4},{6,7},{7,6},{8,9},{9,8},{10,11... | collective-permute-start | bytes 786440 | tf_op jit(solution)/shard_map/ppermute | solution.py:293
  33.8 0.1 collective-permute-start.14
  33.9 0.4 collective-permute-start.10
  34.3 0.1 collective-permute-start.16
  34.4 11.9 %shard_map.84.refs_1_ = f32[32,128,256]{2,1,0:T(8,128)S(1)} custom-call(s32[9,32]{1,0:T(8,128)S(1)} %select_add_fusion.tab, bf16[6,2048,256]{2,1,0:T(8,128)(2,1)S(1)} %shard_map.82.refs_0_, f32[32,128,256]{2,1,0:T(8,128)S(1)} %shard_map.83.refs_1_, f32[2,128,256]{2,1,0:T(8,128)S(1)} %collective-permute-done.2.refs_2_, ...), custom_call_target="tpu_custom_call" | custom-call | flops 4294967296 | bytes 6291456 | tf_op jit(solution)/shard_map/pallas_call | solution.py:268
  46.4 5.8 %shard_map.85.refs_1_ = f32[32,128,256]{2,1,0:T(8,128)S(1)} custom-call(s32[9,32]{1,0:T(8,128)S(1)} %select_add_fusion.tab, bf16[6,2048,256]{2,1,0:T(8,128)(2,1)S(1)} %shard_map.82.refs_0_, f32[32,128,256]{2,1,0:T(8,128)S(1)} %shard_map.84.refs_1_, f32[2,128,256]{2,1,0:T(8,128)S(1)} %collective-permute-done.9.refs_2_, ...), custom_call_target="tpu_custom_call" | custom-call | flops 4294967296 | bytes 6291456 | tf_op jit(solution)/shard_map/pallas_call | solution.py:268
  52.2 3.4 %shard_map.86 = (f32[32,128,256]{2,1,0:T(8,128)S(1)}, f32[4,128,256]{2,1,0:T(8,128)S(1)}, f32[4,128,256]{2,1,0:T(8,128)S(1)}) custom-call(s32[9,32]{1,0:T(8,128)S(1)} %select_add_fusion.tab, bf16[6,2048,256]{2,1,0:T(8,128)(2,1)S(1)} %shard_map.82.refs_0_, f32[32,128,256]{2,1,0:T(8,128)S(1)} %shard_map.85.refs_1_, ...), custom_call_target="tpu_custom_call" | custom-call | flops 4294967296 | bytes 6291456 | tf_op jit(solution)/shard_map/pallas_call | solution.py:268
  55.5 0.8 collective-permute-start.19
  56.4 7.8 %shard_map.87 = (f32[4,128,256]{2,1,0:T(8,128)S(1)}, f32[4,128,256]{2,1,0:T(8,128)S(1)}, f32[2,128,256]{2,1,0:T(8,128)S(1)}, f32[2,128,256]{2,1,0:T(8,128)S(1)},...) custom-call(s32[9,32]{1,0:T(8,128)S(1)} %select_add_fusion.tab, ...), custom_call_target="tpu_custom_call" | custom-call | flops 4294967296 | bytes 6291456 | tf_op jit(solution)/shard_map/pallas_call | solution.py:268
  64.2 0.1 collective-permute-start.18
  64.2 0.5 collective-permute-start.26
  64.7 0.1 add.333
  64.9 0.8 collective-permute-start.20
  65.7 1.6 %collective-permute-start.27 = (f32[2,128,256]{2,1,0:T(8,128)S(1)}, f32[2,128,256]{2,1,0:T(8,128)S(1)}, u32[]{:S(2)}, u32[]{:S(2)}) collective-permute-start(f32[2,128,256]{2,1,0:T(8,128)S(1)} %get-tuple-element.46), channel_id=1, source_target_pairs={{0,2},{1,5},{2,0},{3,7},{4,6},{5,1},{6,4},{7,3},{8,10},{9,13},{10,... | collective-permute-start | bytes 786440 | tf_op jit(solution)/shard_map/ppermute | solution.py:293
  67.3 0.1 add.332
  67.4 3.9 %collective-permute-done.20 = f32[2,128,256]{2,1,0:T(8,128)S(1)} collective-permute-done((f32[2,128,256]{2,1,0:T(8,128)S(1)}, f32[2,128,256]{2,1,0:T(8,128)S(1)}, u32[]{:S(2)}, u32[]{:S(2)}) %collective-permute-start.20) | collective-permute-done | bytes 262176 | tf_op jit(solution)/shard_map/ppermute | solution.py:293
  71.3 0.1 slice_add_fusion.3
  71.4 0.6 collective-permute-start.21
  71.9 2.0 %collective-permute-start.22 = (f32[2,128,256]{2,1,0:T(8,128)S(1)}, f32[2,128,256]{2,1,0:T(8,128)S(1)}, u32[]{:S(2)}, u32[]{:S(2)}) collective-permute-start(f32[2,128,256]{2,1,0:T(8,128)S(1)} %get-tuple-element.42), channel_id=1, source_target_pairs={{0,2},{1,3},{2,0},{3,1},{4,6},{5,7},{6,4},{7,5},{8,10},{9,11},{10,... | collective-permute-start | bytes 786440 | tf_op jit(solution)/shard_map/ppermute | solution.py:293
  74.0 0.1 add.340
  74.0 0.4 collective-permute-done.27
  74.5 0.1 slice_add_fusion.1
  74.5 0.3 collective-permute-start.28
  74.8 2.5 %collective-permute-start.29 = (f32[2,128,256]{2,1,0:T(8,128)S(1)}, f32[2,128,256]{2,1,0:T(8,128)S(1)}, u32[]{:S(2)}, u32[]{:S(2)}) collective-permute-start(f32[2,128,256]{2,1,0:T(8,128)S(1)} %get-tuple-element.44), channel_id=1, source_target_pairs={{0,2},{1,3},{2,0},{3,1},{4,6},{5,7},{6,4},{7,5},{8,10},{9,11},{10,... | collective-permute-start | bytes 786440 | tf_op jit(solution)/shard_map/ppermute | solution.py:293
  77.3 3.1 %collective-permute-done.21 = f32[2,128,256]{2,1,0:T(8,128)S(1)} collective-permute-done((f32[2,128,256]{2,1,0:T(8,128)S(1)}, f32[2,128,256]{2,1,0:T(8,128)S(1)}, u32[]{:S(2)}, u32[]{:S(2)}) %collective-permute-start.21) | collective-permute-done | bytes 262176 | tf_op jit(solution)/shard_map/ppermute | solution.py:293
  80.4 0.7 collective-permute-done.22
  81.1 0.1 add_add_fusion.1
  81.2 5.3 %collective-permute-start.23 = (f32[128,256]{1,0:T(8,128)S(1)}, f32[128,256]{1,0:T(8,128)S(1)}, u32[]{:S(2)}, u32[]{:S(2)}) collective-permute-start(f32[128,256]{1,0:T(8,128)S(1)} %get-tuple-element.48), channel_id=1, source_target_pairs={{0,16},{1,17},{2,18},{3,19},{4,20},{5,21},{6,22},{7,23},{8,24},{9,... | collective-permute-start | bytes 393224 | tf_op jit(solution)/shard_map/ppermute | solution.py:293
  86.5 1.5 %collective-permute-start.24 = (f32[128,256]{1,0:T(8,128)S(1)}, f32[128,256]{1,0:T(8,128)S(1)}, u32[]{:S(2)}, u32[]{:S(2)}) collective-permute-start(f32[128,256]{1,0:T(8,128)S(1)} %get-tuple-element.47), channel_id=1, source_target_pairs={{0,24},{1,25},{2,26},{3,27},{4,28},{5,29},{6,30},{7,31},{8,16},{9,... | collective-permute-start | bytes 393224 | tf_op jit(solution)/shard_map/ppermute | solution.py:293
  88.0 0.1 add_add_fusion
  88.1 1.1 %collective-permute-start.30 = (f32[128,256]{1,0:T(8,128)S(1)}, f32[128,256]{1,0:T(8,128)S(1)}, u32[]{:S(2)}, u32[]{:S(2)}) collective-permute-start(f32[128,256]{1,0:T(8,128)S(1)} %slice_bitcast_fusion), channel_id=1, source_target_pairs={{0,8},{1,9},{2,10},{3,11},{4,12},{5,13},{6,14},{7,15},{8,0},{9,1},... | collective-permute-start | bytes 393224 | tf_op jit(solution)/shard_map/ppermute | solution.py:293
  89.2 4.3 %collective-permute-done.23 = f32[128,256]{1,0:T(8,128)S(1)} collective-permute-done((f32[128,256]{1,0:T(8,128)S(1)}, f32[128,256]{1,0:T(8,128)S(1)}, u32[]{:S(2)}, u32[]{:S(2)}) %collective-permute-start.23) | collective-permute-done | bytes 131104 | tf_op jit(solution)/shard_map/ppermute | solution.py:293
  93.5 0.7 collective-permute-done.24
  94.2 0.9 collective-permute-done.30
  95.1 0.3 fusion
  95.4 0.4 fusion.6
  95.8 0.8 copy.11
  (35 shorter events, 0.3 us)
Async XLA Ops:
  0.0 95.1 %copy-start = (f32[1024,128]{1,0:T(8,128)S(1)}, f32[1024,128]{1,0:T(8,128)}, u32[]{:S(2)}) copy-start(f32[1024,128]{1,0:T(8,128)} %param.10) | copy-start | bytes 1572868
  0.0 11.1 %collective-permute-start = (f32[128,256]{1,0:T(8,128)}, f32[128,256]{1,0:T(8,128)S(1)}, u32[]{:S(2)}, u32[]{:S(2)}) collective-permute-start(f32[128,256]{1,0:T(8,128)} %param.8), channel_id=1, source_target_pairs={{0,8},{1,9},{2,10},{3,11},{4,12},{5,13},{6,14},{7,15},{8,0},{9,1},... | collective-permute-start | bytes 393224 | tf_op jit(solution)/shard_map/ppermute | solution.py:293
  3.1 13.1 %collective-permute-start.6 = (f32[128,256]{1,0:T(8,128)}, f32[128,256]{1,0:T(8,128)S(1)}, u32[]{:S(2)}, u32[]{:S(2)}) collective-permute-start(f32[128,256]{1,0:T(8,128)} %param.8), channel_id=1, source_target_pairs={{0,16},{1,17},{2,18},{3,19},{4,20},{5,21},{6,22},{7,23},{8,24},{9,... | collective-permute-start | bytes 393224 | tf_op jit(solution)/shard_map/ppermute | solution.py:293
  5.6 10.5 %collective-permute-start.7 = (f32[128,256]{1,0:T(8,128)}, f32[128,256]{1,0:T(8,128)S(1)}, u32[]{:S(2)}, u32[]{:S(2)}) collective-permute-start(f32[128,256]{1,0:T(8,128)} %param.8), channel_id=1, source_target_pairs={{0,24},{1,25},{2,26},{3,27},{4,28},{5,29},{6,30},{7,31},{8,16},{9,... | collective-permute-start | bytes 393224 | tf_op jit(solution)/shard_map/ppermute | solution.py:293
  8.0 3.1 %copy-start.1 = (f32[128,256]{1,0:T(8,128)S(1)}, f32[128,256]{1,0:T(8,128)}, u32[]{:S(2)}) copy-start(f32[128,256]{1,0:T(8,128)} %param.8) | copy-start | bytes 393220
  11.2 9.2 %collective-permute-start.2 = (f32[2,128,256]{2,1,0:T(8,128)S(1)}, f32[2,128,256]{2,1,0:T(8,128)S(1)}, u32[]{:S(2)}, u32[]{:S(2)}) collective-permute-start(f32[2,128,256]{2,1,0:T(8,128)S(1)} %pad_maximum_fusion.refs_1_), channel_id=1, source_target_pairs={{0,4},{1,5},{2,6},{3,7},{4,0},{5,1},{6,2},{7,3},{8,12},{9,13},{10,... | collective-permute-start | bytes 786440 | tf_op jit(solution)/shard_map/ppermute | solution.py:293
  12.9 9.2 %collective-permute-start.4 = (f32[2,128,256]{2,1,0:T(8,128)S(1)}, f32[2,128,256]{2,1,0:T(8,128)S(1)}, u32[]{:S(2)}, u32[]{:S(2)}) collective-permute-start(f32[2,128,256]{2,1,0:T(8,128)S(1)} %pad_maximum_fusion.refs_1_), channel_id=1, source_target_pairs={{0,2},{1,3},{2,0},{3,1},{4,6},{5,7},{6,4},{7,5},{8,10},{9,11},{10,... | collective-permute-start | bytes 786440 | tf_op jit(solution)/shard_map/ppermute | solution.py:293
  16.2 8.9 %collective-permute-start.11 = (f32[2,128,256]{2,1,0:T(8,128)S(1)}, f32[2,128,256]{2,1,0:T(8,128)S(1)}, u32[]{:S(2)}, u32[]{:S(2)}) collective-permute-start(f32[2,128,256]{2,1,0:T(8,128)S(1)} %pad_maximum_fusion.1.refs_6_), channel_id=1, source_target_pairs={{0,4},{1,5},{2,6},{3,7},{4,0},{5,1},{6,2},{7,3},{8,12},{9,13},{10,... | collective-permute-start | bytes 786440 | tf_op jit(solution)/shard_map/ppermute | solution.py:293
  17.7 7.8 %collective-permute-start.13 = (f32[2,128,256]{2,1,0:T(8,128)S(1)}, f32[2,128,256]{2,1,0:T(8,128)S(1)}, u32[]{:S(2)}, u32[]{:S(2)}) collective-permute-start(f32[2,128,256]{2,1,0:T(8,128)S(1)} %pad_maximum_fusion.1.refs_6_), channel_id=1, source_target_pairs={{0,2},{1,3},{2,0},{3,1},{4,6},{5,7},{6,4},{7,5},{8,10},{9,11},{10,... | collective-permute-start | bytes 786440 | tf_op jit(solution)/shard_map/ppermute | solution.py:293
  19.3 7.8 %collective-permute-start.1 = (f32[2,128,256]{2,1,0:T(8,128)S(1)}, f32[2,128,256]{2,1,0:T(8,128)S(1)}, u32[]{:S(2)}, u32[]{:S(2)}) collective-permute-start(f32[2,128,256]{2,1,0:T(8,128)S(1)} %pad_maximum_fusion.refs_1_), channel_id=1, source_target_pairs={{0,1},{1,0},{2,3},{3,2},{4,5},{5,4},{6,7},{7,6},{8,9},{9,8},{10,11... | collective-permute-start | bytes 786440 | tf_op jit(solution)/shard_map/ppermute | solution.py:293
  20.4 11.7 %collective-permute-start.8 = (f32[2,128,256]{2,1,0:T(8,128)S(1)}, f32[2,128,256]{2,1,0:T(8,128)S(1)}, u32[]{:S(2)}, u32[]{:S(2)}) collective-permute-start(f32[2,128,256]{2,1,0:T(8,128)S(1)} %pad_maximum_fusion.1.refs_6_), channel_id=1, source_target_pairs={{0,1},{1,0},{2,3},{3,2},{4,5},{5,4},{6,7},{7,6},{8,9},{9,8},{10,11... | collective-permute-start | bytes 786440 | tf_op jit(solution)/shard_map/ppermute | solution.py:293
  22.2 11.8 %collective-permute-start.9 = (f32[2,128,256]{2,1,0:T(8,128)S(1)}, f32[2,128,256]{2,1,0:T(8,128)S(1)}, u32[]{:S(2)}, u32[]{:S(2)}) collective-permute-start(f32[2,128,256]{2,1,0:T(8,128)S(1)} %broadcast_select_fusion.1), channel_id=1, source_target_pairs={{0,2},{1,5},{2,0},{3,7},{4,6},{5,1},{6,4},{7,3},{8,10},{9,13},{10,... | collective-permute-start | bytes 786440 | tf_op jit(solution)/shard_map/ppermute | solution.py:293
  25.6 8.8 %collective-permute-start.15 = (f32[2,128,256]{2,1,0:T(8,128)S(1)}, f32[2,128,256]{2,1,0:T(8,128)S(1)}, u32[]{:S(2)}, u32[]{:S(2)}) collective-permute-start(f32[2,128,256]{2,1,0:T(8,128)S(1)} %broadcast_select_fusion), channel_id=1, source_target_pairs={{0,2},{1,5},{2,0},{3,7},{4,6},{5,1},{6,4},{7,3},{8,10},{9,13},{10,... | collective-permute-start | bytes 786440 | tf_op jit(solution)/shard_map/ppermute | solution.py:293
  27.2 6.6 %collective-permute-start.3 = (f32[2,128,256]{2,1,0:T(8,128)S(1)}, f32[2,128,256]{2,1,0:T(8,128)S(1)}, u32[]{:S(2)}, u32[]{:S(2)}) collective-permute-start(f32[2,128,256]{2,1,0:T(8,128)S(1)} %collective-permute-done.2.refs_2_), channel_id=1, source_target_pairs={{0,1},{1,0},{2,3},{3,2},{4,5},{5,4},{6,7},{7,6},{8,9},{9,8},{10,11... | collective-permute-start | bytes 786440 | tf_op jit(solution)/shard_map/ppermute | solution.py:293
  27.2 7.2 %collective-permute-start.5 = (f32[2,128,256]{2,1,0:T(8,128)S(1)}, f32[2,128,256]{2,1,0:T(8,128)S(1)}, u32[]{:S(2)}, u32[]{:S(2)}) collective-permute-start(f32[2,128,256]{2,1,0:T(8,128)S(1)} %collective-permute-done.4.refs_4_), channel_id=1, source_target_pairs={{0,1},{1,0},{2,3},{3,2},{4,5},{5,4},{6,7},{7,6},{8,9},{9,8},{10,11... | collective-permute-start | bytes 786440 | tf_op jit(solution)/shard_map/ppermute | solution.py:293
  32.2 14.2 %collective-permute-start.12 = (f32[2,128,256]{2,1,0:T(8,128)S(1)}, f32[2,128,256]{2,1,0:T(8,128)S(1)}, u32[]{:S(2)}, u32[]{:S(2)}) collective-permute-start(f32[2,128,256]{2,1,0:T(8,128)S(1)} %collective-permute-done.11.refs_4_), channel_id=1, source_target_pairs={{0,1},{1,0},{2,3},{3,2},{4,5},{5,4},{6,7},{7,6},{8,9},{9,8},{10,11... | collective-permute-start | bytes 786440 | tf_op jit(solution)/shard_map/ppermute | solution.py:293
  33.8 12.6 %collective-permute-start.14 = (f32[2,128,256]{2,1,0:T(8,128)S(1)}, f32[2,128,256]{2,1,0:T(8,128)S(1)}, u32[]{:S(2)}, u32[]{:S(2)}) collective-permute-start(f32[2,128,256]{2,1,0:T(8,128)S(1)} %collective-permute-done.13.refs_6_), channel_id=1, source_target_pairs={{0,1},{1,0},{2,3},{3,2},{4,5},{5,4},{6,7},{7,6},{8,9},{9,8},{10,11... | collective-permute-start | bytes 786440 | tf_op jit(solution)/shard_map/ppermute | solution.py:293
  33.9 12.5 %collective-permute-start.10 = (f32[2,128,256]{2,1,0:T(8,128)S(1)}, f32[2,128,256]{2,1,0:T(8,128)S(1)}, u32[]{:S(2)}, u32[]{:S(2)}) collective-permute-start(f32[2,128,256]{2,1,0:T(8,128)S(1)} %collective-permute-done.9.refs_2_), channel_id=1, source_target_pairs={{0,1},{1,0},{2,3},{3,2},{4,5},{5,4},{6,7},{7,6},{8,9},{9,8},{10,11... | collective-permute-start | bytes 786440 | tf_op jit(solution)/shard_map/ppermute | solution.py:293
  34.3 17.8 %collective-permute-start.16 = (f32[2,128,256]{2,1,0:T(8,128)S(1)}, f32[2,128,256]{2,1,0:T(8,128)S(1)}, u32[]{:S(2)}, u32[]{:S(2)}) collective-permute-start(f32[2,128,256]{2,1,0:T(8,128)S(1)} %collective-permute-done.15.refs_2_.refs_8_), channel_id=1, source_target_pairs={{0,1},{1,0},{2,3},{3,2},{4,5},{5,4},{6,7},{7,6},{8,9},{9,8},{10,11... | collective-permute-start | bytes 786440 | tf_op jit(solution)/shard_map/ppermute | solution.py:293
  55.5 9.2 %collective-permute-start.19 = (f32[4,128,256]{2,1,0:T(8,128)S(1)}, f32[4,128,256]{2,1,0:T(8,128)S(1)}, u32[]{:S(2)}, u32[]{:S(2)}) collective-permute-start(f32[4,128,256]{2,1,0:T(8,128)S(1)} %get-tuple-element.28), channel_id=1, source_target_pairs={{0,1},{1,0},{2,3},{3,2},{4,5},{5,4},{6,7},{7,6},{8,9},{9,8},{10,11... | collective-permute-start | bytes 1572872 | tf_op jit(solution)/shard_map/ppermute | solution.py:293
  64.2 3.1 %collective-permute-start.18 = (f32[4,128,256]{2,1,0:T(8,128)S(1)}, f32[4,128,256]{2,1,0:T(8,128)S(1)}, u32[]{:S(2)}, u32[]{:S(2)}) collective-permute-start(f32[4,128,256]{2,1,0:T(8,128)S(1)} %get-tuple-element.26), channel_id=1, source_target_pairs={{0,1},{1,0},{2,3},{3,2},{4,5},{5,4},{6,7},{7,6},{8,9},{9,8},{10,11... | collective-permute-start | bytes 1572872 | tf_op jit(solution)/shard_map/ppermute | solution.py:293
  64.2 9.7 %collective-permute-start.26 = (f32[4,128,256]{2,1,0:T(8,128)S(1)}, f32[4,128,256]{2,1,0:T(8,128)S(1)}, u32[]{:S(2)}, u32[]{:S(2)}) collective-permute-start(f32[4,128,256]{2,1,0:T(8,128)S(1)} %get-tuple-element.32), channel_id=1, source_target_pairs={{0,1},{1,0},{2,3},{3,2},{4,5},{5,4},{6,7},{7,6},{8,9},{9,8},{10,11... | collective-permute-start | bytes 1572872 | tf_op jit(solution)/shard_map/ppermute | solution.py:293
  64.9 6.4 %collective-permute-start.20 = (f32[2,128,256]{2,1,0:T(8,128)S(1)}, f32[2,128,256]{2,1,0:T(8,128)S(1)}, u32[]{:S(2)}, u32[]{:S(2)}) collective-permute-start(f32[2,128,256]{2,1,0:T(8,128)S(1)} %get-tuple-element.45), channel_id=1, source_target_pairs={{0,2},{1,5},{2,0},{3,7},{4,6},{5,1},{6,4},{7,3},{8,10},{9,13},{10,... | collective-permute-start | bytes 786440 | tf_op jit(solution)/shard_map/ppermute | solution.py:293
  65.7 9.1 %collective-permute-start.17 = (f32[2,128,256]{2,1,0:T(8,128)S(1)}, f32[2,128,256]{2,1,0:T(8,128)S(1)}, u32[]{:S(2)}, u32[]{:S(2)}) collective-permute-start(f32[2,128,256]{2,1,0:T(8,128)S(1)} %get-tuple-element.24), channel_id=1, source_target_pairs={{0,1},{1,0},{2,3},{3,2},{4,5},{5,4},{6,7},{7,6},{8,9},{9,8},{10,11... | collective-permute-start | bytes 786440 | tf_op jit(solution)/shard_map/ppermute | solution.py:293
  65.7 8.8 %collective-permute-start.27 = (f32[2,128,256]{2,1,0:T(8,128)S(1)}, f32[2,128,256]{2,1,0:T(8,128)S(1)}, u32[]{:S(2)}, u32[]{:S(2)}) collective-permute-start(f32[2,128,256]{2,1,0:T(8,128)S(1)} %get-tuple-element.46), channel_id=1, source_target_pairs={{0,2},{1,5},{2,0},{3,7},{4,6},{5,1},{6,4},{7,3},{8,10},{9,13},{10,... | collective-permute-start | bytes 786440 | tf_op jit(solution)/shard_map/ppermute | solution.py:293
  71.4 9.1 %collective-permute-start.21 = (f32[2,128,256]{2,1,0:T(8,128)S(1)}, f32[2,128,256]{2,1,0:T(8,128)S(1)}, u32[]{:S(2)}, u32[]{:S(2)}) collective-permute-start(f32[2,128,256]{2,1,0:T(8,128)S(1)} %get-tuple-element.41), channel_id=1, source_target_pairs={{0,4},{1,5},{2,6},{3,7},{4,0},{5,1},{6,2},{7,3},{8,12},{9,13},{10,... | collective-permute-start | bytes 786440 | tf_op jit(solution)/shard_map/ppermute | solution.py:293
  71.9 9.2 %collective-permute-start.22 = (f32[2,128,256]{2,1,0:T(8,128)S(1)}, f32[2,128,256]{2,1,0:T(8,128)S(1)}, u32[]{:S(2)}, u32[]{:S(2)}) collective-permute-start(f32[2,128,256]{2,1,0:T(8,128)S(1)} %get-tuple-element.42), channel_id=1, source_target_pairs={{0,2},{1,3},{2,0},{3,1},{4,6},{5,7},{6,4},{7,5},{8,10},{9,11},{10,... | collective-permute-start | bytes 786440 | tf_op jit(solution)/shard_map/ppermute | solution.py:293
  74.0 14.1 %collective-permute-start.25 = (f32[2,128,256]{2,1,0:T(8,128)S(1)}, f32[2,128,256]{2,1,0:T(8,128)S(1)}, u32[]{:S(2)}, u32[]{:S(2)}) collective-permute-start(f32[2,128,256]{2,1,0:T(8,128)S(1)} %get-tuple-element.30), channel_id=1, source_target_pairs={{0,1},{1,0},{2,3},{3,2},{4,5},{5,4},{6,7},{7,6},{8,9},{9,8},{10,11... | collective-permute-start | bytes 786440 | tf_op jit(solution)/shard_map/ppermute | solution.py:293
  74.5 13.5 %collective-permute-start.28 = (f32[2,128,256]{2,1,0:T(8,128)S(1)}, f32[2,128,256]{2,1,0:T(8,128)S(1)}, u32[]{:S(2)}, u32[]{:S(2)}) collective-permute-start(f32[2,128,256]{2,1,0:T(8,128)S(1)} %get-tuple-element.43), channel_id=1, source_target_pairs={{0,4},{1,5},{2,6},{3,7},{4,0},{5,1},{6,2},{7,3},{8,12},{9,13},{10,... | collective-permute-start | bytes 786440 | tf_op jit(solution)/shard_map/ppermute | solution.py:293
  74.8 13.2 %collective-permute-start.29 = (f32[2,128,256]{2,1,0:T(8,128)S(1)}, f32[2,128,256]{2,1,0:T(8,128)S(1)}, u32[]{:S(2)}, u32[]{:S(2)}) collective-permute-start(f32[2,128,256]{2,1,0:T(8,128)S(1)} %get-tuple-element.44), channel_id=1, source_target_pairs={{0,2},{1,3},{2,0},{3,1},{4,6},{5,7},{6,4},{7,5},{8,10},{9,11},{10,... | collective-permute-start | bytes 786440 | tf_op jit(solution)/shard_map/ppermute | solution.py:293
  81.2 12.3 %collective-permute-start.23 = (f32[128,256]{1,0:T(8,128)S(1)}, f32[128,256]{1,0:T(8,128)S(1)}, u32[]{:S(2)}, u32[]{:S(2)}) collective-permute-start(f32[128,256]{1,0:T(8,128)S(1)} %get-tuple-element.48), channel_id=1, source_target_pairs={{0,16},{1,17},{2,18},{3,19},{4,20},{5,21},{6,22},{7,23},{8,24},{9,... | collective-permute-start | bytes 393224 | tf_op jit(solution)/shard_map/ppermute | solution.py:293
  86.5 7.7 %collective-permute-start.24 = (f32[128,256]{1,0:T(8,128)S(1)}, f32[128,256]{1,0:T(8,128)S(1)}, u32[]{:S(2)}, u32[]{:S(2)}) collective-permute-start(f32[128,256]{1,0:T(8,128)S(1)} %get-tuple-element.47), channel_id=1, source_target_pairs={{0,24},{1,25},{2,26},{3,27},{4,28},{5,29},{6,30},{7,31},{8,16},{9,... | collective-permute-start | bytes 393224 | tf_op jit(solution)/shard_map/ppermute | solution.py:293
  88.1 7.0 %collective-permute-start.30 = (f32[128,256]{1,0:T(8,128)S(1)}, f32[128,256]{1,0:T(8,128)S(1)}, u32[]{:S(2)}, u32[]{:S(2)}) collective-permute-start(f32[128,256]{1,0:T(8,128)S(1)} %slice_bitcast_fusion), channel_id=1, source_target_pairs={{0,8},{1,9},{2,10},{3,11},{4,12},{5,13},{6,14},{7,15},{8,0},{9,1},... | collective-permute-start | bytes 393224 | tf_op jit(solution)/shard_map/ppermute | solution.py:293

commit v4 on v3

--- a/solution.py
+++ b/solution.py
@@ -131,7 +131,9 @@
 
 MIB = 1 << 20
 UNROLL = 4
-ROW_STAGE, ROW_SHARD, ROW_PART, ROW_LEFT, ROW_RIGHT, ROW_A, ROW_AC, ROW_B, ROW_BC = range(9)
+STAGES = 5
+FIELDS = 8
+LEFT, RIGHT, STACK, PART, ROW_A, PART_A, ROW_B, PART_B = range(FIELDS)
 
 
 def split(x):
@@ -140,11 +142,67 @@
     return hi, lo
 
 
-def prep_kernel(f_hbm, o_ref, buf, sem):
+def plan_tasks(depth, per_block, aux_count, source, column, row, target, pairs, info, plan):
+    tasks = pairs.shape[1]
+    chunks = depth // 2
+    tile_me, aux_me = lax.axis_index("tile"), lax.axis_index("aux")
+    z_me, x_me, y_me, c_me = tile_me >> 1, tile_me & 1, aux_me >> 1, aux_me & 1
+    start = (tile_me * aux_count + aux_me) * tasks
+
+    def place(a, b):
+        aux = lax.div(b, per_block)
+        side = (((aux >> 1) ^ y_me) << 1) | ((a & 1) ^ x_me)
+        return (aux & 1) ^ c_me, (a >> 1) ^ z_me, side, lax.rem(b, per_block)
+
+    def target_of(a, b):
+        dc, dz, side, part = place(a, b)
+        turn = (chunks - 1 - (dz >> 1)) * 2
+        straight = jnp.where(side == 0, 3 * depth, 0) + turn + (dz & 1)
+        sideways = depth + turn * 2 + (side - 1) * 2 + (dz & 1)
+        at = jnp.where((side == 1) | (side == 2), sideways, straight)
+        return side == 3, dc * 4 * depth + at, part
+
+    def read(q, carry):
+        at = start + q
+        dc, dz, side, part = place(source[0, at], column[0, at])
+        one = lambda test: jnp.where(test, 1, 0)
+        corner_a, row_a, part_a = target_of(row[0, at], target[0, at])
+        corner_b, row_b, part_b = target_of(target[0, at], row[0, at])
+        stack = ((dc * chunks + (dz >> 1)) * 4 + side) * 2 + (dz & 1)
+        for f, value in enumerate((pairs[0, q], pairs[1, q], stack, part, row_a, part_a, row_b, part_b)):
+            info[f, q] = value
+        info[FIELDS, q] = one(side > 0) + one(side == 3) + one(dz > 1)
+        info[FIELDS + 1, q] = one(corner_a | corner_b)
+        return carry
+
+    lax.fori_loop(0, tasks, read, 0)
+    for s in range(STAGES):
+        plan[s, 0] = 0
+    for urgent in (1, 0):
+        def put(q, carry, urgent=urgent):
+            @pl.when(info[FIELDS + 1, q] == urgent)
+            def _():
+                wave = info[FIELDS, q]
+                late = jnp.maximum(wave, 2) if urgent else 4
+                stage = jnp.where((wave <= 1) & (plan[1, 0] < tasks * 3 // 8), 1, late)
+                stage = jnp.where((wave == 0) & (plan[0, 0] < tasks // 4), 0, stage)
+                n = plan[stage, 0]
+                plan[stage, 0] = n + 1
+                for f in range(FIELDS):
+                    plan[stage, (n + 1) * FIELDS + f] = info[f, q]
+
+            return carry
+
+        lax.fori_loop(0, tasks, put, 0)
+
+
+def prepare_kernel(depth, per_block, aux_count, *refs):
+    f_hbm, plan, o_ref, buf, info, sem = refs[5:]
     slots, rows, w = f_hbm.shape
     copies = [pltpu.make_async_copy(f_hbm.at[s], buf.at[s], sem.at[s]) for s in range(slots)]
     for copy in copies:
         copy.start()
+    plan_tasks(depth, per_block, aux_count, *refs[:5], info, plan)
     step = 256
     for s, copy in enumerate(copies):
         copy.wait()
@@ -157,21 +215,33 @@
             o_ref[s, at, w:] = lo
 
 
-def prep(factors):
+def prepare(depth, per_block, aux_count, tables, pairs, factors):
     s, p, w, _ = factors.shape
     rows = p * w
+    tasks = pairs.shape[0]
+    smem = pl.BlockSpec(memory_space=pltpu.SMEM)
     return pl.pallas_call(
-        prep_kernel,
-        in_specs=[pl.BlockSpec(memory_space=pltpu.HBM)],
-        out_specs=pl.BlockSpec(memory_space=pltpu.VMEM),
-        out_shape=jax.ShapeDtypeStruct((s, rows, 2 * w), jnp.bfloat16),
-        scratch_shapes=[pltpu.VMEM((s, rows, w), jnp.float32), pltpu.SemaphoreType.DMA((s,))],
+        functools.partial(prepare_kernel, depth, per_block, aux_count),
+        in_specs=[smem] * 5 + [pl.BlockSpec(memory_space=pltpu.HBM)],
+        out_specs=[smem, pl.BlockSpec(memory_space=pltpu.VMEM)],
+        out_shape=[
+            jax.ShapeDtypeStruct((STAGES, (tasks + 1) * FIELDS), jnp.int32),
+            jax.ShapeDtypeStruct((s, rows, 2 * w), jnp.bfloat16),
+        ],
+        scratch_shapes=[
+            pltpu.VMEM((s, rows, w), jnp.float32),
+            pltpu.SMEM((FIELDS + 2, tasks), jnp.int32),
+            pltpu.SemaphoreType.DMA((s,)),
+        ],
         compiler_params=pltpu.CompilerParams(vmem_limit_bytes=8 * MIB),
         cost_estimate=pl.CostEstimate(flops=2 * factors.size, bytes_accessed=8 * factors.size, transcendentals=0),
-    )(pltpu.with_memory_space_constraint(factors.reshape(s, rows, w), pltpu.HBM))
-
-
-def task_kernel(stage, first, keep, firsts, cuts, tab, *refs):
+    )(
+        *(pltpu.with_memory_space_constraint(table.T, pltpu.HBM) for table in (*tables, pairs)),
+        pltpu.with_memory_space_constraint(factors.reshape(s, rows, w), pltpu.HBM),
+    )
+
+
+def task_kernel(stage, first, keep, firsts, cuts, plan, *refs):
     f2, *refs = refs
     if not first:
         sums_in, *refs = refs
@@ -181,37 +251,33 @@
     outs, refs = refs[: len(cuts)], refs[len(cuts) :]
     if not keep:
         sums, *refs = refs
-    order, tiles, sem = refs
+    tiles, sem = refs
     w = f2.shape[2] // 2
-    tasks = tab.shape[1]
     pairs = f2.shape[1] // (2 * w)
     f32 = jnp.float32
 
-    def pick(q, count):
-        mine = tab[ROW_STAGE, q] == stage
-
-        @pl.when(mine)
-        def _():
-            order[count] = q
-            shard, part = tab[ROW_SHARD, q], pl.multiple_of(tab[ROW_PART, q] * w, w)
-            for start, stack in zip(firsts, stacks):
-                @pl.when((shard >= start) & (shard < start + stack.shape[0]))
-                def _(start=start, stack=stack):
-                    pltpu.make_async_copy(
-                        stack.at[shard - start, :, pl.ds(part, w)], tiles.at[count], sem.at[count]
-                    ).start()
-
-        return count + mine.astype(jnp.int32)
-
-    count = lax.fori_loop(0, tasks, pick, 0)
+    count = plan[stage, 0]
+
+    def field(i, f):
+        return plan[stage, (i + 1) * FIELDS + f]
+
+    def fetch(i, carry):
+        shard, part = field(i, STACK), pl.multiple_of(field(i, PART) * w, w)
+        for start, stack in zip(firsts, stacks):
+            @pl.when((shard >= start) & (shard < start + stack.shape[0]))
+            def _(start=start, stack=stack):
+                pltpu.make_async_copy(stack.at[shard - start, :, pl.ds(part, w)], tiles.at[i], sem.at[i]).start()
+
+        return carry
+
+    lax.fori_loop(0, count, fetch, 0)
     sums[...] = jnp.zeros_like(sums) if first else sums_in[...]
 
     def rows(p):
         return slice(p * 2 * w, (p + 1) * 2 * w)
 
     def one(i):
-        q = order[i]
-        left, right = tab[ROW_LEFT, q], tab[ROW_RIGHT, q]
+        left, right = field(i, LEFT), field(i, RIGHT)
         hi, lo = split(tiles[i])
         half = jnp.concatenate([hi, lo], axis=1)
         wt = jnp.concatenate([half, half], axis=0)
@@ -226,10 +292,9 @@
             acc = d if acc is None else acc + d
         part = acc[:w] + acc[w:]
         part = part[:, :w] + part[:, w:]
-        c = pl.ds(pl.multiple_of(tab[ROW_AC, q] * w, w), w)
-        sums[tab[ROW_A, q], :, c] = sums[tab[ROW_A, q], :, c] + part
-        c = pl.ds(pl.multiple_of(tab[ROW_BC, q] * w, w), w)
-        sums[tab[ROW_B, q], :, c] = sums[tab[ROW_B, q], :, c] + part.T
+        for row, column, value in ((ROW_A, PART_A, part), (ROW_B, PART_B, part.T)):
+            at, c = field(i, row), pl.ds(pl.multiple_of(field(i, column) * w, w), w)
+            sums[at, :, c] = sums[at, :, c] + value
 
     def several(start, n):
         for k in range(n):
@@ -257,8 +322,8 @@
         out[...] = sums[start : start + size]
 
 
-def run_stage(table, stage, f2, stacks, firsts, sums, shape, cuts, keep):
-    tasks = table.shape[1]
+def run_stage(plan, stage, f2, stacks, firsts, sums, shape, cuts, keep):
+    tasks = plan.shape[1] // FIELDS - 1
     w = f2.shape[2] // 2
     first = sums is None
     vmem = pl.BlockSpec(memory_space=pltpu.VMEM)
@@ -272,13 +337,12 @@
         out_specs=[vmem] * len(outs),
         out_shape=outs,
         scratch_shapes=([] if keep else [pltpu.VMEM(shape, jnp.float32)]) + [
-            pltpu.SMEM((tasks,), jnp.int32),
             pltpu.VMEM((tasks, w, w), jnp.float32),
             pltpu.SemaphoreType.DMA((tasks,)),
         ],
         compiler_params=pltpu.CompilerParams(vmem_limit_bytes=12 * MIB),
         cost_estimate=pl.CostEstimate(flops=tasks * f2.shape[1] * w * w * 4, bytes_accessed=2 * f2.size, transcendentals=0),
-    )(table, f2, *([] if first else [sums]), *stacks)
+    )(plan, f2, *([] if first else [sums]), *stacks)
 
 
 def shift(value, sizes, move):
@@ -328,52 +392,18 @@
     tile_me = lax.axis_index("tile")
     aux_me = lax.axis_index("aux")
     tile_width = factors.shape[-1]
-    task_count = slot_pairs.shape[0]
     per_block = tiles_all // aux_count
     depth = tiles_all // 2
     chunks = depth // 2
     sizes = (depth, 2, aux_count // 2, 2)
-    z_me, x_me = tile_me >> 1, tile_me & 1
-    y_me, core_me = aux_me >> 1, aux_me & 1
-    on_first = core_me == 0
+    on_first = (aux_me & 1) == 0
 
     def move(value, how):
         return shift(value, sizes, how)
 
-    start = (tile_me * aux_count + aux_me) * task_count
-
-    def own(table):
-        return lax.dynamic_slice_in_dim(table[:, 0], start, task_count)
-
-    def place(row, column):
-        aux = column // per_block
-        side = ((aux >> 1) ^ y_me) * 2 + ((row & 1) ^ x_me)
-        return (aux & 1) ^ core_me, (row >> 1) ^ z_me, side, column % per_block
-
-    def source_of(row, column):
-        dc, dz, side, part = place(row, column)
-        stage = jnp.where(side > 0, 1, 0) + jnp.where(side == 3, 1, 0) + jnp.where(dz > 1, 1, 0)
-        return stage, ((dc * chunks + (dz >> 1)) * 4 + side) * 2 + (dz & 1), part
-
-    def target_of(row, column):
-        dc, dz, side, part = place(row, column)
-        turn = (chunks - 1 - (dz >> 1)) * 2
-        straight = jnp.where(side == 0, 3 * depth, 0) + turn + (dz & 1)
-        sideways = depth + turn * 2 + (side - 1) * 2 + (dz & 1)
-        at = jnp.where((side == 1) | (side == 2), sideways, straight)
-        return side == 3, dc * 4 * depth + at, part
-
-    row_a, col_b = own(target_row), own(target_column)
-    corner_a, *target_a = target_of(row_a, col_b)
-    corner_b, *target_b = target_of(col_b, row_a)
-    stage, *source = source_of(own(density_source), own(density_column))
-    stage = jnp.where((stage > 1) & ~(corner_a | corner_b), 4, stage)
-    rows = [stage, *source, slot_pairs[:, 0], slot_pairs[:, 1], *target_a, *target_b]
-    which = lax.broadcasted_iota(jnp.int32, (len(rows), task_count), 0)
-    table = sum(jnp.where(which == at, row[None, :], 0) for at, row in enumerate(rows))
-
     column = [density] + [move(density, across_z(step)) for step in range(1, depth)]
-    split_factors = prep(factors)
+    tables = (density_source, density_column, target_row, target_column)
+    plan, split_factors = prepare(depth, per_block, aux_count, tables, slot_pairs, factors)
     by_stage = [([], []) for _ in range(4)]
     for k in range(chunks):
         here = jnp.stack(column[2 * k : 2 * k + 2])
@@ -389,6 +419,9 @@
                 by_stage[stage][0].append(stack)
                 by_stage[stage][1].append(at)
 
+    for known in range(2):
+        by_stage[1][known].extend(by_stage[0][known])
+        by_stage[2][known].extend(by_stage[1][known])
     by_stage.append(tuple(one + other for one, other in zip(by_stage[2], by_stage[3])))
     shape = (8 * depth,) + density.shape
     corner_cuts = [(at, depth) for at in (0, 4 * depth)]
@@ -397,7 +430,7 @@
     sums = None
     for stage, (values, firsts) in enumerate(by_stage):
         cut = {3: corner_cuts, 4: cuts}.get(stage, ())
-        results = run_stage(table, stage, split_factors, values, firsts, sums, shape, cut, stage < 4)
+        results = run_stage(plan, stage, split_factors, values, firsts, sums, shape, cut, stage < 4)
         sums = results[0]
         if stage == 3:
             corner_mine, corner_other = results[1:]

time: 96.7 us -> 107 us (1.11)
  waiting for transfers between devices: 20.2 us -> 39 us
  starting transfers between devices: 35.2 us -> 25.6 us
  Pallas kernels: 36.3 us -> 39.5 us
  other arithmetic: 2.27 us -> 0.62 us
    ppermute x31, waiting for transfers between devices: 20.2 us -> 39 us  [shift(): return lax.ppermute(value, AXES, pairs)]
    ppermute x31, starting transfers between devices: 35.2 us -> 25.6 us  [shift(): return lax.ppermute(value, AXES, pairs)]
    pallas_call x1, Pallas kernels: 3.07 us -> 7.67 us  [prepare(): pl.pallas_call(functools.partial(prepare_kernel, depth, per_block, aux_co...]
    select_n x3 -> x0, other arithmetic: 1.55 us -> none  [the longest x1 0.79 us: gathered(): stage = jnp.where((stage > 1) & ~(corner_a | corner_b), 4, stage)]
    pallas_call x5, Pallas kernels: 33.3 us -> 31.8 us  [run_stage(): pl.pallas_call(body, in_specs=[pl.BlockSpec(memory_space=pltpu.SMEM)] + [...]
  transfers between devices with their start and end apart: 31 -> 31, of which waited for: 12 -> 12; matrix products, arithmetic and copies ran while one was open for 3% -> 1% of each run, Pallas kernels for 34% -> 34%
where the time goes in v4:
time: 107 us; the launch traced here: 106 us
  Pallas kernels  39.5 us (37%)
  waiting for transfers between devices  39 us (36%)
  starting transfers between devices  25.6 us (24%)
    ppermute x31, waiting for transfers between devices, shift(): return lax.ppermute(value, AXES, pairs)  39 us
    pallas_call x5, Pallas kernels, run_stage(): pl.pallas_call(body, in_specs=[pl.BlockSpec(memory_space=pltpu.SMEM)] + [...  31.8 us
    ppermute x31, starting transfers between devices, shift(): return lax.ppermute(value, AXES, pairs)  25.6 us
    pallas_call x1, Pallas kernels, prepare(): pl.pallas_call(functools.partial(prepare_kernel, depth, per_block, aux_co...  7.67 us
  transfers between devices with their start and end apart: 31, of which 12 were waited for; matrix products, arithmetic and copies ran while one was open for 1% of the time, Pallas kernels for 34%

profile of v4, /device:TPU:0, one launch (start us, length us, event | category | flops | bytes accessed | tf_op | source)
XLA Modules:
  0.0 106.5 jit_solution(9435672789189598684)
XLA Ops:
  0.0 5.1 %collective-permute-start.7 = (f32[128,256]{1,0:T(8,128)}, f32[128,256]{1,0:T(8,128)S(1)}, u32[]{:S(2)}, u32[]{:S(2)}) collective-permute-start(f32[128,256]{1,0:T(8,128)} %param.8), channel_id=1, source_target_pairs={{0,24},{1,25},{2,26},{3,27},{4,28},{5,29},{6,30},{7,31},{8,16},{9,... | collective-permute-start | bytes 393224 | tf_op jit(solution)/shard_map/ppermute | solution.py:357
  5.1 0.0 collective-permute-start.6
  5.1 0.6 collective-permute-start
  5.7 4.1 %collective-permute-done.7 = f32[128,256]{1,0:T(8,128)S(1)} collective-permute-done((f32[128,256]{1,0:T(8,128)}, f32[128,256]{1,0:T(8,128)S(1)}, u32[]{:S(2)}, u32[]{:S(2)}) %collective-permute-start.7) | collective-permute-done | bytes 131104 | tf_op jit(solution)/shard_map/ppermute | solution.py:357
  9.8 6.6 %collective-permute-done.6 = f32[128,256]{1,0:T(8,128)S(1)} collective-permute-done((f32[128,256]{1,0:T(8,128)}, f32[128,256]{1,0:T(8,128)S(1)}, u32[]{:S(2)}, u32[]{:S(2)}) %collective-permute-start.6) | collective-permute-done | bytes 131104 | tf_op jit(solution)/shard_map/ppermute | solution.py:357
  16.4 1.6 %collective-permute-start.13 = (f32[2,128,256]{2,1,0:T(8,128)S(1)}, f32[2,128,256]{2,1,0:T(8,128)S(1)}, u32[]{:S(2)}, u32[]{:S(2)}) collective-permute-start(f32[2,128,256]{2,1,0:T(8,128)S(1)} %pad_maximum_fusion.1.refs_6_.refs_12_), channel_id=1, source_target_pairs={{0,2},{1,3},{2,0},{3,1},{4,6},{5,7},{6,4},{7,5},{8,10},{9,11},{10,... | collective-permute-start | bytes 786440 | tf_op jit(solution)/shard_map/ppermute | solution.py:357
  18.0 1.5 %collective-permute-start.11 = (f32[2,128,256]{2,1,0:T(8,128)S(1)}, f32[2,128,256]{2,1,0:T(8,128)S(1)}, u32[]{:S(2)}, u32[]{:S(2)}) collective-permute-start(f32[2,128,256]{2,1,0:T(8,128)S(1)} %pad_maximum_fusion.1.refs_6_.refs_12_), channel_id=1, source_target_pairs={{0,4},{1,5},{2,6},{3,7},{4,0},{5,1},{6,2},{7,3},{8,12},{9,13},{10,... | collective-permute-start | bytes 786440 | tf_op jit(solution)/shard_map/ppermute | solution.py:357
  19.5 7.7 %shard_map.82 = (s32[5,264]{1,0:T(8,128)S(1)}, bf16[6,2048,256]{2,1,0:T(8,128)(2,1)S(1)}) custom-call(s32[1,1024]{1,0:T(1,128)} %bitcast.51, s32[1,1024]{1,0:T(1,128)} %bitcast.52, s32[1,1024]{1,0:T(1,128)} %bitcast.53, s32[1,1024]{1,0:T(1,128)} %bitcast.54, s32[2,32]{1,0:T(2,128)} %bitcast.55, f32[6,2048,128]{2,1,0:T(8,128)} %bitcast.45), custom_call_target="tpu_custom_call" | custom-call | flops 3145728 | bytes 12582912 | tf_op jit(solution)/shard_map/pallas_call | solution.py:223
  27.1 0.0 collective-permute-done
  27.2 0.6 collective-permute-start.4
  27.8 0.5 collective-permute-start.2
  28.3 0.0 collective-permute-start.8
  28.3 0.0 collective-permute-done.13.refs_6_
  28.3 0.5 collective-permute-start.1
  28.8 0.0 collective-permute-done.11.refs_4_
  28.9 1.6 %collective-permute-start.15 = (f32[2,128,256]{2,1,0:T(8,128)S(1)}, f32[2,128,256]{2,1,0:T(8,128)S(1)}, u32[]{:S(2)}, u32[]{:S(2)}) collective-permute-start(f32[2,128,256]{2,1,0:T(8,128)S(1)} %broadcast_select_fusion), channel_id=1, source_target_pairs={{0,2},{1,5},{2,0},{3,7},{4,6},{5,1},{6,4},{7,3},{8,10},{9,13},{10,... | collective-permute-start | bytes 786440 | tf_op jit(solution)/shard_map/ppermute | solution.py:357
  30.4 3.6 %collective-permute-done.4.refs_4_.refs_10_ = f32[2,128,256]{2,1,0:T(8,128)S(1)} collective-permute-done((f32[2,128,256]{2,1,0:T(8,128)S(1)}, f32[2,128,256]{2,1,0:T(8,128)S(1)}, u32[]{:S(2)}, u32[]{:S(2)}) %collective-permute-start.4) | collective-permute-done | bytes 262176 | tf_op jit(solution)/shard_map/ppermute | solution.py:357
  34.0 2.9 %collective-permute-done.2.refs_2_.refs_8_ = f32[2,128,256]{2,1,0:T(8,128)S(1)} collective-permute-done((f32[2,128,256]{2,1,0:T(8,128)S(1)}, f32[2,128,256]{2,1,0:T(8,128)S(1)}, u32[]{:S(2)}, u32[]{:S(2)}) %collective-permute-start.2) | collective-permute-done | bytes 262176 | tf_op jit(solution)/shard_map/ppermute | solution.py:357
  37.0 1.6 %collective-permute-start.9 = (f32[2,128,256]{2,1,0:T(8,128)S(1)}, f32[2,128,256]{2,1,0:T(8,128)S(1)}, u32[]{:S(2)}, u32[]{:S(2)}) collective-permute-start(f32[2,128,256]{2,1,0:T(8,128)S(1)} %broadcast_select_fusion.1), channel_id=1, source_target_pairs={{0,2},{1,5},{2,0},{3,7},{4,6},{5,1},{6,4},{7,3},{8,10},{9,13},{10,... | collective-permute-start | bytes 786440 | tf_op jit(solution)/shard_map/ppermute | solution.py:357
  38.6 0.0 collective-permute-start.5
  38.6 0.5 collective-permute-start.3
  39.1 4.1 %shard_map.83.refs_1_ = f32[32,128,256]{2,1,0:T(8,128)S(1)} custom-call(s32[5,264]{1,0:T(8,128)S(1)} %get-tuple-element.21.plan, bf16[6,2048,256]{2,1,0:T(8,128)(2,1)S(1)} %get-tuple-element.23.refs_0_, f32[2,128,256]{2,1,0:T(8,128)S(1)} %pad_maximum_fusion.refs_1_.refs_8_.refs_14_, f32[2,128,256]{2,1,0:T(8,128)S(1)} %collective-permute-done.1.refs_2_.refs_9_.refs_15_), custom_call_target="tpu_custom_call" | custom-call | flops 4294967296 | bytes 6291456 | tf_op jit(solution)/shard_map/pallas_call | solution.py:333
  43.2 1.7 %collective-permute-start.14 = (f32[2,128,256]{2,1,0:T(8,128)S(1)}, f32[2,128,256]{2,1,0:T(8,128)S(1)}, u32[]{:S(2)}, u32[]{:S(2)}) collective-permute-start(f32[2,128,256]{2,1,0:T(8,128)S(1)} %collective-permute-done.13.refs_6_), channel_id=1, source_target_pairs={{0,1},{1,0},{2,3},{3,2},{4,5},{5,4},{6,7},{7,6},{8,9},{9,8},{10,11... | collective-permute-start | bytes 786440 | tf_op jit(solution)/shard_map/ppermute | solution.py:357
  44.9 0.1 collective-permute-start.12
  44.9 0.0 collective-permute-done.5.refs_5_.refs_11_
  44.9 0.4 collective-permute-start.16
  45.4 0.1 collective-permute-start.10
  45.5 10.0 %shard_map.84.refs_1_ = f32[32,128,256]{2,1,0:T(8,128)S(1)} custom-call(s32[5,264]{1,0:T(8,128)S(1)} %get-tuple-element.21.plan, bf16[6,2048,256]{2,1,0:T(8,128)(2,1)S(1)} %get-tuple-element.23.refs_0_, f32[32,128,256]{2,1,0:T(8,128)S(1)} %shard_map.83.refs_1_, f32[2,128,256]{2,1,0:T(8,128)S(1)} %collective-permute-done.2.refs_2_.refs_8_, ...), custom_call_target="tpu_custom_call" | custom-call | flops 4294967296 | bytes 6291456 | tf_op jit(solution)/shard_map/pallas_call | solution.py:333
  55.5 0.0 collective-permute-done.14.refs_7_
  55.5 0.0 collective-permute-done.10.refs_3_
  55.5 5.7 %shard_map.85.refs_1_ = f32[32,128,256]{2,1,0:T(8,128)S(1)} custom-call(s32[5,264]{1,0:T(8,128)S(1)} %get-tuple-element.21.plan, bf16[6,2048,256]{2,1,0:T(8,128)(2,1)S(1)} %get-tuple-element.23.refs_0_, f32[32,128,256]{2,1,0:T(8,128)S(1)} %shard_map.84.refs_1_, f32[2,128,256]{2,1,0:T(8,128)S(1)} %collective-permute-done.9.refs_2_, ...), custom_call_target="tpu_custom_call" | custom-call | flops 4294967296 | bytes 6291456 | tf_op jit(solution)/shard_map/pallas_call | solution.py:333
  61.2 0.0 collective-permute-done.16.refs_3_.refs_17_
  61.2 3.0 %shard_map.86 = (f32[32,128,256]{2,1,0:T(8,128)S(1)}, f32[4,128,256]{2,1,0:T(8,128)S(1)}, f32[4,128,256]{2,1,0:T(8,128)S(1)}) custom-call(s32[5,264]{1,0:T(8,128)S(1)} %get-tuple-element.21.plan, bf16[6,2048,256]{2,1,0:T(8,128)(2,1)S(1)} %get-tuple-element.23.refs_0_, f32[32,128,256]{2,1,0:T(8,128)S(1)} %shard_map.85.refs_1_, ...), custom_call_target="tpu_custom_call" | custom-call | flops 4294967296 | bytes 6291456 | tf_op jit(solution)/shard_map/pallas_call | solution.py:333
  64.2 2.6 %collective-permute-start.19 = (f32[4,128,256]{2,1,0:T(8,128)S(1)}, f32[4,128,256]{2,1,0:T(8,128)S(1)}, u32[]{:S(2)}, u32[]{:S(2)}) collective-permute-start(f32[4,128,256]{2,1,0:T(8,128)S(1)} %get-tuple-element.32), channel_id=1, source_target_pairs={{0,1},{1,0},{2,3},{3,2},{4,5},{5,4},{6,7},{7,6},{8,9},{9,8},{10,11... | collective-permute-start | bytes 1572872 | tf_op jit(solution)/shard_map/ppermute | solution.py:357
  66.8 9.0 %shard_map.87 = (f32[4,128,256]{2,1,0:T(8,128)S(1)}, f32[4,128,256]{2,1,0:T(8,128)S(1)}, f32[2,128,256]{2,1,0:T(8,128)S(1)}, f32[2,128,256]{2,1,0:T(8,128)S(1)},...) custom-call(s32[5,264]{1,0:T(8,128)S(1)} %get-tuple-element.21.plan,, ...), custom_call_target="tpu_custom_call" | custom-call | flops 4294967296 | bytes 6291456 | tf_op jit(solution)/shard_map/pallas_call | solution.py:333
  75.8 0.1 collective-permute-start.18
  75.9 0.5 collective-permute-start.26
  76.4 0.1 add.58
  76.5 0.1 collective-permute-start.20
  76.6 0.1 collective-permute-start.17
  76.7 1.9 %collective-permute-start.27 = (f32[2,128,256]{2,1,0:T(8,128)S(1)}, f32[2,128,256]{2,1,0:T(8,128)S(1)}, u32[]{:S(2)}, u32[]{:S(2)}) collective-permute-start(f32[2,128,256]{2,1,0:T(8,128)S(1)} %get-tuple-element.42), channel_id=1, source_target_pairs={{0,2},{1,5},{2,0},{3,7},{4,6},{5,1},{6,4},{7,3},{8,10},{9,13},{10,... | collective-permute-start | bytes 786440 | tf_op jit(solution)/shard_map/ppermute | solution.py:357
  78.6 0.1 add.57
  78.7 4.2 %collective-permute-done.20 = f32[2,128,256]{2,1,0:T(8,128)S(1)} collective-permute-done((f32[2,128,256]{2,1,0:T(8,128)S(1)}, f32[2,128,256]{2,1,0:T(8,128)S(1)}, u32[]{:S(2)}, u32[]{:S(2)}) %collective-permute-start.20) | collective-permute-done | bytes 262176 | tf_op jit(solution)/shard_map/ppermute | solution.py:357
  82.9 0.1 slice_add_fusion.3
  83.0 0.1 collective-permute-start.21
  83.1 0.7 collective-permute-start.22
  83.8 0.1 add.65
  83.8 2.7 %collective-permute-done.27 = f32[2,128,256]{2,1,0:T(8,128)S(1)} collective-permute-done((f32[2,128,256]{2,1,0:T(8,128)S(1)}, f32[2,128,256]{2,1,0:T(8,128)S(1)}, u32[]{:S(2)}, u32[]{:S(2)}) %collective-permute-start.27) | collective-permute-done | bytes 262176 | tf_op jit(solution)/shard_map/ppermute | solution.py:357
  86.5 0.1 slice_add_fusion.1
  86.6 0.1 collective-permute-start.28
  86.7 0.7 collective-permute-start.29
  87.4 4.9 %collective-permute-done.21 = f32[2,128,256]{2,1,0:T(8,128)S(1)} collective-permute-done((f32[2,128,256]{2,1,0:T(8,128)S(1)}, f32[2,128,256]{2,1,0:T(8,128)S(1)}, u32[]{:S(2)}, u32[]{:S(2)}) %collective-permute-start.21) | collective-permute-done | bytes 262176 | tf_op jit(solution)/shard_map/ppermute | solution.py:357
  92.3 0.1 collective-permute-done.22
  92.3 0.1 add_add_fusion.1
  92.4 2.5 %collective-permute-start.24 = (f32[128,256]{1,0:T(8,128)S(1)}, f32[128,256]{1,0:T(8,128)S(1)}, u32[]{:S(2)}, u32[]{:S(2)}) collective-permute-start(f32[128,256]{1,0:T(8,128)S(1)} %get-tuple-element.43), channel_id=1, source_target_pairs={{0,24},{1,25},{2,26},{3,27},{4,28},{5,29},{6,30},{7,31},{8,16},{9,... | collective-permute-start | bytes 393224 | tf_op jit(solution)/shard_map/ppermute | solution.py:357
  94.9 1.2 %collective-permute-done.28 = f32[2,128,256]{2,1,0:T(8,128)S(1)} collective-permute-done((f32[2,128,256]{2,1,0:T(8,128)S(1)}, f32[2,128,256]{2,1,0:T(8,128)S(1)}, u32[]{:S(2)}, u32[]{:S(2)}) %collective-permute-start.28) | collective-permute-done | bytes 262176 | tf_op jit(solution)/shard_map/ppermute | solution.py:357
  96.1 0.9 collective-permute-done.29
  97.0 0.1 add_add_fusion
  97.1 0.1 collective-permute-start.30
  97.2 2.3 %collective-permute-done.24 = f32[128,256]{1,0:T(8,128)S(1)} collective-permute-done((f32[128,256]{1,0:T(8,128)S(1)}, f32[128,256]{1,0:T(8,128)S(1)}, u32[]{:S(2)}, u32[]{:S(2)}) %collective-permute-start.24) | collective-permute-done | bytes 131104 | tf_op jit(solution)/shard_map/ppermute | solution.py:357
  99.4 5.5 %collective-permute-done.23 = f32[128,256]{1,0:T(8,128)S(1)} collective-permute-done((f32[128,256]{1,0:T(8,128)S(1)}, f32[128,256]{1,0:T(8,128)S(1)}, u32[]{:S(2)}, u32[]{:S(2)}) %collective-permute-start.23) | collective-permute-done | bytes 131104 | tf_op jit(solution)/shard_map/ppermute | solution.py:357
  105.0 0.3 fusion
  105.3 0.4 fusion.6
  105.7 0.8 copy.11
  (25 shorter events, 0.2 us)
Async XLA Ops:
  0.0 105.0 %copy-start = (f32[1024,128]{1,0:T(8,128)S(1)}, f32[1024,128]{1,0:T(8,128)}, u32[]{:S(2)}) copy-start(f32[1024,128]{1,0:T(8,128)} %param.10) | copy-start | bytes 1572868
  0.0 27.2 %copy-start.1 = (f32[128,256]{1,0:T(8,128)S(1)}, f32[128,256]{1,0:T(8,128)}, u32[]{:S(2)}) copy-start(f32[128,256]{1,0:T(8,128)} %param.8) | copy-start | bytes 393220
  0.0 9.8 %collective-permute-start.7 = (f32[128,256]{1,0:T(8,128)}, f32[128,256]{1,0:T(8,128)S(1)}, u32[]{:S(2)}, u32[]{:S(2)}) collective-permute-start(f32[128,256]{1,0:T(8,128)} %param.8), channel_id=1, source_target_pairs={{0,24},{1,25},{2,26},{3,27},{4,28},{5,29},{6,30},{7,31},{8,16},{9,... | collective-permute-start | bytes 393224 | tf_op jit(solution)/shard_map/ppermute | solution.py:357
  5.1 11.3 %collective-permute-start.6 = (f32[128,256]{1,0:T(8,128)}, f32[128,256]{1,0:T(8,128)S(1)}, u32[]{:S(2)}, u32[]{:S(2)}) collective-permute-start(f32[128,256]{1,0:T(8,128)} %param.8), channel_id=1, source_target_pairs={{0,16},{1,17},{2,18},{3,19},{4,20},{5,21},{6,22},{7,23},{8,24},{9,... | collective-permute-start | bytes 393224 | tf_op jit(solution)/shard_map/ppermute | solution.py:357
  5.1 22.1 %collective-permute-start = (f32[128,256]{1,0:T(8,128)}, f32[128,256]{1,0:T(8,128)S(1)}, u32[]{:S(2)}, u32[]{:S(2)}) collective-permute-start(f32[128,256]{1,0:T(8,128)} %param.8), channel_id=1, source_target_pairs={{0,8},{1,9},{2,10},{3,11},{4,12},{5,13},{6,14},{7,15},{8,0},{9,1},... | collective-permute-start | bytes 393224 | tf_op jit(solution)/shard_map/ppermute | solution.py:357
  16.4 11.9 %collective-permute-start.13 = (f32[2,128,256]{2,1,0:T(8,128)S(1)}, f32[2,128,256]{2,1,0:T(8,128)S(1)}, u32[]{:S(2)}, u32[]{:S(2)}) collective-permute-start(f32[2,128,256]{2,1,0:T(8,128)S(1)} %pad_maximum_fusion.1.refs_6_.refs_12_), channel_id=1, source_target_pairs={{0,2},{1,3},{2,0},{3,1},{4,6},{5,7},{6,4},{7,5},{8,10},{9,11},{10,... | collective-permute-start | bytes 786440 | tf_op jit(solution)/shard_map/ppermute | solution.py:357
  18.0 10.8 %collective-permute-start.11 = (f32[2,128,256]{2,1,0:T(8,128)S(1)}, f32[2,128,256]{2,1,0:T(8,128)S(1)}, u32[]{:S(2)}, u32[]{:S(2)}) collective-permute-start(f32[2,128,256]{2,1,0:T(8,128)S(1)} %pad_maximum_fusion.1.refs_6_.refs_12_), channel_id=1, source_target_pairs={{0,4},{1,5},{2,6},{3,7},{4,0},{5,1},{6,2},{7,3},{8,12},{9,13},{10,... | collective-permute-start | bytes 786440 | tf_op jit(solution)/shard_map/ppermute | solution.py:357
  27.2 6.8 %collective-permute-start.4 = (f32[2,128,256]{2,1,0:T(8,128)S(1)}, f32[2,128,256]{2,1,0:T(8,128)S(1)}, u32[]{:S(2)}, u32[]{:S(2)}) collective-permute-start(f32[2,128,256]{2,1,0:T(8,128)S(1)} %pad_maximum_fusion.refs_1_.refs_8_.refs_14_), channel_id=1, source_target_pairs={{0,2},{1,3},{2,0},{3,1},{4,6},{5,7},{6,4},{7,5},{8,10},{9,11},{10,... | collective-permute-start | bytes 786440 | tf_op jit(solution)/shard_map/ppermute | solution.py:357
  27.8 9.2 %collective-permute-start.2 = (f32[2,128,256]{2,1,0:T(8,128)S(1)}, f32[2,128,256]{2,1,0:T(8,128)S(1)}, u32[]{:S(2)}, u32[]{:S(2)}) collective-permute-start(f32[2,128,256]{2,1,0:T(8,128)S(1)} %pad_maximum_fusion.refs_1_.refs_8_.refs_14_), channel_id=1, source_target_pairs={{0,4},{1,5},{2,6},{3,7},{4,0},{5,1},{6,2},{7,3},{8,12},{9,13},{10,... | collective-permute-start | bytes 786440 | tf_op jit(solution)/shard_map/ppermute | solution.py:357
  28.3 14.9 %collective-permute-start.8 = (f32[2,128,256]{2,1,0:T(8,128)S(1)}, f32[2,128,256]{2,1,0:T(8,128)S(1)}, u32[]{:S(2)}, u32[]{:S(2)}) collective-permute-start(f32[2,128,256]{2,1,0:T(8,128)S(1)} %pad_maximum_fusion.1.refs_6_.refs_12_), channel_id=1, source_target_pairs={{0,1},{1,0},{2,3},{3,2},{4,5},{5,4},{6,7},{7,6},{8,9},{9,8},{10,11... | collective-permute-start | bytes 786440 | tf_op jit(solution)/shard_map/ppermute | solution.py:357
  28.3 10.3 %collective-permute-start.1 = (f32[2,128,256]{2,1,0:T(8,128)S(1)}, f32[2,128,256]{2,1,0:T(8,128)S(1)}, u32[]{:S(2)}, u32[]{:S(2)}) collective-permute-start(f32[2,128,256]{2,1,0:T(8,128)S(1)} %pad_maximum_fusion.refs_1_.refs_8_.refs_14_), channel_id=1, source_target_pairs={{0,1},{1,0},{2,3},{3,2},{4,5},{5,4},{6,7},{7,6},{8,9},{9,8},{10,11... | collective-permute-start | bytes 786440 | tf_op jit(solution)/shard_map/ppermute | solution.py:357
  28.9 16.0 %collective-permute-start.15 = (f32[2,128,256]{2,1,0:T(8,128)S(1)}, f32[2,128,256]{2,1,0:T(8,128)S(1)}, u32[]{:S(2)}, u32[]{:S(2)}) collective-permute-start(f32[2,128,256]{2,1,0:T(8,128)S(1)} %broadcast_select_fusion), channel_id=1, source_target_pairs={{0,2},{1,5},{2,0},{3,7},{4,6},{5,1},{6,4},{7,3},{8,10},{9,13},{10,... | collective-permute-start | bytes 786440 | tf_op jit(solution)/shard_map/ppermute | solution.py:357
  37.0 8.4 %collective-permute-start.9 = (f32[2,128,256]{2,1,0:T(8,128)S(1)}, f32[2,128,256]{2,1,0:T(8,128)S(1)}, u32[]{:S(2)}, u32[]{:S(2)}) collective-permute-start(f32[2,128,256]{2,1,0:T(8,128)S(1)} %broadcast_select_fusion.1), channel_id=1, source_target_pairs={{0,2},{1,5},{2,0},{3,7},{4,6},{5,1},{6,4},{7,3},{8,10},{9,13},{10,... | collective-permute-start | bytes 786440 | tf_op jit(solution)/shard_map/ppermute | solution.py:357
  38.6 6.4 %collective-permute-start.5 = (f32[2,128,256]{2,1,0:T(8,128)S(1)}, f32[2,128,256]{2,1,0:T(8,128)S(1)}, u32[]{:S(2)}, u32[]{:S(2)}) collective-permute-start(f32[2,128,256]{2,1,0:T(8,128)S(1)} %collective-permute-done.4.refs_4_.refs_10_), channel_id=1, source_target_pairs={{0,1},{1,0},{2,3},{3,2},{4,5},{5,4},{6,7},{7,6},{8,9},{9,8},{10,11... | collective-permute-start | bytes 786440 | tf_op jit(solution)/shard_map/ppermute | solution.py:357
  38.6 6.9 %collective-permute-start.3 = (f32[2,128,256]{2,1,0:T(8,128)S(1)}, f32[2,128,256]{2,1,0:T(8,128)S(1)}, u32[]{:S(2)}, u32[]{:S(2)}) collective-permute-start(f32[2,128,256]{2,1,0:T(8,128)S(1)} %collective-permute-done.2.refs_2_.refs_8_), channel_id=1, source_target_pairs={{0,1},{1,0},{2,3},{3,2},{4,5},{5,4},{6,7},{7,6},{8,9},{9,8},{10,11... | collective-permute-start | bytes 786440 | tf_op jit(solution)/shard_map/ppermute | solution.py:357
  43.2 12.3 %collective-permute-start.14 = (f32[2,128,256]{2,1,0:T(8,128)S(1)}, f32[2,128,256]{2,1,0:T(8,128)S(1)}, u32[]{:S(2)}, u32[]{:S(2)}) collective-permute-start(f32[2,128,256]{2,1,0:T(8,128)S(1)} %collective-permute-done.13.refs_6_), channel_id=1, source_target_pairs={{0,1},{1,0},{2,3},{3,2},{4,5},{5,4},{6,7},{7,6},{8,9},{9,8},{10,11... | collective-permute-start | bytes 786440 | tf_op jit(solution)/shard_map/ppermute | solution.py:357
  44.9 10.7 %collective-permute-start.12 = (f32[2,128,256]{2,1,0:T(8,128)S(1)}, f32[2,128,256]{2,1,0:T(8,128)S(1)}, u32[]{:S(2)}, u32[]{:S(2)}) collective-permute-start(f32[2,128,256]{2,1,0:T(8,128)S(1)} %collective-permute-done.11.refs_4_), channel_id=1, source_target_pairs={{0,1},{1,0},{2,3},{3,2},{4,5},{5,4},{6,7},{7,6},{8,9},{9,8},{10,11... | collective-permute-start | bytes 786440 | tf_op jit(solution)/shard_map/ppermute | solution.py:357
  44.9 16.3 %collective-permute-start.16 = (f32[2,128,256]{2,1,0:T(8,128)S(1)}, f32[2,128,256]{2,1,0:T(8,128)S(1)}, u32[]{:S(2)}, u32[]{:S(2)}) collective-permute-start(f32[2,128,256]{2,1,0:T(8,128)S(1)} %collective-permute-done.15.refs_2_.refs_16_), channel_id=1, source_target_pairs={{0,1},{1,0},{2,3},{3,2},{4,5},{5,4},{6,7},{7,6},{8,9},{9,8},{10,11... | collective-permute-start | bytes 786440 | tf_op jit(solution)/shard_map/ppermute | solution.py:357
  45.4 10.2 %collective-permute-start.10 = (f32[2,128,256]{2,1,0:T(8,128)S(1)}, f32[2,128,256]{2,1,0:T(8,128)S(1)}, u32[]{:S(2)}, u32[]{:S(2)}) collective-permute-start(f32[2,128,256]{2,1,0:T(8,128)S(1)} %collective-permute-done.9.refs_2_), channel_id=1, source_target_pairs={{0,1},{1,0},{2,3},{3,2},{4,5},{5,4},{6,7},{7,6},{8,9},{9,8},{10,11... | collective-permute-start | bytes 786440 | tf_op jit(solution)/shard_map/ppermute | solution.py:357
  64.2 12.2 %collective-permute-start.19 = (f32[4,128,256]{2,1,0:T(8,128)S(1)}, f32[4,128,256]{2,1,0:T(8,128)S(1)}, u32[]{:S(2)}, u32[]{:S(2)}) collective-permute-start(f32[4,128,256]{2,1,0:T(8,128)S(1)} %get-tuple-element.32), channel_id=1, source_target_pairs={{0,1},{1,0},{2,3},{3,2},{4,5},{5,4},{6,7},{7,6},{8,9},{9,8},{10,11... | collective-permute-start | bytes 1572872 | tf_op jit(solution)/shard_map/ppermute | solution.py:357
  75.8 2.8 %collective-permute-start.18 = (f32[4,128,256]{2,1,0:T(8,128)S(1)}, f32[4,128,256]{2,1,0:T(8,128)S(1)}, u32[]{:S(2)}, u32[]{:S(2)}) collective-permute-start(f32[4,128,256]{2,1,0:T(8,128)S(1)} %get-tuple-element.30), channel_id=1, source_target_pairs={{0,1},{1,0},{2,3},{3,2},{4,5},{5,4},{6,7},{7,6},{8,9},{9,8},{10,11... | collective-permute-start | bytes 1572872 | tf_op jit(solution)/shard_map/ppermute | solution.py:357
  75.9 7.9 %collective-permute-start.26 = (f32[4,128,256]{2,1,0:T(8,128)S(1)}, f32[4,128,256]{2,1,0:T(8,128)S(1)}, u32[]{:S(2)}, u32[]{:S(2)}) collective-permute-start(f32[4,128,256]{2,1,0:T(8,128)S(1)} %get-tuple-element.36), channel_id=1, source_target_pairs={{0,1},{1,0},{2,3},{3,2},{4,5},{5,4},{6,7},{7,6},{8,9},{9,8},{10,11... | collective-permute-start | bytes 1572872 | tf_op jit(solution)/shard_map/ppermute | solution.py:357
  76.5 6.4 %collective-permute-start.20 = (f32[2,128,256]{2,1,0:T(8,128)S(1)}, f32[2,128,256]{2,1,0:T(8,128)S(1)}, u32[]{:S(2)}, u32[]{:S(2)}) collective-permute-start(f32[2,128,256]{2,1,0:T(8,128)S(1)} %get-tuple-element.41), channel_id=1, source_target_pairs={{0,2},{1,5},{2,0},{3,7},{4,6},{5,1},{6,4},{7,3},{8,10},{9,13},{10,... | collective-permute-start | bytes 786440 | tf_op jit(solution)/shard_map/ppermute | solution.py:357
  76.6 10.1 %collective-permute-start.17 = (f32[2,128,256]{2,1,0:T(8,128)S(1)}, f32[2,128,256]{2,1,0:T(8,128)S(1)}, u32[]{:S(2)}, u32[]{:S(2)}) collective-permute-start(f32[2,128,256]{2,1,0:T(8,128)S(1)} %get-tuple-element.28), channel_id=1, source_target_pairs={{0,1},{1,0},{2,3},{3,2},{4,5},{5,4},{6,7},{7,6},{8,9},{9,8},{10,11... | collective-permute-start | bytes 786440 | tf_op jit(solution)/shard_map/ppermute | solution.py:357
  76.7 9.8 %collective-permute-start.27 = (f32[2,128,256]{2,1,0:T(8,128)S(1)}, f32[2,128,256]{2,1,0:T(8,128)S(1)}, u32[]{:S(2)}, u32[]{:S(2)}) collective-permute-start(f32[2,128,256]{2,1,0:T(8,128)S(1)} %get-tuple-element.42), channel_id=1, source_target_pairs={{0,2},{1,5},{2,0},{3,7},{4,6},{5,1},{6,4},{7,3},{8,10},{9,13},{10,... | collective-permute-start | bytes 786440 | tf_op jit(solution)/shard_map/ppermute | solution.py:357
  83.0 9.2 %collective-permute-start.21 = (f32[2,128,256]{2,1,0:T(8,128)S(1)}, f32[2,128,256]{2,1,0:T(8,128)S(1)}, u32[]{:S(2)}, u32[]{:S(2)}) collective-permute-start(f32[2,128,256]{2,1,0:T(8,128)S(1)} %get-tuple-element.37), channel_id=1, source_target_pairs={{0,4},{1,5},{2,6},{3,7},{4,0},{5,1},{6,2},{7,3},{8,12},{9,13},{10,... | collective-permute-start | bytes 786440 | tf_op jit(solution)/shard_map/ppermute | solution.py:357
  83.1 9.2 %collective-permute-start.22 = (f32[2,128,256]{2,1,0:T(8,128)S(1)}, f32[2,128,256]{2,1,0:T(8,128)S(1)}, u32[]{:S(2)}, u32[]{:S(2)}) collective-permute-start(f32[2,128,256]{2,1,0:T(8,128)S(1)} %get-tuple-element.38), channel_id=1, source_target_pairs={{0,2},{1,3},{2,0},{3,1},{4,6},{5,7},{6,4},{7,5},{8,10},{9,11},{10,... | collective-permute-start | bytes 786440 | tf_op jit(solution)/shard_map/ppermute | solution.py:357
  83.8 11.2 %collective-permute-start.25 = (f32[2,128,256]{2,1,0:T(8,128)S(1)}, f32[2,128,256]{2,1,0:T(8,128)S(1)}, u32[]{:S(2)}, u32[]{:S(2)}) collective-permute-start(f32[2,128,256]{2,1,0:T(8,128)S(1)} %get-tuple-element.34), channel_id=1, source_target_pairs={{0,1},{1,0},{2,3},{3,2},{4,5},{5,4},{6,7},{7,6},{8,9},{9,8},{10,11... | collective-permute-start | bytes 786440 | tf_op jit(solution)/shard_map/ppermute | solution.py:357
  86.6 9.5 %collective-permute-start.28 = (f32[2,128,256]{2,1,0:T(8,128)S(1)}, f32[2,128,256]{2,1,0:T(8,128)S(1)}, u32[]{:S(2)}, u32[]{:S(2)}) collective-permute-start(f32[2,128,256]{2,1,0:T(8,128)S(1)} %get-tuple-element.39), channel_id=1, source_target_pairs={{0,4},{1,5},{2,6},{3,7},{4,0},{5,1},{6,2},{7,3},{8,12},{9,13},{10,... | collective-permute-start | bytes 786440 | tf_op jit(solution)/shard_map/ppermute | solution.py:357
  86.7 10.3 %collective-permute-start.29 = (f32[2,128,256]{2,1,0:T(8,128)S(1)}, f32[2,128,256]{2,1,0:T(8,128)S(1)}, u32[]{:S(2)}, u32[]{:S(2)}) collective-permute-start(f32[2,128,256]{2,1,0:T(8,128)S(1)} %get-tuple-element.40), channel_id=1, source_target_pairs={{0,2},{1,3},{2,0},{3,1},{4,6},{5,7},{6,4},{7,5},{8,10},{9,11},{10,... | collective-permute-start | bytes 786440 | tf_op jit(solution)/shard_map/ppermute | solution.py:357
  92.4 7.0 %collective-permute-start.24 = (f32[128,256]{1,0:T(8,128)S(1)}, f32[128,256]{1,0:T(8,128)S(1)}, u32[]{:S(2)}, u32[]{:S(2)}) collective-permute-start(f32[128,256]{1,0:T(8,128)S(1)} %get-tuple-element.43), channel_id=1, source_target_pairs={{0,24},{1,25},{2,26},{3,27},{4,28},{5,29},{6,30},{7,31},{8,16},{9,... | collective-permute-start | bytes 393224 | tf_op jit(solution)/shard_map/ppermute | solution.py:357
  94.9 10.1 %collective-permute-start.23 = (f32[128,256]{1,0:T(8,128)S(1)}, f32[128,256]{1,0:T(8,128)S(1)}, u32[]{:S(2)}, u32[]{:S(2)}) collective-permute-start(f32[128,256]{1,0:T(8,128)S(1)} %get-tuple-element.44), channel_id=1, source_target_pairs={{0,16},{1,17},{2,18},{3,19},{4,20},{5,21},{6,22},{7,23},{8,24},{9,... | collective-permute-start | bytes 393224 | tf_op jit(solution)/shard_map/ppermute | solution.py:357
  97.1 7.9 %collective-permute-start.30 = (f32[128,256]{1,0:T(8,128)S(1)}, f32[128,256]{1,0:T(8,128)S(1)}, u32[]{:S(2)}, u32[]{:S(2)}) collective-permute-start(f32[128,256]{1,0:T(8,128)S(1)} %slice_bitcast_fusion), channel_id=1, source_target_pairs={{0,8},{1,9},{2,10},{3,11},{4,12},{5,13},{6,14},{7,15},{8,0},{9,1},... | collective-permute-start | bytes 393224 | tf_op jit(solution)/shard_map/ppermute | solution.py:357

commit v5 on v4

--- a/solution.py
+++ b/solution.py
@@ -131,6 +131,7 @@
 
 MIB = 1 << 20
 UNROLL = 4
+LANES = 128
 STAGES = 5
 FIELDS = 8
 LEFT, RIGHT, STACK, PART, ROW_A, PART_A, ROW_B, PART_B = range(FIELDS)
@@ -142,67 +143,93 @@
     return hi, lo
 
 
-def plan_tasks(depth, per_block, aux_count, source, column, row, target, pairs, info, plan):
+def waves_of(chunks):
+    return [0, 2, 4 + 2 * chunks, 2 + 6 * chunks]
+
+
+def plan_tasks(depth, per_block, aux_count, source, column, row, target, pairs, plan):
     tasks = pairs.shape[1]
+    width = plan.shape[1]
     chunks = depth // 2
+    begin = waves_of(chunks)
     tile_me, aux_me = lax.axis_index("tile"), lax.axis_index("aux")
     z_me, x_me, y_me, c_me = tile_me >> 1, tile_me & 1, aux_me >> 1, aux_me & 1
     start = (tile_me * aux_count + aux_me) * tasks
+    where, f32 = jnp.where, jnp.float32
+
+    def own(table):
+        line = table[pl.ds(lax.div(start, LANES), 1), :]
+        return pltpu.roll(line, lax.rem(LANES - lax.rem(start, LANES), LANES), 1)[:, :tasks]
 
     def place(a, b):
-        aux = lax.div(b, per_block)
+        aux = lax.div(b, jnp.full_like(b, per_block))
         side = (((aux >> 1) ^ y_me) << 1) | ((a & 1) ^ x_me)
-        return (aux & 1) ^ c_me, (a >> 1) ^ z_me, side, lax.rem(b, per_block)
+        return (aux & 1) ^ c_me, (a >> 1) ^ z_me, side, b - aux * per_block
 
     def target_of(a, b):
         dc, dz, side, part = place(a, b)
         turn = (chunks - 1 - (dz >> 1)) * 2
-        straight = jnp.where(side == 0, 3 * depth, 0) + turn + (dz & 1)
+        straight = where(side == 0, 3 * depth, 0) + turn + (dz & 1)
         sideways = depth + turn * 2 + (side - 1) * 2 + (dz & 1)
-        at = jnp.where((side == 1) | (side == 2), sideways, straight)
-        return side == 3, dc * 4 * depth + at, part
-
-    def read(q, carry):
-        at = start + q
-        dc, dz, side, part = place(source[0, at], column[0, at])
-        one = lambda test: jnp.where(test, 1, 0)
-        corner_a, row_a, part_a = target_of(row[0, at], target[0, at])
-        corner_b, row_b, part_b = target_of(target[0, at], row[0, at])
-        stack = ((dc * chunks + (dz >> 1)) * 4 + side) * 2 + (dz & 1)
-        for f, value in enumerate((pairs[0, q], pairs[1, q], stack, part, row_a, part_a, row_b, part_b)):
-            info[f, q] = value
-        info[FIELDS, q] = one(side > 0) + one(side == 3) + one(dz > 1)
-        info[FIELDS + 1, q] = one(corner_a | corner_b)
-        return carry
-
-    lax.fori_loop(0, tasks, read, 0)
-    for s in range(STAGES):
-        plan[s, 0] = 0
-    for urgent in (1, 0):
-        def put(q, carry, urgent=urgent):
-            @pl.when(info[FIELDS + 1, q] == urgent)
-            def _():
-                wave = info[FIELDS, q]
-                late = jnp.maximum(wave, 2) if urgent else 4
-                stage = jnp.where((wave <= 1) & (plan[1, 0] < tasks * 3 // 8), 1, late)
-                stage = jnp.where((wave == 0) & (plan[0, 0] < tasks // 4), 0, stage)
-                n = plan[stage, 0]
-                plan[stage, 0] = n + 1
-                for f in range(FIELDS):
-                    plan[stage, (n + 1) * FIELDS + f] = info[f, q]
-
-            return carry
-
-        lax.fori_loop(0, tasks, put, 0)
+        at = where((side == 1) | (side == 2), sideways, straight)
+        return where(side == 3, 1, 0), dc * 4 * depth + at, part
+
+    dc, dz, side, part = place(own(source), own(column))
+    far = dz >> 1
+    near_at = where(side == 0, begin[0], where(side == 3, begin[2], 2 * side))
+    far_at = where(side == 0, begin[1] + 2 + 2 * far, where(side == 3, begin[3] - 2 + 2 * far, begin[2] - 4 + 4 * far + 2 * side))
+    stack = dc * 4 * depth + where(far == 0, near_at, far_at) + (dz & 1)
+    wave = where(side > 0, 1, 0) + where(side == 3, 1, 0) + where(far > 0, 1, 0)
+    a, b = own(row), own(target)
+    corner_a, row_a, part_a = target_of(a, b)
+    corner_b, row_b, part_b = target_of(b, a)
+    urgent = corner_a | corner_b
+
+    above = lax.broadcasted_iota(jnp.int32, (tasks, tasks), 0)
+    along = lax.broadcasted_iota(jnp.int32, (tasks, tasks), 1)
+
+    def upright(line):
+        return jnp.sum(where(above == along, line.astype(f32), 0.0), axis=1, keepdims=True)
+
+    place_in = lax.broadcasted_iota(jnp.int32, (1, tasks), 1)
+    key = (place_in + (1 - urgent) * tasks).astype(f32)
+    before = where(upright(key) < key, 1.0, 0.0)
+
+    def rank(which):
+        return jnp.sum(before * upright(which), axis=0, keepdims=True)
+
+    first = where(wave == 0, 1, 0)
+    first = where(rank(first) < tasks // 4, first, 0)
+    second = where(wave <= 1, 1 - first, 0)
+    second = where(rank(second) < tasks * 3 // 8, second, 0)
+    late = where(urgent > 0, jnp.maximum(wave, 2), 4)
+    stage = where(first > 0, 0, where(second > 0, 1, late))
+    stage_up = upright(stage)
+    earlier = where(above < along, 1.0, 0.0)
+    turn = jnp.sum(where(stage_up == stage.astype(f32), earlier, 0.0), axis=0, keepdims=True)
+    slot_up = upright(stage.astype(f32) * tasks + turn)
+    slots = lax.broadcasted_iota(jnp.int32, (tasks, width), 1)
+    slots = slots.astype(f32)
+    chosen = where(slot_up == slots, 1.0, 0.0).astype(jnp.bfloat16)
+    values = jnp.zeros((FIELDS, tasks), jnp.int32)
+    lines = lax.broadcasted_iota(jnp.int32, (FIELDS, tasks), 0)
+    for f, value in enumerate((pairs[0:1, :], pairs[1:2, :], stack, part, row_a, part_a, row_b, part_b)):
+        values = where(lines == f, value, values)
+    listed = jnp.dot(values.astype(f32).astype(jnp.bfloat16), chosen, preferred_element_type=f32)
+    plan[:FIELDS, :] = listed.astype(jnp.int32)
+    lowest = stage_up * tasks
+    inside = where(lowest <= slots, 1.0, 0.0) * where(slots < lowest + tasks, 1.0, 0.0)
+    counts = jnp.sum(inside, axis=0, keepdims=True)
+    plan[FIELDS:, :] = jnp.broadcast_to(counts, (FIELDS, width)).astype(jnp.int32)
 
 
 def prepare_kernel(depth, per_block, aux_count, *refs):
-    f_hbm, plan, o_ref, buf, info, sem = refs[5:]
+    f_hbm, plan, o_ref, buf, sem = refs[5:]
     slots, rows, w = f_hbm.shape
     copies = [pltpu.make_async_copy(f_hbm.at[s], buf.at[s], sem.at[s]) for s in range(slots)]
     for copy in copies:
         copy.start()
-    plan_tasks(depth, per_block, aux_count, *refs[:5], info, plan)
+    plan_tasks(depth, per_block, aux_count, *refs[:5], plan)
     step = 256
     for s, copy in enumerate(copies):
         copy.wait()
@@ -219,24 +246,25 @@
     s, p, w, _ = factors.shape
     rows = p * w
     tasks = pairs.shape[0]
-    smem = pl.BlockSpec(memory_space=pltpu.SMEM)
+    vmem = pl.BlockSpec(memory_space=pltpu.VMEM)
+    width = -(-STAGES * tasks // LANES) * LANES
     return pl.pallas_call(
         functools.partial(prepare_kernel, depth, per_block, aux_count),
-        in_specs=[smem] * 5 + [pl.BlockSpec(memory_space=pltpu.HBM)],
-        out_specs=[smem, pl.BlockSpec(memory_space=pltpu.VMEM)],
+        in_specs=[vmem] * 5 + [pl.BlockSpec(memory_space=pltpu.HBM)],
+        out_specs=[vmem, vmem],
         out_shape=[
-            jax.ShapeDtypeStruct((STAGES, (tasks + 1) * FIELDS), jnp.int32),
+            jax.ShapeDtypeStruct((2 * FIELDS, width), jnp.int32),
             jax.ShapeDtypeStruct((s, rows, 2 * w), jnp.bfloat16),
         ],
         scratch_shapes=[
             pltpu.VMEM((s, rows, w), jnp.float32),
-            pltpu.SMEM((FIELDS + 2, tasks), jnp.int32),
             pltpu.SemaphoreType.DMA((s,)),
         ],
         compiler_params=pltpu.CompilerParams(vmem_limit_bytes=8 * MIB),
         cost_estimate=pl.CostEstimate(flops=2 * factors.size, bytes_accessed=8 * factors.size, transcendentals=0),
     )(
-        *(pltpu.with_memory_space_constraint(table.T, pltpu.HBM) for table in (*tables, pairs)),
+        *(pltpu.with_memory_space_constraint(table.reshape(-1, LANES), pltpu.HBM) for table in tables),
+        pltpu.with_memory_space_constraint(pairs.T, pltpu.HBM),
         pltpu.with_memory_space_constraint(factors.reshape(s, rows, w), pltpu.HBM),
     )
 
@@ -256,10 +284,11 @@
     pairs = f2.shape[1] // (2 * w)
     f32 = jnp.float32
 
-    count = plan[stage, 0]
+    tasks = tiles.shape[0]
+    count = plan[FIELDS, stage * tasks]
 
     def field(i, f):
-        return plan[stage, (i + 1) * FIELDS + f]
+        return plan[f, stage * tasks + i]
 
     def fetch(i, carry):
         shard, part = field(i, STACK), pl.multiple_of(field(i, PART) * w, w)
@@ -322,8 +351,7 @@
         out[...] = sums[start : start + size]
 
 
-def run_stage(plan, stage, f2, stacks, firsts, sums, shape, cuts, keep):
-    tasks = plan.shape[1] // FIELDS - 1
+def run_stage(plan, tasks, stage, f2, stacks, firsts, sums, shape, cuts, keep):
     w = f2.shape[2] // 2
     first = sums is None
     vmem = pl.BlockSpec(memory_space=pltpu.VMEM)
@@ -392,6 +420,7 @@
     tile_me = lax.axis_index("tile")
     aux_me = lax.axis_index("aux")
     tile_width = factors.shape[-1]
+    task_count = slot_pairs.shape[0]
     per_block = tiles_all // aux_count
     depth = tiles_all // 2
     chunks = depth // 2
@@ -404,7 +433,8 @@
     column = [density] + [move(density, across_z(step)) for step in range(1, depth)]
     tables = (density_source, density_column, target_row, target_column)
     plan, split_factors = prepare(depth, per_block, aux_count, tables, slot_pairs, factors)
-    by_stage = [([], []) for _ in range(4)]
+    begin = waves_of(chunks)
+    waves = [[], [], [], []]
     for k in range(chunks):
         here = jnp.stack(column[2 * k : 2 * k + 2])
         if k == 0:
@@ -412,12 +442,14 @@
         side_x = move(here, across_x)
         side_y = move(here, across_y)
         corner = move(jnp.where(on_first, side_x, side_y), across_diagonal)
-        for side, value in enumerate((here, side_x, side_y, corner)):
-            stage = min(side, 1) + (side == 3) + (k > 0)
-            first = (k * 4 + side) * 2
-            for at, stack in ((first, value), (first + 4 * depth, move(value, across_core))):
-                by_stage[stage][0].append(stack)
-                by_stage[stage][1].append(at)
+        first = int(k > 0)
+        waves[first].append(here)
+        waves[first + 1].extend((side_x, side_y))
+        waves[first + 2].append(corner)
+    by_stage = []
+    for stage, parts in enumerate(waves):
+        wave = jnp.concatenate(parts) if len(parts) > 1 else parts[0]
+        by_stage.append(([wave, move(wave, across_core)], [begin[stage], begin[stage] + 4 * depth]))
 
     for known in range(2):
         by_stage[1][known].extend(by_stage[0][known])
@@ -430,7 +462,7 @@
     sums = None
     for stage, (values, firsts) in enumerate(by_stage):
         cut = {3: corner_cuts, 4: cuts}.get(stage, ())
-        results = run_stage(plan, stage, split_factors, values, firsts, sums, shape, cut, stage < 4)
+        results = run_stage(plan, task_count, stage, split_factors, values, firsts, sums, shape, cut, stage < 4)
         sums = results[0]
         if stage == 3:
             corner_mine, corner_other = results[1:]
@@ -463,7 +495,7 @@
     tiles_all = lax.axis_size("tile")
     aux_count = lax.axis_size("aux")
     whole = density.size * density.dtype.itemsize * tiles_all * aux_count
-    cube = aux_count == 4 and tiles_all >= aux_count and tiles_all & (tiles_all - 1) == 0
+    cube = aux_count == 4 and LANES % rest[2].shape[0] == 0 and tiles_all >= aux_count and tiles_all & (tiles_all - 1) == 0
     if cube and whole <= GATHER_LIMIT:
         return gathered(density, *rest)
     return routed(density, *rest)

time: 107 us -> 98.1 us (0.917)
  waiting for transfers between devices: 39 us -> 31 us
  Pallas kernels: 39.5 us -> 34.8 us
  starting transfers between devices: 25.6 us -> 29.8 us
    ppermute x31 -> x27, waiting for transfers between devices: 39 us -> 31 us  [shift(): return lax.ppermute(value, AXES, pairs)]
    ppermute x31 -> x27, starting transfers between devices: 25.6 us -> 29.8 us  [shift(): return lax.ppermute(value, AXES, pairs)]
    pallas_call x1, Pallas kernels: 7.67 us -> 3.79 us  [prepare(): pl.pallas_call(functools.partial(prepare_kernel, depth, per_block, aux_co...]
  transfers between devices with their start and end apart: 31 -> 27, of which waited for: 12 -> 14; matrix products, arithmetic and copies ran while one was open for 1% -> 1% of each run, Pallas kernels for 34% -> 32%
where the time goes in v5:
time: 98.1 us; the launch traced here: 98 us
  Pallas kernels  34.8 us (35%)
  waiting for transfers between devices  31 us (32%)
  starting transfers between devices  29.8 us (30%)
    ppermute x27, waiting for transfers between devices, shift(): return lax.ppermute(value, AXES, pairs)  31 us
    pallas_call x5, Pallas kernels, run_stage(): pl.pallas_call(body, in_specs=[pl.BlockSpec(memory_space=pltpu.SMEM)] + [...  31 us
    ppermute x27, starting transfers between devices, shift(): return lax.ppermute(value, AXES, pairs)  29.8 us
    pallas_call x1, Pallas kernels, prepare(): pl.pallas_call(functools.partial(prepare_kernel, depth, per_block, aux_co...  3.79 us
  transfers between devices with their start and end apart: 27, of which 14 were waited for; matrix products, arithmetic and copies ran while one was open for 1% of the time, Pallas kernels for 32%

profile of v5, /device:TPU:0, one launch (start us, length us, event | category | flops | bytes accessed | tf_op | source)
XLA Modules:
  0.0 98.0 jit_solution(17978561192192385316)
XLA Ops:
  0.0 3.1 %collective-permute-start = (f32[128,256]{1,0:T(8,128)}, f32[128,256]{1,0:T(8,128)S(1)}, u32[]{:S(2)}, u32[]{:S(2)}) collective-permute-start(f32[128,256]{1,0:T(8,128)} %param.8), channel_id=1, source_target_pairs={{0,8},{1,9},{2,10},{3,11},{4,12},{5,13},{6,14},{7,15},{8,0},{9,1},... | collective-permute-start | bytes 393224 | tf_op jit(solution)/shard_map/ppermute | solution.py:385
  3.1 3.8 %shard_map.82 = (s32[16,256]{1,0:T(8,128)S(1)}, bf16[6,2048,256]{2,1,0:T(8,128)(2,1)S(1)}) custom-call(s32[8,128]{1,0:T(8,128)} %bitcast.53, s32[8,128]{1,0:T(8,128)} %bitcast.54, s32[8,128]{1,0:T(8,128)} %bitcast.55, s32[8,128]{1,0:T(8,128)} %bitcast.56, s32[2,32]{1,0:T(2,128)} %bitcast.57, f32[6,2048,128]{2,1,0:T(8,128)} %bitcast.45), custom_call_target="tpu_custom_call" | custom-call | flops 3145728 | bytes 12582912 | tf_op jit(solution)/shard_map/pallas_call | solution.py:251
  6.9 0.0 collective-permute-done
  6.9 1.6 %collective-permute-start.3 = (f32[2,128,256]{2,1,0:T(8,128)S(1)}, f32[2,128,256]{2,1,0:T(8,128)S(1)}, u32[]{:S(2)}, u32[]{:S(2)}) collective-permute-start(f32[2,128,256]{2,1,0:T(8,128)S(1)} %pad_maximum_fusion.1.refs_1_.refs_4_.refs_6_), channel_id=1, source_target_pairs={{0,2},{1,3},{2,0},{3,1},{4,6},{5,7},{6,4},{7,5},{8,10},{9,11},{10,... | collective-permute-start | bytes 786440 | tf_op jit(solution)/shard_map/ppermute | solution.py:385
  8.5 1.5 %collective-permute-start.2 = (f32[2,128,256]{2,1,0:T(8,128)S(1)}, f32[2,128,256]{2,1,0:T(8,128)S(1)}, u32[]{:S(2)}, u32[]{:S(2)}) collective-permute-start(f32[2,128,256]{2,1,0:T(8,128)S(1)} %pad_maximum_fusion.1.refs_1_.refs_4_.refs_6_), channel_id=1, source_target_pairs={{0,4},{1,5},{2,6},{3,7},{4,0},{5,1},{6,2},{7,3},{8,12},{9,13},{10,... | collective-permute-start | bytes 786440 | tf_op jit(solution)/shard_map/ppermute | solution.py:385
  10.0 3.6 %collective-permute-start.5 = (f32[128,256]{1,0:T(8,128)S(1)}, f32[128,256]{1,0:T(8,128)S(1)}, u32[]{:S(2)}, u32[]{:S(2)}) collective-permute-start(f32[128,256]{1,0:T(8,128)S(1)} %copy-done.1), channel_id=1, source_target_pairs={{0,24},{1,25},{2,26},{3,27},{4,28},{5,29},{6,30},{7,31},{8,16},{9,... | collective-permute-start | bytes 393224 | tf_op jit(solution)/shard_map/ppermute | solution.py:385
  13.6 1.1 %collective-permute-done.3 = f32[2,128,256]{2,1,0:T(8,128)S(1)} collective-permute-done((f32[2,128,256]{2,1,0:T(8,128)S(1)}, f32[2,128,256]{2,1,0:T(8,128)S(1)}, u32[]{:S(2)}, u32[]{:S(2)}) %collective-permute-start.3) | collective-permute-done | bytes 262176 | tf_op jit(solution)/shard_map/ppermute | solution.py:385
  14.7 1.2 %collective-permute-done.2 = f32[2,128,256]{2,1,0:T(8,128)S(1)} collective-permute-done((f32[2,128,256]{2,1,0:T(8,128)S(1)}, f32[2,128,256]{2,1,0:T(8,128)S(1)}, u32[]{:S(2)}, u32[]{:S(2)}) %collective-permute-start.2) | collective-permute-done | bytes 262176 | tf_op jit(solution)/shard_map/ppermute | solution.py:385
  16.0 0.6 collective-permute-start.7
  16.6 1.1 %collective-permute-done.5 = f32[128,256]{1,0:T(8,128)S(1)} collective-permute-done((f32[128,256]{1,0:T(8,128)S(1)}, f32[128,256]{1,0:T(8,128)S(1)}, u32[]{:S(2)}, u32[]{:S(2)}) %collective-permute-start.5) | collective-permute-done | bytes 131104 | tf_op jit(solution)/shard_map/ppermute | solution.py:385
  17.7 6.0 %collective-permute-done.4 = f32[128,256]{1,0:T(8,128)S(1)} collective-permute-done((f32[128,256]{1,0:T(8,128)S(1)}, f32[128,256]{1,0:T(8,128)S(1)}, u32[]{:S(2)}, u32[]{:S(2)}) %collective-permute-start.4) | collective-permute-done | bytes 131104 | tf_op jit(solution)/shard_map/ppermute | solution.py:385
  23.7 0.6 collective-permute-start.8
  24.3 0.5 collective-permute-start.9
  24.8 0.0 collective-permute-start.1
  24.8 0.1 pad_maximum_fusion.refs_2_.refs_4_
  24.9 0.6 collective-permute-start.6
  25.5 5.5 %collective-permute-done.8 = f32[2,128,256]{2,1,0:T(8,128)S(1)} collective-permute-done((f32[2,128,256]{2,1,0:T(8,128)S(1)}, f32[2,128,256]{2,1,0:T(8,128)S(1)}, u32[]{:S(2)}, u32[]{:S(2)}) %collective-permute-start.8) | collective-permute-done | bytes 262176 | tf_op jit(solution)/shard_map/ppermute | solution.py:385
  31.0 0.2 collective-permute-done.9
  31.3 0.6 collective-permute-start.11
  31.9 0.0 collective-permute-start.10
  31.9 0.0 collective-permute-done.1.refs_2_.refs_5_.refs_7_
  31.9 4.1 %shard_map.83.refs_1_ = f32[32,128,256]{2,1,0:T(8,128)S(1)} custom-call(s32[16,256]{1,0:T(8,128)S(1)} %get-tuple-element.21.plan, bf16[6,2048,256]{2,1,0:T(8,128)(2,1)S(1)} %get-tuple-element.23.refs_0_, f32[2,128,256]{2,1,0:T(8,128)S(1)} %pad_maximum_fusion.1.refs_1_.refs_4_.refs_6_, f32[2,128,256]{2,1,0:T(8,128)S(1)} %collective-permute-done.1.refs_2_.refs_5_.refs_7_), custom_call_target="tpu_custom_call" | custom-call | flops 4294967296 | bytes 6291456 | tf_op jit(solution)/shard_map/pallas_call | solution.py:361
  36.0 1.7 %collective-permute-done.11.refs_2_.refs_8_ = f32[2,128,256]{2,1,0:T(8,128)S(1)} collective-permute-done((f32[2,128,256]{2,1,0:T(8,128)S(1)}, f32[2,128,256]{2,1,0:T(8,128)S(1)}, u32[]{:S(2)}, u32[]{:S(2)}) %collective-permute-start.11) | collective-permute-done | bytes 262176 | tf_op jit(solution)/shard_map/ppermute | solution.py:385
  37.7 0.4 collective-permute-start.12
  38.2 0.0 collective-permute-done.6.refs_3_.refs_5_
  38.2 9.8 %shard_map.84.refs_1_ = f32[32,128,256]{2,1,0:T(8,128)S(1)} custom-call(s32[16,256]{1,0:T(8,128)S(1)} %get-tuple-element.21.plan, bf16[6,2048,256]{2,1,0:T(8,128)(2,1)S(1)} %get-tuple-element.23.refs_0_, f32[32,128,256]{2,1,0:T(8,128)S(1)} %shard_map.83.refs_1_, f32[6,128,256]{2,1,0:T(8,128)S(1)} %pad_maximum_fusion.refs_2_.refs_4_, ...), custom_call_target="tpu_custom_call" | custom-call | flops 4294967296 | bytes 6291456 | tf_op jit(solution)/shard_map/pallas_call | solution.py:361
  48.0 0.0 collective-permute-done.10.refs_3_
  48.0 5.4 %shard_map.85.refs_1_ = f32[32,128,256]{2,1,0:T(8,128)S(1)} custom-call(s32[16,256]{1,0:T(8,128)S(1)} %get-tuple-element.21.plan, bf16[6,2048,256]{2,1,0:T(8,128)(2,1)S(1)} %get-tuple-element.23.refs_0_, f32[32,128,256]{2,1,0:T(8,128)S(1)} %shard_map.84.refs_1_, f32[6,128,256]{2,1,0:T(8,128)S(1)} %get-tuple-element.46.refs_2_, ...), custom_call_target="tpu_custom_call" | custom-call | flops 4294967296 | bytes 6291456 | tf_op jit(solution)/shard_map/pallas_call | solution.py:361
  53.4 3.0 %shard_map.86 = (f32[32,128,256]{2,1,0:T(8,128)S(1)}, f32[4,128,256]{2,1,0:T(8,128)S(1)}, f32[4,128,256]{2,1,0:T(8,128)S(1)}) custom-call(s32[16,256]{1,0:T(8,128)S(1)} %get-tuple-element.21.plan, bf16[6,2048,256]{2,1,0:T(8,128)(2,1)S(1)} %get-tuple-element.23.refs_0_, f32[32,128,256]{2,1,0:T(8,128)S(1)} %shard_map.85.refs_1_, ...), custom_call_target="tpu_custom_call" | custom-call | flops 4294967296 | bytes 6291456 | tf_op jit(solution)/shard_map/pallas_call | solution.py:361
  56.5 2.2 %collective-permute-start.15 = (f32[4,128,256]{2,1,0:T(8,128)S(1)}, f32[4,128,256]{2,1,0:T(8,128)S(1)}, u32[]{:S(2)}, u32[]{:S(2)}) collective-permute-start(f32[4,128,256]{2,1,0:T(8,128)S(1)} %get-tuple-element.32), channel_id=1, source_target_pairs={{0,1},{1,0},{2,3},{3,2},{4,5},{5,4},{6,7},{7,6},{8,9},{9,8},{10,11... | collective-permute-start | bytes 1572872 | tf_op jit(solution)/shard_map/ppermute | solution.py:385
  58.6 8.6 %shard_map.87 = (f32[4,128,256]{2,1,0:T(8,128)S(1)}, f32[4,128,256]{2,1,0:T(8,128)S(1)}, f32[2,128,256]{2,1,0:T(8,128)S(1)}, f32[2,128,256]{2,1,0:T(8,128)S(1)},...) custom-call(s32[16,256]{1,0:T(8,128)S(1)} %get-tuple-element.21.plan, ...), custom_call_target="tpu_custom_call" | custom-call | flops 4294967296 | bytes 6291456 | tf_op jit(solution)/shard_map/pallas_call | solution.py:361
  67.3 0.1 collective-permute-start.14
  67.3 0.5 collective-permute-start.22
  67.8 0.0 collective-permute-done.15
  67.9 0.1 add.58
  68.0 0.9 collective-permute-start.16
  68.9 0.0 collective-permute-start.13
  68.9 2.2 %collective-permute-start.23 = (f32[2,128,256]{2,1,0:T(8,128)S(1)}, f32[2,128,256]{2,1,0:T(8,128)S(1)}, u32[]{:S(2)}, u32[]{:S(2)}) collective-permute-start(f32[2,128,256]{2,1,0:T(8,128)S(1)} %get-tuple-element.42), channel_id=1, source_target_pairs={{0,2},{1,5},{2,0},{3,7},{4,6},{5,1},{6,4},{7,3},{8,10},{9,13},{10,... | collective-permute-start | bytes 786440 | tf_op jit(solution)/shard_map/ppermute | solution.py:385
  71.1 0.1 add.57
  71.2 3.2 %collective-permute-done.16 = f32[2,128,256]{2,1,0:T(8,128)S(1)} collective-permute-done((f32[2,128,256]{2,1,0:T(8,128)S(1)}, f32[2,128,256]{2,1,0:T(8,128)S(1)}, u32[]{:S(2)}, u32[]{:S(2)}) %collective-permute-start.16) | collective-permute-done | bytes 262176 | tf_op jit(solution)/shard_map/ppermute | solution.py:385
  74.4 0.1 slice_add_fusion.3
  74.5 1.3 %collective-permute-start.17 = (f32[2,128,256]{2,1,0:T(8,128)S(1)}, f32[2,128,256]{2,1,0:T(8,128)S(1)}, u32[]{:S(2)}, u32[]{:S(2)}) collective-permute-start(f32[2,128,256]{2,1,0:T(8,128)S(1)} %get-tuple-element.37), channel_id=1, source_target_pairs={{0,4},{1,5},{2,6},{3,7},{4,0},{5,1},{6,2},{7,3},{8,12},{9,13},{10,... | collective-permute-start | bytes 786440 | tf_op jit(solution)/shard_map/ppermute | solution.py:385
  75.8 2.0 %collective-permute-start.18 = (f32[2,128,256]{2,1,0:T(8,128)S(1)}, f32[2,128,256]{2,1,0:T(8,128)S(1)}, u32[]{:S(2)}, u32[]{:S(2)}) collective-permute-start(f32[2,128,256]{2,1,0:T(8,128)S(1)} %get-tuple-element.38), channel_id=1, source_target_pairs={{0,2},{1,3},{2,0},{3,1},{4,6},{5,7},{6,4},{7,5},{8,10},{9,11},{10,... | collective-permute-start | bytes 786440 | tf_op jit(solution)/shard_map/ppermute | solution.py:385
  77.8 0.0 collective-permute-done.22
  77.8 0.0 collective-permute-start.21
  77.8 0.1 add.65
  77.9 0.0 collective-permute-done.23
  77.9 0.1 slice_add_fusion.1
  77.9 1.0 %collective-permute-start.24 = (f32[2,128,256]{2,1,0:T(8,128)S(1)}, f32[2,128,256]{2,1,0:T(8,128)S(1)}, u32[]{:S(2)}, u32[]{:S(2)}) collective-permute-start(f32[2,128,256]{2,1,0:T(8,128)S(1)} %get-tuple-element.39), channel_id=1, source_target_pairs={{0,4},{1,5},{2,6},{3,7},{4,0},{5,1},{6,2},{7,3},{8,12},{9,13},{10,... | collective-permute-start | bytes 786440 | tf_op jit(solution)/shard_map/ppermute | solution.py:385
  78.9 2.5 %collective-permute-start.25 = (f32[2,128,256]{2,1,0:T(8,128)S(1)}, f32[2,128,256]{2,1,0:T(8,128)S(1)}, u32[]{:S(2)}, u32[]{:S(2)}) collective-permute-start(f32[2,128,256]{2,1,0:T(8,128)S(1)} %get-tuple-element.40), channel_id=1, source_target_pairs={{0,2},{1,3},{2,0},{3,1},{4,6},{5,7},{6,4},{7,5},{8,10},{9,11},{10,... | collective-permute-start | bytes 786440 | tf_op jit(solution)/shard_map/ppermute | solution.py:385
  81.4 1.4 %collective-permute-done.17 = f32[2,128,256]{2,1,0:T(8,128)S(1)} collective-permute-done((f32[2,128,256]{2,1,0:T(8,128)S(1)}, f32[2,128,256]{2,1,0:T(8,128)S(1)}, u32[]{:S(2)}, u32[]{:S(2)}) %collective-permute-start.17) | collective-permute-done | bytes 262176 | tf_op jit(solution)/shard_map/ppermute | solution.py:385
  82.8 2.1 %collective-permute-done.18 = f32[2,128,256]{2,1,0:T(8,128)S(1)} collective-permute-done((f32[2,128,256]{2,1,0:T(8,128)S(1)}, f32[2,128,256]{2,1,0:T(8,128)S(1)}, u32[]{:S(2)}, u32[]{:S(2)}) %collective-permute-start.18) | collective-permute-done | bytes 262176 | tf_op jit(solution)/shard_map/ppermute | solution.py:385
  84.9 0.1 add_add_fusion.1
  85.0 2.4 %collective-permute-start.20 = (f32[128,256]{1,0:T(8,128)S(1)}, f32[128,256]{1,0:T(8,128)S(1)}, u32[]{:S(2)}, u32[]{:S(2)}) collective-permute-start(f32[128,256]{1,0:T(8,128)S(1)} %get-tuple-element.43), channel_id=1, source_target_pairs={{0,24},{1,25},{2,26},{3,27},{4,28},{5,29},{6,30},{7,31},{8,16},{9,... | collective-permute-start | bytes 393224 | tf_op jit(solution)/shard_map/ppermute | solution.py:385
  87.4 0.6 collective-permute-start.19
  88.0 0.8 collective-permute-done.25
  88.8 0.1 add_add_fusion
  88.9 1.2 %collective-permute-start.26 = (f32[128,256]{1,0:T(8,128)S(1)}, f32[128,256]{1,0:T(8,128)S(1)}, u32[]{:S(2)}, u32[]{:S(2)}) collective-permute-start(f32[128,256]{1,0:T(8,128)S(1)} %slice_bitcast_fusion), channel_id=1, source_target_pairs={{0,8},{1,9},{2,10},{3,11},{4,12},{5,13},{6,14},{7,15},{8,0},{9,1},... | collective-permute-start | bytes 393224 | tf_op jit(solution)/shard_map/ppermute | solution.py:385
  90.1 1.9 %collective-permute-done.20 = f32[128,256]{1,0:T(8,128)S(1)} collective-permute-done((f32[128,256]{1,0:T(8,128)S(1)}, f32[128,256]{1,0:T(8,128)S(1)}, u32[]{:S(2)}, u32[]{:S(2)}) %collective-permute-start.20) | collective-permute-done | bytes 131104 | tf_op jit(solution)/shard_map/ppermute | solution.py:385
  92.0 4.3 %collective-permute-done.19 = f32[128,256]{1,0:T(8,128)S(1)} collective-permute-done((f32[128,256]{1,0:T(8,128)S(1)}, f32[128,256]{1,0:T(8,128)S(1)}, u32[]{:S(2)}, u32[]{:S(2)}) %collective-permute-start.19) | collective-permute-done | bytes 131104 | tf_op jit(solution)/shard_map/ppermute | solution.py:385
  96.3 0.2 collective-permute-done.26
  96.5 0.3 fusion
  96.8 0.4 fusion.6
  97.2 0.8 copy.11
  (20 shorter events, 0.2 us)
Async XLA Ops:
  0.0 96.5 %copy-start = (f32[1024,128]{1,0:T(8,128)S(1)}, f32[1024,128]{1,0:T(8,128)}, u32[]{:S(2)}) copy-start(f32[1024,128]{1,0:T(8,128)} %param.10) | copy-start | bytes 1572868
  0.0 6.9 %copy-start.1 = (f32[128,256]{1,0:T(8,128)S(1)}, f32[128,256]{1,0:T(8,128)}, u32[]{:S(2)}) copy-start(f32[128,256]{1,0:T(8,128)} %param.8) | copy-start | bytes 393220
  0.0 6.9 %collective-permute-start = (f32[128,256]{1,0:T(8,128)}, f32[128,256]{1,0:T(8,128)S(1)}, u32[]{:S(2)}, u32[]{:S(2)}) collective-permute-start(f32[128,256]{1,0:T(8,128)} %param.8), channel_id=1, source_target_pairs={{0,8},{1,9},{2,10},{3,11},{4,12},{5,13},{6,14},{7,15},{8,0},{9,1},... | collective-permute-start | bytes 393224 | tf_op jit(solution)/shard_map/ppermute | solution.py:385
  6.9 7.8 %collective-permute-start.3 = (f32[2,128,256]{2,1,0:T(8,128)S(1)}, f32[2,128,256]{2,1,0:T(8,128)S(1)}, u32[]{:S(2)}, u32[]{:S(2)}) collective-permute-start(f32[2,128,256]{2,1,0:T(8,128)S(1)} %pad_maximum_fusion.1.refs_1_.refs_4_.refs_6_), channel_id=1, source_target_pairs={{0,2},{1,3},{2,0},{3,1},{4,6},{5,7},{6,4},{7,5},{8,10},{9,11},{10,... | collective-permute-start | bytes 786440 | tf_op jit(solution)/shard_map/ppermute | solution.py:385
  8.5 7.4 %collective-permute-start.2 = (f32[2,128,256]{2,1,0:T(8,128)S(1)}, f32[2,128,256]{2,1,0:T(8,128)S(1)}, u32[]{:S(2)}, u32[]{:S(2)}) collective-permute-start(f32[2,128,256]{2,1,0:T(8,128)S(1)} %pad_maximum_fusion.1.refs_1_.refs_4_.refs_6_), channel_id=1, source_target_pairs={{0,4},{1,5},{2,6},{3,7},{4,0},{5,1},{6,2},{7,3},{8,12},{9,13},{10,... | collective-permute-start | bytes 786440 | tf_op jit(solution)/shard_map/ppermute | solution.py:385
  10.0 7.6 %collective-permute-start.5 = (f32[128,256]{1,0:T(8,128)S(1)}, f32[128,256]{1,0:T(8,128)S(1)}, u32[]{:S(2)}, u32[]{:S(2)}) collective-permute-start(f32[128,256]{1,0:T(8,128)S(1)} %copy-done.1), channel_id=1, source_target_pairs={{0,24},{1,25},{2,26},{3,27},{4,28},{5,29},{6,30},{7,31},{8,16},{9,... | collective-permute-start | bytes 393224 | tf_op jit(solution)/shard_map/ppermute | solution.py:385
  13.6 10.0 %collective-permute-start.4 = (f32[128,256]{1,0:T(8,128)S(1)}, f32[128,256]{1,0:T(8,128)S(1)}, u32[]{:S(2)}, u32[]{:S(2)}) collective-permute-start(f32[128,256]{1,0:T(8,128)S(1)} %copy-done.1), channel_id=1, source_target_pairs={{0,16},{1,17},{2,18},{3,19},{4,20},{5,21},{6,22},{7,23},{8,24},{9,... | collective-permute-start | bytes 393224 | tf_op jit(solution)/shard_map/ppermute | solution.py:385
  16.0 9.4 %collective-permute-start.7 = (f32[2,128,256]{2,1,0:T(8,128)S(1)}, f32[2,128,256]{2,1,0:T(8,128)S(1)}, u32[]{:S(2)}, u32[]{:S(2)}) collective-permute-start(f32[2,128,256]{2,1,0:T(8,128)S(1)} %broadcast_select_fusion.1), channel_id=1, source_target_pairs={{0,2},{1,5},{2,0},{3,7},{4,6},{5,1},{6,4},{7,3},{8,10},{9,13},{10,... | collective-permute-start | bytes 786440 | tf_op jit(solution)/shard_map/ppermute | solution.py:385
  23.7 7.3 %collective-permute-start.8 = (f32[2,128,256]{2,1,0:T(8,128)S(1)}, f32[2,128,256]{2,1,0:T(8,128)S(1)}, u32[]{:S(2)}, u32[]{:S(2)}) collective-permute-start(f32[2,128,256]{2,1,0:T(8,128)S(1)} %pad_maximum_fusion.2), channel_id=1, source_target_pairs={{0,4},{1,5},{2,6},{3,7},{4,0},{5,1},{6,2},{7,3},{8,12},{9,13},{10,... | collective-permute-start | bytes 786440 | tf_op jit(solution)/shard_map/ppermute | solution.py:385
  24.3 7.0 %collective-permute-start.9 = (f32[2,128,256]{2,1,0:T(8,128)S(1)}, f32[2,128,256]{2,1,0:T(8,128)S(1)}, u32[]{:S(2)}, u32[]{:S(2)}) collective-permute-start(f32[2,128,256]{2,1,0:T(8,128)S(1)} %pad_maximum_fusion.2), channel_id=1, source_target_pairs={{0,2},{1,3},{2,0},{3,1},{4,6},{5,7},{6,4},{7,5},{8,10},{9,11},{10,... | collective-permute-start | bytes 786440 | tf_op jit(solution)/shard_map/ppermute | solution.py:385
  24.8 7.1 %collective-permute-start.1 = (f32[2,128,256]{2,1,0:T(8,128)S(1)}, f32[2,128,256]{2,1,0:T(8,128)S(1)}, u32[]{:S(2)}, u32[]{:S(2)}) collective-permute-start(f32[2,128,256]{2,1,0:T(8,128)S(1)} %pad_maximum_fusion.1.refs_1_.refs_4_.refs_6_), channel_id=1, source_target_pairs={{0,1},{1,0},{2,3},{3,2},{4,5},{5,4},{6,7},{7,6},{8,9},{9,8},{10,11... | collective-permute-start | bytes 786440 | tf_op jit(solution)/shard_map/ppermute | solution.py:385
  24.9 13.3 %collective-permute-start.6 = (f32[6,128,256]{2,1,0:T(8,128)S(1)}, f32[6,128,256]{2,1,0:T(8,128)S(1)}, u32[]{:S(2)}, u32[]{:S(2)}) collective-permute-start(f32[6,128,256]{2,1,0:T(8,128)S(1)} %pad_maximum_fusion.refs_2_.refs_4_), channel_id=1, source_target_pairs={{0,1},{1,0},{2,3},{3,2},{4,5},{5,4},{6,7},{7,6},{8,9},{9,8},{10,11... | collective-permute-start | bytes 2359304 | tf_op jit(solution)/shard_map/ppermute | solution.py:385
  31.3 6.4 %collective-permute-start.11 = (f32[2,128,256]{2,1,0:T(8,128)S(1)}, f32[2,128,256]{2,1,0:T(8,128)S(1)}, u32[]{:S(2)}, u32[]{:S(2)}) collective-permute-start(f32[2,128,256]{2,1,0:T(8,128)S(1)} %get-tuple-element.45), channel_id=1, source_target_pairs={{0,2},{1,5},{2,0},{3,7},{4,6},{5,1},{6,4},{7,3},{8,10},{9,13},{10,... | collective-permute-start | bytes 786440 | tf_op jit(solution)/shard_map/ppermute | solution.py:385
  31.9 16.1 %collective-permute-start.10 = (f32[6,128,256]{2,1,0:T(8,128)S(1)}, f32[6,128,256]{2,1,0:T(8,128)S(1)}, u32[]{:S(2)}, u32[]{:S(2)}) collective-permute-start(f32[6,128,256]{2,1,0:T(8,128)S(1)} %get-tuple-element.46.refs_2_), channel_id=1, source_target_pairs={{0,1},{1,0},{2,3},{3,2},{4,5},{5,4},{6,7},{7,6},{8,9},{9,8},{10,11... | collective-permute-start | bytes 2359304 | tf_op jit(solution)/shard_map/ppermute | solution.py:385
  37.7 15.7 %collective-permute-start.12 = (f32[2,128,256]{2,1,0:T(8,128)S(1)}, f32[2,128,256]{2,1,0:T(8,128)S(1)}, u32[]{:S(2)}, u32[]{:S(2)}) collective-permute-start(f32[2,128,256]{2,1,0:T(8,128)S(1)} %collective-permute-done.11.refs_2_.refs_8_), channel_id=1, source_target_pairs={{0,1},{1,0},{2,3},{3,2},{4,5},{5,4},{6,7},{7,6},{8,9},{9,8},{10,11... | collective-permute-start | bytes 786440 | tf_op jit(solution)/shard_map/ppermute | solution.py:385
  56.5 11.4 %collective-permute-start.15 = (f32[4,128,256]{2,1,0:T(8,128)S(1)}, f32[4,128,256]{2,1,0:T(8,128)S(1)}, u32[]{:S(2)}, u32[]{:S(2)}) collective-permute-start(f32[4,128,256]{2,1,0:T(8,128)S(1)} %get-tuple-element.32), channel_id=1, source_target_pairs={{0,1},{1,0},{2,3},{3,2},{4,5},{5,4},{6,7},{7,6},{8,9},{9,8},{10,11... | collective-permute-start | bytes 1572872 | tf_op jit(solution)/shard_map/ppermute | solution.py:385
  67.3 3.8 %collective-permute-start.14 = (f32[4,128,256]{2,1,0:T(8,128)S(1)}, f32[4,128,256]{2,1,0:T(8,128)S(1)}, u32[]{:S(2)}, u32[]{:S(2)}) collective-permute-start(f32[4,128,256]{2,1,0:T(8,128)S(1)} %get-tuple-element.30), channel_id=1, source_target_pairs={{0,1},{1,0},{2,3},{3,2},{4,5},{5,4},{6,7},{7,6},{8,9},{9,8},{10,11... | collective-permute-start | bytes 1572872 | tf_op jit(solution)/shard_map/ppermute | solution.py:385
  67.3 10.4 %collective-permute-start.22 = (f32[4,128,256]{2,1,0:T(8,128)S(1)}, f32[4,128,256]{2,1,0:T(8,128)S(1)}, u32[]{:S(2)}, u32[]{:S(2)}) collective-permute-start(f32[4,128,256]{2,1,0:T(8,128)S(1)} %get-tuple-element.36), channel_id=1, source_target_pairs={{0,1},{1,0},{2,3},{3,2},{4,5},{5,4},{6,7},{7,6},{8,9},{9,8},{10,11... | collective-permute-start | bytes 1572872 | tf_op jit(solution)/shard_map/ppermute | solution.py:385
  68.0 6.4 %collective-permute-start.16 = (f32[2,128,256]{2,1,0:T(8,128)S(1)}, f32[2,128,256]{2,1,0:T(8,128)S(1)}, u32[]{:S(2)}, u32[]{:S(2)}) collective-permute-start(f32[2,128,256]{2,1,0:T(8,128)S(1)} %get-tuple-element.41), channel_id=1, source_target_pairs={{0,2},{1,5},{2,0},{3,7},{4,6},{5,1},{6,4},{7,3},{8,10},{9,13},{10,... | collective-permute-start | bytes 786440 | tf_op jit(solution)/shard_map/ppermute | solution.py:385
  68.9 10.1 %collective-permute-start.13 = (f32[2,128,256]{2,1,0:T(8,128)S(1)}, f32[2,128,256]{2,1,0:T(8,128)S(1)}, u32[]{:S(2)}, u32[]{:S(2)}) collective-permute-start(f32[2,128,256]{2,1,0:T(8,128)S(1)} %get-tuple-element.28), channel_id=1, source_target_pairs={{0,1},{1,0},{2,3},{3,2},{4,5},{5,4},{6,7},{7,6},{8,9},{9,8},{10,11... | collective-permute-start | bytes 786440 | tf_op jit(solution)/shard_map/ppermute | solution.py:385
  68.9 9.0 %collective-permute-start.23 = (f32[2,128,256]{2,1,0:T(8,128)S(1)}, f32[2,128,256]{2,1,0:T(8,128)S(1)}, u32[]{:S(2)}, u32[]{:S(2)}) collective-permute-start(f32[2,128,256]{2,1,0:T(8,128)S(1)} %get-tuple-element.42), channel_id=1, source_target_pairs={{0,2},{1,5},{2,0},{3,7},{4,6},{5,1},{6,4},{7,3},{8,10},{9,13},{10,... | collective-permute-start | bytes 786440 | tf_op jit(solution)/shard_map/ppermute | solution.py:385
  74.5 8.4 %collective-permute-start.17 = (f32[2,128,256]{2,1,0:T(8,128)S(1)}, f32[2,128,256]{2,1,0:T(8,128)S(1)}, u32[]{:S(2)}, u32[]{:S(2)}) collective-permute-start(f32[2,128,256]{2,1,0:T(8,128)S(1)} %get-tuple-element.37), channel_id=1, source_target_pairs={{0,4},{1,5},{2,6},{3,7},{4,0},{5,1},{6,2},{7,3},{8,12},{9,13},{10,... | collective-permute-start | bytes 786440 | tf_op jit(solution)/shard_map/ppermute | solution.py:385
  75.8 9.2 %collective-permute-start.18 = (f32[2,128,256]{2,1,0:T(8,128)S(1)}, f32[2,128,256]{2,1,0:T(8,128)S(1)}, u32[]{:S(2)}, u32[]{:S(2)}) collective-permute-start(f32[2,128,256]{2,1,0:T(8,128)S(1)} %get-tuple-element.38), channel_id=1, source_target_pairs={{0,2},{1,3},{2,0},{3,1},{4,6},{5,7},{6,4},{7,5},{8,10},{9,11},{10,... | collective-permute-start | bytes 786440 | tf_op jit(solution)/shard_map/ppermute | solution.py:385
  77.8 10.2 %collective-permute-start.21 = (f32[2,128,256]{2,1,0:T(8,128)S(1)}, f32[2,128,256]{2,1,0:T(8,128)S(1)}, u32[]{:S(2)}, u32[]{:S(2)}) collective-permute-start(f32[2,128,256]{2,1,0:T(8,128)S(1)} %get-tuple-element.34), channel_id=1, source_target_pairs={{0,1},{1,0},{2,3},{3,2},{4,5},{5,4},{6,7},{7,6},{8,9},{9,8},{10,11... | collective-permute-start | bytes 786440 | tf_op jit(solution)/shard_map/ppermute | solution.py:385
  77.9 10.0 %collective-permute-start.24 = (f32[2,128,256]{2,1,0:T(8,128)S(1)}, f32[2,128,256]{2,1,0:T(8,128)S(1)}, u32[]{:S(2)}, u32[]{:S(2)}) collective-permute-start(f32[2,128,256]{2,1,0:T(8,128)S(1)} %get-tuple-element.39), channel_id=1, source_target_pairs={{0,4},{1,5},{2,6},{3,7},{4,0},{5,1},{6,2},{7,3},{8,12},{9,13},{10,... | collective-permute-start | bytes 786440 | tf_op jit(solution)/shard_map/ppermute | solution.py:385
  78.9 9.9 %collective-permute-start.25 = (f32[2,128,256]{2,1,0:T(8,128)S(1)}, f32[2,128,256]{2,1,0:T(8,128)S(1)}, u32[]{:S(2)}, u32[]{:S(2)}) collective-permute-start(f32[2,128,256]{2,1,0:T(8,128)S(1)} %get-tuple-element.40), channel_id=1, source_target_pairs={{0,2},{1,3},{2,0},{3,1},{4,6},{5,7},{6,4},{7,5},{8,10},{9,11},{10,... | collective-permute-start | bytes 786440 | tf_op jit(solution)/shard_map/ppermute | solution.py:385
  85.0 7.0 %collective-permute-start.20 = (f32[128,256]{1,0:T(8,128)S(1)}, f32[128,256]{1,0:T(8,128)S(1)}, u32[]{:S(2)}, u32[]{:S(2)}) collective-permute-start(f32[128,256]{1,0:T(8,128)S(1)} %get-tuple-element.43), channel_id=1, source_target_pairs={{0,24},{1,25},{2,26},{3,27},{4,28},{5,29},{6,30},{7,31},{8,16},{9,... | collective-permute-start | bytes 393224 | tf_op jit(solution)/shard_map/ppermute | solution.py:385
  87.4 8.9 %collective-permute-start.19 = (f32[128,256]{1,0:T(8,128)S(1)}, f32[128,256]{1,0:T(8,128)S(1)}, u32[]{:S(2)}, u32[]{:S(2)}) collective-permute-start(f32[128,256]{1,0:T(8,128)S(1)} %get-tuple-element.44), channel_id=1, source_target_pairs={{0,16},{1,17},{2,18},{3,19},{4,20},{5,21},{6,22},{7,23},{8,24},{9,... | collective-permute-start | bytes 393224 | tf_op jit(solution)/shard_map/ppermute | solution.py:385
  88.9 7.6 %collective-permute-start.26 = (f32[128,256]{1,0:T(8,128)S(1)}, f32[128,256]{1,0:T(8,128)S(1)}, u32[]{:S(2)}, u32[]{:S(2)}) collective-permute-start(f32[128,256]{1,0:T(8,128)S(1)} %slice_bitcast_fusion), channel_id=1, source_target_pairs={{0,8},{1,9},{2,10},{3,11},{4,12},{5,13},{6,14},{7,15},{8,0},{9,1},... | collective-permute-start | bytes 393224 | tf_op jit(solution)/shard_map/ppermute | solution.py:385

commit v6 on v5

--- a/solution.py
+++ b/solution.py
@@ -199,9 +199,15 @@
         return jnp.sum(before * upright(which), axis=0, keepdims=True)
 
     first = where(wave == 0, 1, 0)
-    first = where(rank(first) < tasks // 4, first, 0)
+
+    def most(which, top):
+        n = jnp.sum(which.astype(f32), axis=1, keepdims=True)
+        groups = jnp.floor(n / UNROLL) * UNROLL
+        return where(n < UNROLL, n, jnp.minimum(groups, top))
+
+    first = where(rank(first) < most(first, tasks // 4), first, 0)
     second = where(wave <= 1, 1 - first, 0)
-    second = where(rank(second) < tasks * 3 // 8, second, 0)
+    second = where(rank(second) < most(second, tasks * 3 // 8), second, 0)
     late = where(urgent > 0, jnp.maximum(wave, 2), 4)
     stage = where(first > 0, 0, where(second > 0, 1, late))
     stage_up = upright(stage)
@@ -305,31 +311,39 @@
     def rows(p):
         return slice(p * 2 * w, (p + 1) * 2 * w)
 
-    def one(i):
-        left, right = field(i, LEFT), field(i, RIGHT)
+    def weights(i):
         hi, lo = split(tiles[i])
         half = jnp.concatenate([hi, lo], axis=1)
-        wt = jnp.concatenate([half, half], axis=0)
-        acc = None
-        for p in range(pairs):
-            h = jnp.dot(f2[left, rows(p), :], wt, preferred_element_type=f32)
+        return jnp.concatenate([half, half], axis=0)
+
+    def several(start, n):
+        for i in range(n):
+            pltpu.make_async_copy(stacks[0].at[0, :, pl.ds(0, w)], tiles.at[start + i], sem.at[start + i]).wait()
+        kept = [weights(start + i) for i in range(n)]
+        totals, waiting = [None] * n, []
+
+        def second(i, p, h):
             hi, lo = split(h[:, :w] + h[:, w:])
             lhs = jnp.concatenate(
                 [jnp.concatenate([hi[:w], hi[w:]], axis=1), jnp.concatenate([lo[:w], lo[w:]], axis=1)], axis=0
             )
-            d = jnp.dot(lhs, f2[right, rows(p), :], preferred_element_type=f32)
-            acc = d if acc is None else acc + d
-        part = acc[:w] + acc[w:]
-        part = part[:, :w] + part[:, w:]
-        for row, column, value in ((ROW_A, PART_A, part), (ROW_B, PART_B, part.T)):
-            at, c = field(i, row), pl.ds(pl.multiple_of(field(i, column) * w, w), w)
-            sums[at, :, c] = sums[at, :, c] + value
-
-    def several(start, n):
-        for k in range(n):
-            pltpu.make_async_copy(stacks[0].at[0, :, pl.ds(0, w)], tiles.at[start + k], sem.at[start + k]).wait()
-        for k in range(n):
-            one(start + k)
+            d = jnp.dot(lhs, f2[field(start + i, RIGHT), rows(p), :], preferred_element_type=f32)
+            totals[i] = d if totals[i] is None else totals[i] + d
+
+        for p in range(pairs):
+            for i in range(n):
+                h = jnp.dot(f2[field(start + i, LEFT), rows(p), :], kept[i], preferred_element_type=f32)
+                waiting.append((i, p, h))
+                if len(waiting) > n + 2:
+                    second(*waiting.pop(0))
+        for step in waiting:
+            second(*step)
+        for i, total in enumerate(totals):
+            part = total[:w] + total[w:]
+            part = part[:, :w] + part[:, w:]
+            for row, column, value in ((ROW_A, PART_A, part), (ROW_B, PART_B, part.T)):
+                at, c = field(start + i, row), pl.ds(pl.multiple_of(field(start + i, column) * w, w), w)
+                sums[at, :, c] = sums[at, :, c] + value
 
     def many(i, carry):
         several(i * UNROLL, UNROLL)
@@ -470,7 +484,8 @@
 
     corner = corner_mine + move(corner_other, across_core)
     merged = [a + move(b, across_core) for a, b in zip(mine, others)]
-    corners = [move(corner[2 * k : 2 * k + 2], across_diagonal) for k in range(chunks)]
+    corner = move(corner, across_diagonal)
+    corners = [corner[2 * k : 2 * k + 2] for k in range(chunks)]
     total = None
     for k in range(chunks):
         sides, here = merged[k], merged[chunks + k]

time: 98.1 us -> 100 us (1.019)
  waiting for transfers between devices: 31 us -> 39 us
  starting transfers between devices: 29.8 us -> 25.6 us
  Pallas kernels: 34.8 us -> 33.2 us
    ppermute x27 -> x26, waiting for transfers between devices: 31 us -> 39 us  [shift(): return lax.ppermute(value, AXES, pairs)]
    ppermute x27 -> x26, starting transfers between devices: 29.8 us -> 25.6 us  [shift(): return lax.ppermute(value, AXES, pairs)]
    pallas_call x5, Pallas kernels: 31 us -> 29.4 us  [run_stage(): pl.pallas_call(body, in_specs=[pl.BlockSpec(memory_space=pltpu.SMEM)] + [...]
  transfers between devices with their start and end apart: 27 -> 26, of which waited for: 14 -> 14; matrix products, arithmetic and copies ran while one was open for 1% -> 1% of each run, Pallas kernels for 32% -> 30%
where the time goes in v6:
time: 100 us
  waiting for transfers between devices  39 us (39%)
  Pallas kernels  33.2 us (33%)
  starting transfers between devices  25.6 us (26%)
    ppermute x26, waiting for transfers between devices, shift(): return lax.ppermute(value, AXES, pairs)  39 us
    pallas_call x5, Pallas kernels, run_stage(): pl.pallas_call(body, in_specs=[pl.BlockSpec(memory_space=pltpu.SMEM)] + [...  29.4 us
    ppermute x26, starting transfers between devices, shift(): return lax.ppermute(value, AXES, pairs)  25.6 us
    pallas_call x1, Pallas kernels, prepare(): pl.pallas_call(functools.partial(prepare_kernel, depth, per_block, aux_co...  3.79 us
  transfers between devices with their start and end apart: 26, of which 14 were waited for; matrix products, arithmetic and copies ran while one was open for 1% of the time, Pallas kernels for 30%

profile of v6, /device:TPU:0, one launch (start us, length us, event | category | flops | bytes accessed | tf_op | source)
XLA Modules:
  0.0 100.2 jit_solution(11099750697448367326)
XLA Ops:
  0.0 3.1 %collective-permute-start = (f32[128,256]{1,0:T(8,128)}, f32[128,256]{1,0:T(8,128)S(1)}, u32[]{:S(2)}, u32[]{:S(2)}) collective-permute-start(f32[128,256]{1,0:T(8,128)} %param.8), channel_id=1, source_target_pairs={{0,8},{1,9},{2,10},{3,11},{4,12},{5,13},{6,14},{7,15},{8,0},{9,1},... | collective-permute-start | bytes 393224 | tf_op jit(solution)/shard_map/ppermute | solution.py:399
  3.1 3.8 %shard_map.82 = (s32[16,256]{1,0:T(8,128)S(1)}, bf16[6,2048,256]{2,1,0:T(8,128)(2,1)S(1)}) custom-call(s32[8,128]{1,0:T(8,128)} %bitcast.53, s32[8,128]{1,0:T(8,128)} %bitcast.54, s32[8,128]{1,0:T(8,128)} %bitcast.55, s32[8,128]{1,0:T(8,128)} %bitcast.56, s32[2,32]{1,0:T(2,128)} %bitcast.57, f32[6,2048,128]{2,1,0:T(8,128)} %bitcast.45), custom_call_target="tpu_custom_call" | custom-call | flops 3145728 | bytes 12582912 | tf_op jit(solution)/shard_map/pallas_call | solution.py:257
  6.9 0.0 collective-permute-done
  6.9 1.6 %collective-permute-start.3 = (f32[2,128,256]{2,1,0:T(8,128)S(1)}, f32[2,128,256]{2,1,0:T(8,128)S(1)}, u32[]{:S(2)}, u32[]{:S(2)}) collective-permute-start(f32[2,128,256]{2,1,0:T(8,128)S(1)} %pad_maximum_fusion.1.refs_1_.refs_4_.refs_6_), channel_id=1, source_target_pairs={{0,2},{1,3},{2,0},{3,1},{4,6},{5,7},{6,4},{7,5},{8,10},{9,11},{10,... | collective-permute-start | bytes 786440 | tf_op jit(solution)/shard_map/ppermute | solution.py:399
  8.5 1.5 %collective-permute-start.2 = (f32[2,128,256]{2,1,0:T(8,128)S(1)}, f32[2,128,256]{2,1,0:T(8,128)S(1)}, u32[]{:S(2)}, u32[]{:S(2)}) collective-permute-start(f32[2,128,256]{2,1,0:T(8,128)S(1)} %pad_maximum_fusion.1.refs_1_.refs_4_.refs_6_), channel_id=1, source_target_pairs={{0,4},{1,5},{2,6},{3,7},{4,0},{5,1},{6,2},{7,3},{8,12},{9,13},{10,... | collective-permute-start | bytes 786440 | tf_op jit(solution)/shard_map/ppermute | solution.py:399
  10.0 3.6 %collective-permute-start.5 = (f32[128,256]{1,0:T(8,128)S(1)}, f32[128,256]{1,0:T(8,128)S(1)}, u32[]{:S(2)}, u32[]{:S(2)}) collective-permute-start(f32[128,256]{1,0:T(8,128)S(1)} %copy-done.1), channel_id=1, source_target_pairs={{0,24},{1,25},{2,26},{3,27},{4,28},{5,29},{6,30},{7,31},{8,16},{9,... | collective-permute-start | bytes 393224 | tf_op jit(solution)/shard_map/ppermute | solution.py:399
  13.6 0.0 collective-permute-start.4
  13.6 1.1 %collective-permute-done.3 = f32[2,128,256]{2,1,0:T(8,128)S(1)} collective-permute-done((f32[2,128,256]{2,1,0:T(8,128)S(1)}, f32[2,128,256]{2,1,0:T(8,128)S(1)}, u32[]{:S(2)}, u32[]{:S(2)}) %collective-permute-start.3) | collective-permute-done | bytes 262176 | tf_op jit(solution)/shard_map/ppermute | solution.py:399
  14.7 1.2 %collective-permute-done.2 = f32[2,128,256]{2,1,0:T(8,128)S(1)} collective-permute-done((f32[2,128,256]{2,1,0:T(8,128)S(1)}, f32[2,128,256]{2,1,0:T(8,128)S(1)}, u32[]{:S(2)}, u32[]{:S(2)}) %collective-permute-start.2) | collective-permute-done | bytes 262176 | tf_op jit(solution)/shard_map/ppermute | solution.py:399
  16.0 0.6 collective-permute-start.7
  16.6 1.1 %collective-permute-done.5 = f32[128,256]{1,0:T(8,128)S(1)} collective-permute-done((f32[128,256]{1,0:T(8,128)S(1)}, f32[128,256]{1,0:T(8,128)S(1)}, u32[]{:S(2)}, u32[]{:S(2)}) %collective-permute-start.5) | collective-permute-done | bytes 131104 | tf_op jit(solution)/shard_map/ppermute | solution.py:399
  17.7 6.0 %collective-permute-done.4 = f32[128,256]{1,0:T(8,128)S(1)} collective-permute-done((f32[128,256]{1,0:T(8,128)S(1)}, f32[128,256]{1,0:T(8,128)S(1)}, u32[]{:S(2)}, u32[]{:S(2)}) %collective-permute-start.4) | collective-permute-done | bytes 131104 | tf_op jit(solution)/shard_map/ppermute | solution.py:399
  23.7 0.6 collective-permute-start.8
  24.3 0.5 collective-permute-start.9
  24.8 0.0 collective-permute-start.1
  24.8 0.1 pad_maximum_fusion.refs_2_.refs_4_
  24.9 0.6 collective-permute-start.6
  25.4 0.0 collective-permute-done.7
  25.5 5.5 %collective-permute-done.8 = f32[2,128,256]{2,1,0:T(8,128)S(1)} collective-permute-done((f32[2,128,256]{2,1,0:T(8,128)S(1)}, f32[2,128,256]{2,1,0:T(8,128)S(1)}, u32[]{:S(2)}, u32[]{:S(2)}) %collective-permute-start.8) | collective-permute-done | bytes 262176 | tf_op jit(solution)/shard_map/ppermute | solution.py:399
  31.0 0.2 collective-permute-done.9
  31.3 0.6 collective-permute-start.11
  31.9 0.0 collective-permute-start.10
  31.9 0.0 collective-permute-done.1.refs_2_.refs_5_.refs_7_
  31.9 3.9 %shard_map.83.refs_1_ = f32[32,128,256]{2,1,0:T(8,128)S(1)} custom-call(s32[16,256]{1,0:T(8,128)S(1)} %get-tuple-element.21.plan, bf16[6,2048,256]{2,1,0:T(8,128)(2,1)S(1)} %get-tuple-element.23.refs_0_, f32[2,128,256]{2,1,0:T(8,128)S(1)} %pad_maximum_fusion.1.refs_1_.refs_4_.refs_6_, f32[2,128,256]{2,1,0:T(8,128)S(1)} %collective-permute-done.1.refs_2_.refs_5_.refs_7_), custom_call_target="tpu_custom_call" | custom-call | flops 4294967296 | bytes 6291456 | tf_op jit(solution)/shard_map/pallas_call | solution.py:375
  35.8 1.9 %collective-permute-done.11.refs_2_.refs_8_ = f32[2,128,256]{2,1,0:T(8,128)S(1)} collective-permute-done((f32[2,128,256]{2,1,0:T(8,128)S(1)}, f32[2,128,256]{2,1,0:T(8,128)S(1)}, u32[]{:S(2)}, u32[]{:S(2)}) %collective-permute-start.11) | collective-permute-done | bytes 262176 | tf_op jit(solution)/shard_map/ppermute | solution.py:399
  37.7 0.0 collective-permute-start.12
  37.8 0.0 collective-permute-done.6.refs_3_.refs_5_
  37.8 9.2 %shard_map.84.refs_1_ = f32[32,128,256]{2,1,0:T(8,128)S(1)} custom-call(s32[16,256]{1,0:T(8,128)S(1)} %get-tuple-element.21.plan, bf16[6,2048,256]{2,1,0:T(8,128)(2,1)S(1)} %get-tuple-element.23.refs_0_, f32[32,128,256]{2,1,0:T(8,128)S(1)} %shard_map.83.refs_1_, f32[6,128,256]{2,1,0:T(8,128)S(1)} %pad_maximum_fusion.refs_2_.refs_4_, ...), custom_call_target="tpu_custom_call" | custom-call | flops 4294967296 | bytes 6291456 | tf_op jit(solution)/shard_map/pallas_call | solution.py:375
  46.9 0.0 collective-permute-done.10.refs_3_
  47.0 5.2 %shard_map.85.refs_1_ = f32[32,128,256]{2,1,0:T(8,128)S(1)} custom-call(s32[16,256]{1,0:T(8,128)S(1)} %get-tuple-element.21.plan, bf16[6,2048,256]{2,1,0:T(8,128)(2,1)S(1)} %get-tuple-element.23.refs_0_, f32[32,128,256]{2,1,0:T(8,128)S(1)} %shard_map.84.refs_1_, f32[6,128,256]{2,1,0:T(8,128)S(1)} %get-tuple-element.46.refs_2_, ...), custom_call_target="tpu_custom_call" | custom-call | flops 4294967296 | bytes 6291456 | tf_op jit(solution)/shard_map/pallas_call | solution.py:375
  52.2 0.0 collective-permute-done.12.refs_3_.refs_9_
  52.2 2.9 %shard_map.86 = (f32[32,128,256]{2,1,0:T(8,128)S(1)}, f32[4,128,256]{2,1,0:T(8,128)S(1)}, f32[4,128,256]{2,1,0:T(8,128)S(1)}) custom-call(s32[16,256]{1,0:T(8,128)S(1)} %get-tuple-element.21.plan, bf16[6,2048,256]{2,1,0:T(8,128)(2,1)S(1)} %get-tuple-element.23.refs_0_, f32[32,128,256]{2,1,0:T(8,128)S(1)} %shard_map.85.refs_1_, ...), custom_call_target="tpu_custom_call" | custom-call | flops 4294967296 | bytes 6291456 | tf_op jit(solution)/shard_map/pallas_call | solution.py:375
  55.1 1.6 %collective-permute-start.15 = (f32[4,128,256]{2,1,0:T(8,128)S(1)}, f32[4,128,256]{2,1,0:T(8,128)S(1)}, u32[]{:S(2)}, u32[]{:S(2)}) collective-permute-start(f32[4,128,256]{2,1,0:T(8,128)S(1)} %get-tuple-element.32), channel_id=1, source_target_pairs={{0,1},{1,0},{2,3},{3,2},{4,5},{5,4},{6,7},{7,6},{8,9},{9,8},{10,11... | collective-permute-start | bytes 1572872 | tf_op jit(solution)/shard_map/ppermute | solution.py:399
  56.7 8.2 %shard_map.87 = (f32[4,128,256]{2,1,0:T(8,128)S(1)}, f32[4,128,256]{2,1,0:T(8,128)S(1)}, f32[2,128,256]{2,1,0:T(8,128)S(1)}, f32[2,128,256]{2,1,0:T(8,128)S(1)},...) custom-call(s32[16,256]{1,0:T(8,128)S(1)} %get-tuple-element.21.plan, ...), custom_call_target="tpu_custom_call" | custom-call | flops 4294967296 | bytes 6291456 | tf_op jit(solution)/shard_map/pallas_call | solution.py:375
  64.9 0.1 collective-permute-start.14
  65.0 0.5 collective-permute-start.22
  65.5 0.0 collective-permute-done.15
  65.5 0.1 add.58
  65.6 3.0 %collective-permute-start.16 = (f32[4,128,256]{2,1,0:T(8,128)S(1)}, f32[4,128,256]{2,1,0:T(8,128)S(1)}, u32[]{:S(2)}, u32[]{:S(2)}) collective-permute-start(f32[4,128,256]{2,1,0:T(8,128)S(1)} %add.58), channel_id=1, source_target_pairs={{0,2},{1,5},{2,0},{3,7},{4,6},{5,1},{6,4},{7,3},{8,10},{9,13},{10,... | collective-permute-start | bytes 1572872 | tf_op jit(solution)/shard_map/ppermute | solution.py:399
  68.6 0.0 collective-permute-start.13
  68.6 0.1 add.57
  68.7 0.1 add.65
  68.7 7.0 %collective-permute-done.16 = f32[4,128,256]{2,1,0:T(8,128)S(1)} collective-permute-done((f32[4,128,256]{2,1,0:T(8,128)S(1)}, f32[4,128,256]{2,1,0:T(8,128)S(1)}, u32[]{:S(2)}, u32[]{:S(2)}) %collective-permute-start.16) | collective-permute-done | bytes 524320 | tf_op jit(solution)/shard_map/ppermute | solution.py:399
  75.7 0.1 slice_add_fusion.3
  75.8 2.7 %collective-permute-start.17 = (f32[2,128,256]{2,1,0:T(8,128)S(1)}, f32[2,128,256]{2,1,0:T(8,128)S(1)}, u32[]{:S(2)}, u32[]{:S(2)}) collective-permute-start(f32[2,128,256]{2,1,0:T(8,128)S(1)} %get-tuple-element.37), channel_id=1, source_target_pairs={{0,4},{1,5},{2,6},{3,7},{4,0},{5,1},{6,2},{7,3},{8,12},{9,13},{10,... | collective-permute-start | bytes 786440 | tf_op jit(solution)/shard_map/ppermute | solution.py:399
  78.5 2.0 %collective-permute-start.18 = (f32[2,128,256]{2,1,0:T(8,128)S(1)}, f32[2,128,256]{2,1,0:T(8,128)S(1)}, u32[]{:S(2)}, u32[]{:S(2)}) collective-permute-start(f32[2,128,256]{2,1,0:T(8,128)S(1)} %get-tuple-element.38), channel_id=1, source_target_pairs={{0,2},{1,3},{2,0},{3,1},{4,6},{5,7},{6,4},{7,5},{8,10},{9,11},{10,... | collective-permute-start | bytes 786440 | tf_op jit(solution)/shard_map/ppermute | solution.py:399
  80.5 0.0 collective-permute-start.24
  80.6 0.2 collective-permute-start.23
  80.8 2.6 %collective-permute-done.17 = f32[2,128,256]{2,1,0:T(8,128)S(1)} collective-permute-done((f32[2,128,256]{2,1,0:T(8,128)S(1)}, f32[2,128,256]{2,1,0:T(8,128)S(1)}, u32[]{:S(2)}, u32[]{:S(2)}) %collective-permute-start.17) | collective-permute-done | bytes 262176 | tf_op jit(solution)/shard_map/ppermute | solution.py:399
  83.4 4.3 %collective-permute-done.18 = f32[2,128,256]{2,1,0:T(8,128)S(1)} collective-permute-done((f32[2,128,256]{2,1,0:T(8,128)S(1)}, f32[2,128,256]{2,1,0:T(8,128)S(1)}, u32[]{:S(2)}, u32[]{:S(2)}) %collective-permute-start.18) | collective-permute-done | bytes 262176 | tf_op jit(solution)/shard_map/ppermute | solution.py:399
  87.7 0.1 add_add_fusion.1
  87.8 0.8 collective-permute-start.20
  88.6 1.3 %collective-permute-start.19 = (f32[128,256]{1,0:T(8,128)S(1)}, f32[128,256]{1,0:T(8,128)S(1)}, u32[]{:S(2)}, u32[]{:S(2)}) collective-permute-start(f32[128,256]{1,0:T(8,128)S(1)} %get-tuple-element.44), channel_id=1, source_target_pairs={{0,16},{1,17},{2,18},{3,19},{4,20},{5,21},{6,22},{7,23},{8,24},{9,... | collective-permute-start | bytes 393224 | tf_op jit(solution)/shard_map/ppermute | solution.py:399
  89.9 0.0 collective-permute-done.21
  89.9 1.7 %collective-permute-done.24 = f32[2,128,256]{2,1,0:T(8,128)S(1)} collective-permute-done((f32[2,128,256]{2,1,0:T(8,128)S(1)}, f32[2,128,256]{2,1,0:T(8,128)S(1)}, u32[]{:S(2)}, u32[]{:S(2)}) %collective-permute-start.24) | collective-permute-done | bytes 262176 | tf_op jit(solution)/shard_map/ppermute | solution.py:399
  91.6 0.0 collective-permute-done.23
  91.6 0.1 add_add_fusion
  91.7 0.8 collective-permute-start.25
  92.4 2.4 %collective-permute-done.20 = f32[128,256]{1,0:T(8,128)S(1)} collective-permute-done((f32[128,256]{1,0:T(8,128)S(1)}, f32[128,256]{1,0:T(8,128)S(1)}, u32[]{:S(2)}, u32[]{:S(2)}) %collective-permute-start.20) | collective-permute-done | bytes 131104 | tf_op jit(solution)/shard_map/ppermute | solution.py:399
  94.8 3.6 %collective-permute-done.19 = f32[128,256]{1,0:T(8,128)S(1)} collective-permute-done((f32[128,256]{1,0:T(8,128)S(1)}, f32[128,256]{1,0:T(8,128)S(1)}, u32[]{:S(2)}, u32[]{:S(2)}) %collective-permute-start.19) | collective-permute-done | bytes 131104 | tf_op jit(solution)/shard_map/ppermute | solution.py:399
  98.4 0.4 collective-permute-done.25
  98.7 0.3 fusion
  99.1 0.4 fusion.6
  99.5 0.8 copy.11
  (16 shorter events, 0.2 us)
Async XLA Ops:
  0.0 98.7 %copy-start = (f32[1024,128]{1,0:T(8,128)S(1)}, f32[1024,128]{1,0:T(8,128)}, u32[]{:S(2)}) copy-start(f32[1024,128]{1,0:T(8,128)} %param.10) | copy-start | bytes 1572868
  0.0 6.9 %copy-start.1 = (f32[128,256]{1,0:T(8,128)S(1)}, f32[128,256]{1,0:T(8,128)}, u32[]{:S(2)}) copy-start(f32[128,256]{1,0:T(8,128)} %param.8) | copy-start | bytes 393220
  0.0 6.9 %collective-permute-start = (f32[128,256]{1,0:T(8,128)}, f32[128,256]{1,0:T(8,128)S(1)}, u32[]{:S(2)}, u32[]{:S(2)}) collective-permute-start(f32[128,256]{1,0:T(8,128)} %param.8), channel_id=1, source_target_pairs={{0,8},{1,9},{2,10},{3,11},{4,12},{5,13},{6,14},{7,15},{8,0},{9,1},... | collective-permute-start | bytes 393224 | tf_op jit(solution)/shard_map/ppermute | solution.py:399
  6.9 7.8 %collective-permute-start.3 = (f32[2,128,256]{2,1,0:T(8,128)S(1)}, f32[2,128,256]{2,1,0:T(8,128)S(1)}, u32[]{:S(2)}, u32[]{:S(2)}) collective-permute-start(f32[2,128,256]{2,1,0:T(8,128)S(1)} %pad_maximum_fusion.1.refs_1_.refs_4_.refs_6_), channel_id=1, source_target_pairs={{0,2},{1,3},{2,0},{3,1},{4,6},{5,7},{6,4},{7,5},{8,10},{9,11},{10,... | collective-permute-start | bytes 786440 | tf_op jit(solution)/shard_map/ppermute | solution.py:399
  8.5 7.4 %collective-permute-start.2 = (f32[2,128,256]{2,1,0:T(8,128)S(1)}, f32[2,128,256]{2,1,0:T(8,128)S(1)}, u32[]{:S(2)}, u32[]{:S(2)}) collective-permute-start(f32[2,128,256]{2,1,0:T(8,128)S(1)} %pad_maximum_fusion.1.refs_1_.refs_4_.refs_6_), channel_id=1, source_target_pairs={{0,4},{1,5},{2,6},{3,7},{4,0},{5,1},{6,2},{7,3},{8,12},{9,13},{10,... | collective-permute-start | bytes 786440 | tf_op jit(solution)/shard_map/ppermute | solution.py:399
  10.0 7.6 %collective-permute-start.5 = (f32[128,256]{1,0:T(8,128)S(1)}, f32[128,256]{1,0:T(8,128)S(1)}, u32[]{:S(2)}, u32[]{:S(2)}) collective-permute-start(f32[128,256]{1,0:T(8,128)S(1)} %copy-done.1), channel_id=1, source_target_pairs={{0,24},{1,25},{2,26},{3,27},{4,28},{5,29},{6,30},{7,31},{8,16},{9,... | collective-permute-start | bytes 393224 | tf_op jit(solution)/shard_map/ppermute | solution.py:399
  13.6 10.0 %collective-permute-start.4 = (f32[128,256]{1,0:T(8,128)S(1)}, f32[128,256]{1,0:T(8,128)S(1)}, u32[]{:S(2)}, u32[]{:S(2)}) collective-permute-start(f32[128,256]{1,0:T(8,128)S(1)} %copy-done.1), channel_id=1, source_target_pairs={{0,16},{1,17},{2,18},{3,19},{4,20},{5,21},{6,22},{7,23},{8,24},{9,... | collective-permute-start | bytes 393224 | tf_op jit(solution)/shard_map/ppermute | solution.py:399
  16.0 9.4 %collective-permute-start.7 = (f32[2,128,256]{2,1,0:T(8,128)S(1)}, f32[2,128,256]{2,1,0:T(8,128)S(1)}, u32[]{:S(2)}, u32[]{:S(2)}) collective-permute-start(f32[2,128,256]{2,1,0:T(8,128)S(1)} %broadcast_select_fusion.1), channel_id=1, source_target_pairs={{0,2},{1,5},{2,0},{3,7},{4,6},{5,1},{6,4},{7,3},{8,10},{9,13},{10,... | collective-permute-start | bytes 786440 | tf_op jit(solution)/shard_map/ppermute | solution.py:399
  23.7 7.3 %collective-permute-start.8 = (f32[2,128,256]{2,1,0:T(8,128)S(1)}, f32[2,128,256]{2,1,0:T(8,128)S(1)}, u32[]{:S(2)}, u32[]{:S(2)}) collective-permute-start(f32[2,128,256]{2,1,0:T(8,128)S(1)} %pad_maximum_fusion.2), channel_id=1, source_target_pairs={{0,4},{1,5},{2,6},{3,7},{4,0},{5,1},{6,2},{7,3},{8,12},{9,13},{10,... | collective-permute-start | bytes 786440 | tf_op jit(solution)/shard_map/ppermute | solution.py:399
  24.3 7.0 %collective-permute-start.9 = (f32[2,128,256]{2,1,0:T(8,128)S(1)}, f32[2,128,256]{2,1,0:T(8,128)S(1)}, u32[]{:S(2)}, u32[]{:S(2)}) collective-permute-start(f32[2,128,256]{2,1,0:T(8,128)S(1)} %pad_maximum_fusion.2), channel_id=1, source_target_pairs={{0,2},{1,3},{2,0},{3,1},{4,6},{5,7},{6,4},{7,5},{8,10},{9,11},{10,... | collective-permute-start | bytes 786440 | tf_op jit(solution)/shard_map/ppermute | solution.py:399
  24.8 7.1 %collective-permute-start.1 = (f32[2,128,256]{2,1,0:T(8,128)S(1)}, f32[2,128,256]{2,1,0:T(8,128)S(1)}, u32[]{:S(2)}, u32[]{:S(2)}) collective-permute-start(f32[2,128,256]{2,1,0:T(8,128)S(1)} %pad_maximum_fusion.1.refs_1_.refs_4_.refs_6_), channel_id=1, source_target_pairs={{0,1},{1,0},{2,3},{3,2},{4,5},{5,4},{6,7},{7,6},{8,9},{9,8},{10,11... | collective-permute-start | bytes 786440 | tf_op jit(solution)/shard_map/ppermute | solution.py:399
  24.9 12.9 %collective-permute-start.6 = (f32[6,128,256]{2,1,0:T(8,128)S(1)}, f32[6,128,256]{2,1,0:T(8,128)S(1)}, u32[]{:S(2)}, u32[]{:S(2)}) collective-permute-start(f32[6,128,256]{2,1,0:T(8,128)S(1)} %pad_maximum_fusion.refs_2_.refs_4_), channel_id=1, source_target_pairs={{0,1},{1,0},{2,3},{3,2},{4,5},{5,4},{6,7},{7,6},{8,9},{9,8},{10,11... | collective-permute-start | bytes 2359304 | tf_op jit(solution)/shard_map/ppermute | solution.py:399
  31.3 6.4 %collective-permute-start.11 = (f32[2,128,256]{2,1,0:T(8,128)S(1)}, f32[2,128,256]{2,1,0:T(8,128)S(1)}, u32[]{:S(2)}, u32[]{:S(2)}) collective-permute-start(f32[2,128,256]{2,1,0:T(8,128)S(1)} %get-tuple-element.45), channel_id=1, source_target_pairs={{0,2},{1,5},{2,0},{3,7},{4,6},{5,1},{6,4},{7,3},{8,10},{9,13},{10,... | collective-permute-start | bytes 786440 | tf_op jit(solution)/shard_map/ppermute | solution.py:399
  31.9 15.1 %collective-permute-start.10 = (f32[6,128,256]{2,1,0:T(8,128)S(1)}, f32[6,128,256]{2,1,0:T(8,128)S(1)}, u32[]{:S(2)}, u32[]{:S(2)}) collective-permute-start(f32[6,128,256]{2,1,0:T(8,128)S(1)} %get-tuple-element.46.refs_2_), channel_id=1, source_target_pairs={{0,1},{1,0},{2,3},{3,2},{4,5},{5,4},{6,7},{7,6},{8,9},{9,8},{10,11... | collective-permute-start | bytes 2359304 | tf_op jit(solution)/shard_map/ppermute | solution.py:399
  37.7 14.5 %collective-permute-start.12 = (f32[2,128,256]{2,1,0:T(8,128)S(1)}, f32[2,128,256]{2,1,0:T(8,128)S(1)}, u32[]{:S(2)}, u32[]{:S(2)}) collective-permute-start(f32[2,128,256]{2,1,0:T(8,128)S(1)} %collective-permute-done.11.refs_2_.refs_8_), channel_id=1, source_target_pairs={{0,1},{1,0},{2,3},{3,2},{4,5},{5,4},{6,7},{7,6},{8,9},{9,8},{10,11... | collective-permute-start | bytes 786440 | tf_op jit(solution)/shard_map/ppermute | solution.py:399
  55.1 10.4 %collective-permute-start.15 = (f32[4,128,256]{2,1,0:T(8,128)S(1)}, f32[4,128,256]{2,1,0:T(8,128)S(1)}, u32[]{:S(2)}, u32[]{:S(2)}) collective-permute-start(f32[4,128,256]{2,1,0:T(8,128)S(1)} %get-tuple-element.32), channel_id=1, source_target_pairs={{0,1},{1,0},{2,3},{3,2},{4,5},{5,4},{6,7},{7,6},{8,9},{9,8},{10,11... | collective-permute-start | bytes 1572872 | tf_op jit(solution)/shard_map/ppermute | solution.py:399
  64.9 3.7 %collective-permute-start.14 = (f32[4,128,256]{2,1,0:T(8,128)S(1)}, f32[4,128,256]{2,1,0:T(8,128)S(1)}, u32[]{:S(2)}, u32[]{:S(2)}) collective-permute-start(f32[4,128,256]{2,1,0:T(8,128)S(1)} %get-tuple-element.30), channel_id=1, source_target_pairs={{0,1},{1,0},{2,3},{3,2},{4,5},{5,4},{6,7},{7,6},{8,9},{9,8},{10,11... | collective-permute-start | bytes 1572872 | tf_op jit(solution)/shard_map/ppermute | solution.py:399
  65.0 3.7 %collective-permute-start.22 = (f32[4,128,256]{2,1,0:T(8,128)S(1)}, f32[4,128,256]{2,1,0:T(8,128)S(1)}, u32[]{:S(2)}, u32[]{:S(2)}) collective-permute-start(f32[4,128,256]{2,1,0:T(8,128)S(1)} %get-tuple-element.36), channel_id=1, source_target_pairs={{0,1},{1,0},{2,3},{3,2},{4,5},{5,4},{6,7},{7,6},{8,9},{9,8},{10,11... | collective-permute-start | bytes 1572872 | tf_op jit(solution)/shard_map/ppermute | solution.py:399
  65.6 10.2 %collective-permute-start.16 = (f32[4,128,256]{2,1,0:T(8,128)S(1)}, f32[4,128,256]{2,1,0:T(8,128)S(1)}, u32[]{:S(2)}, u32[]{:S(2)}) collective-permute-start(f32[4,128,256]{2,1,0:T(8,128)S(1)} %add.58), channel_id=1, source_target_pairs={{0,2},{1,5},{2,0},{3,7},{4,6},{5,1},{6,4},{7,3},{8,10},{9,13},{10,... | collective-permute-start | bytes 1572872 | tf_op jit(solution)/shard_map/ppermute | solution.py:399
  68.6 12.0 %collective-permute-start.13 = (f32[2,128,256]{2,1,0:T(8,128)S(1)}, f32[2,128,256]{2,1,0:T(8,128)S(1)}, u32[]{:S(2)}, u32[]{:S(2)}) collective-permute-start(f32[2,128,256]{2,1,0:T(8,128)S(1)} %get-tuple-element.28), channel_id=1, source_target_pairs={{0,1},{1,0},{2,3},{3,2},{4,5},{5,4},{6,7},{7,6},{8,9},{9,8},{10,11... | collective-permute-start | bytes 786440 | tf_op jit(solution)/shard_map/ppermute | solution.py:399
  75.8 7.5 %collective-permute-start.17 = (f32[2,128,256]{2,1,0:T(8,128)S(1)}, f32[2,128,256]{2,1,0:T(8,128)S(1)}, u32[]{:S(2)}, u32[]{:S(2)}) collective-permute-start(f32[2,128,256]{2,1,0:T(8,128)S(1)} %get-tuple-element.37), channel_id=1, source_target_pairs={{0,4},{1,5},{2,6},{3,7},{4,0},{5,1},{6,2},{7,3},{8,12},{9,13},{10,... | collective-permute-start | bytes 786440 | tf_op jit(solution)/shard_map/ppermute | solution.py:399
  78.5 9.2 %collective-permute-start.18 = (f32[2,128,256]{2,1,0:T(8,128)S(1)}, f32[2,128,256]{2,1,0:T(8,128)S(1)}, u32[]{:S(2)}, u32[]{:S(2)}) collective-permute-start(f32[2,128,256]{2,1,0:T(8,128)S(1)} %get-tuple-element.38), channel_id=1, source_target_pairs={{0,2},{1,3},{2,0},{3,1},{4,6},{5,7},{6,4},{7,5},{8,10},{9,11},{10,... | collective-permute-start | bytes 786440 | tf_op jit(solution)/shard_map/ppermute | solution.py:399
  80.5 9.3 %collective-permute-start.21 = (f32[2,128,256]{2,1,0:T(8,128)S(1)}, f32[2,128,256]{2,1,0:T(8,128)S(1)}, u32[]{:S(2)}, u32[]{:S(2)}) collective-permute-start(f32[2,128,256]{2,1,0:T(8,128)S(1)} %get-tuple-element.34), channel_id=1, source_target_pairs={{0,1},{1,0},{2,3},{3,2},{4,5},{5,4},{6,7},{7,6},{8,9},{9,8},{10,11... | collective-permute-start | bytes 786440 | tf_op jit(solution)/shard_map/ppermute | solution.py:399
  80.5 11.0 %collective-permute-start.24 = (f32[2,128,256]{2,1,0:T(8,128)S(1)}, f32[2,128,256]{2,1,0:T(8,128)S(1)}, u32[]{:S(2)}, u32[]{:S(2)}) collective-permute-start(f32[2,128,256]{2,1,0:T(8,128)S(1)} %get-tuple-element.41), channel_id=1, source_target_pairs={{0,2},{1,3},{2,0},{3,1},{4,6},{5,7},{6,4},{7,5},{8,10},{9,11},{10,... | collective-permute-start | bytes 786440 | tf_op jit(solution)/shard_map/ppermute | solution.py:399
  80.6 11.0 %collective-permute-start.23 = (f32[2,128,256]{2,1,0:T(8,128)S(1)}, f32[2,128,256]{2,1,0:T(8,128)S(1)}, u32[]{:S(2)}, u32[]{:S(2)}) collective-permute-start(f32[2,128,256]{2,1,0:T(8,128)S(1)} %get-tuple-element.42), channel_id=1, source_target_pairs={{0,4},{1,5},{2,6},{3,7},{4,0},{5,1},{6,2},{7,3},{8,12},{9,13},{10,... | collective-permute-start | bytes 786440 | tf_op jit(solution)/shard_map/ppermute | solution.py:399
  87.8 7.0 %collective-permute-start.20 = (f32[128,256]{1,0:T(8,128)S(1)}, f32[128,256]{1,0:T(8,128)S(1)}, u32[]{:S(2)}, u32[]{:S(2)}) collective-permute-start(f32[128,256]{1,0:T(8,128)S(1)} %get-tuple-element.43), channel_id=1, source_target_pairs={{0,24},{1,25},{2,26},{3,27},{4,28},{5,29},{6,30},{7,31},{8,16},{9,... | collective-permute-start | bytes 393224 | tf_op jit(solution)/shard_map/ppermute | solution.py:399
  88.6 9.8 %collective-permute-start.19 = (f32[128,256]{1,0:T(8,128)S(1)}, f32[128,256]{1,0:T(8,128)S(1)}, u32[]{:S(2)}, u32[]{:S(2)}) collective-permute-start(f32[128,256]{1,0:T(8,128)S(1)} %get-tuple-element.44), channel_id=1, source_target_pairs={{0,16},{1,17},{2,18},{3,19},{4,20},{5,21},{6,22},{7,23},{8,24},{9,... | collective-permute-start | bytes 393224 | tf_op jit(solution)/shard_map/ppermute | solution.py:399
  91.7 7.1 %collective-permute-start.25 = (f32[128,256]{1,0:T(8,128)S(1)}, f32[128,256]{1,0:T(8,128)S(1)}, u32[]{:S(2)}, u32[]{:S(2)}) collective-permute-start(f32[128,256]{1,0:T(8,128)S(1)} %slice_bitcast_fusion), channel_id=1, source_target_pairs={{0,8},{1,9},{2,10},{3,11},{4,12},{5,13},{6,14},{7,15},{8,0},{9,1},... | collective-permute-start | bytes 393224 | tf_op jit(solution)/shard_map/ppermute | solution.py:399

commit v7 on v6

--- a/solution.py
+++ b/solution.py
@@ -198,18 +198,13 @@
     def rank(which):
         return jnp.sum(before * upright(which), axis=0, keepdims=True)
 
-    first = where(wave == 0, 1, 0)
-
-    def most(which, top):
-        n = jnp.sum(which.astype(f32), axis=1, keepdims=True)
-        groups = jnp.floor(n / UNROLL) * UNROLL
-        return where(n < UNROLL, n, jnp.minimum(groups, top))
-
-    first = where(rank(first) < most(first, tasks // 4), first, 0)
-    second = where(wave <= 1, 1 - first, 0)
-    second = where(rank(second) < most(second, tasks * 3 // 8), second, 0)
-    late = where(urgent > 0, jnp.maximum(wave, 2), 4)
-    stage = where(first > 0, 0, where(second > 0, 1, late))
+    stage = where(urgent > 0, 3, 4)
+    for known in range(3):
+        open_now = where((wave <= known) & (stage > 2), 1.0, 0.0)
+        found = jnp.sum(open_now, axis=1, keepdims=True)
+        groups = jnp.floor(found / UNROLL) * UNROLL
+        taken = jnp.minimum(where(found < UNROLL, found, groups) if known else found, tasks // 4)
+        stage = where((open_now > 0) & (rank(open_now) < taken), known, stage)
     stage_up = upright(stage)
     earlier = where(above < along, 1.0, 0.0)
     turn = jnp.sum(where(stage_up == stage.astype(f32), earlier, 0.0), axis=0, keepdims=True)
@@ -465,10 +460,9 @@
         wave = jnp.concatenate(parts) if len(parts) > 1 else parts[0]
         by_stage.append(([wave, move(wave, across_core)], [begin[stage], begin[stage] + 4 * depth]))
 
-    for known in range(2):
-        by_stage[1][known].extend(by_stage[0][known])
-        by_stage[2][known].extend(by_stage[1][known])
-    by_stage.append(tuple(one + other for one, other in zip(by_stage[2], by_stage[3])))
+    for stage in range(3):
+        by_stage[stage + 1] = [by_stage[stage][0] + by_stage[stage + 1][0], by_stage[stage][1] + by_stage[stage + 1][1]]
+    by_stage.append(by_stage[3])
     shape = (8 * depth,) + density.shape
     corner_cuts = [(at, depth) for at in (0, 4 * depth)]
     groups = [(depth + 4 * k, 4) for k in range(chunks)] + [(3 * depth + 2 * k, 2) for k in range(chunks)]

time: 100 us -> 99.5 us (level)
  waiting for transfers between devices: 39 us -> 37.6 us
    ppermute x26, waiting for transfers between devices: 39 us -> 37.6 us  [shift(): return lax.ppermute(value, AXES, pairs)]
where the time goes in v7:
time: 99.5 us; the launch traced here: 99.3 us
  waiting for transfers between devices  37.6 us (38%)
  Pallas kernels  32.7 us (33%)
  starting transfers between devices  26.5 us (27%)
    ppermute x26, waiting for transfers between devices, shift(): return lax.ppermute(value, AXES, pairs)  37.6 us
    pallas_call x5, Pallas kernels, run_stage(): pl.pallas_call(body, in_specs=[pl.BlockSpec(memory_space=pltpu.SMEM)] + [...  28.9 us
    ppermute x26, starting transfers between devices, shift(): return lax.ppermute(value, AXES, pairs)  26.5 us
    pallas_call x1, Pallas kernels, prepare(): pl.pallas_call(functools.partial(prepare_kernel, depth, per_block, aux_co...  3.79 us
  transfers between devices with their start and end apart: 26, of which 14 were waited for; matrix products, arithmetic and copies ran while one was open for 1% of the time, Pallas kernels for 30%

profile of v7, /device:TPU:0, one launch (start us, length us, event | category | flops | bytes accessed | tf_op | source)
XLA Modules:
  0.0 99.3 jit_solution(3577693414568837475)
XLA Ops:
  0.0 3.1 %collective-permute-start = (f32[128,256]{1,0:T(8,128)}, f32[128,256]{1,0:T(8,128)S(1)}, u32[]{:S(2)}, u32[]{:S(2)}) collective-permute-start(f32[128,256]{1,0:T(8,128)} %param.8), channel_id=1, source_target_pairs={{0,8},{1,9},{2,10},{3,11},{4,12},{5,13},{6,14},{7,15},{8,0},{9,1},... | collective-permute-start | bytes 393224 | tf_op jit(solution)/shard_map/ppermute | solution.py:394
  3.1 3.8 %shard_map.82 = (s32[16,256]{1,0:T(8,128)S(1)}, bf16[6,2048,256]{2,1,0:T(8,128)(2,1)S(1)}) custom-call(s32[8,128]{1,0:T(8,128)} %bitcast.53, s32[8,128]{1,0:T(8,128)} %bitcast.54, s32[8,128]{1,0:T(8,128)} %bitcast.55, s32[8,128]{1,0:T(8,128)} %bitcast.56, s32[2,32]{1,0:T(2,128)} %bitcast.57, f32[6,2048,128]{2,1,0:T(8,128)} %bitcast.45), custom_call_target="tpu_custom_call" | custom-call | flops 3145728 | bytes 12582912 | tf_op jit(solution)/shard_map/pallas_call | solution.py:252
  6.9 0.0 collective-permute-done
  6.9 1.6 %collective-permute-start.3 = (f32[2,128,256]{2,1,0:T(8,128)S(1)}, f32[2,128,256]{2,1,0:T(8,128)S(1)}, u32[]{:S(2)}, u32[]{:S(2)}) collective-permute-start(f32[2,128,256]{2,1,0:T(8,128)S(1)} %pad_maximum_fusion.1.refs_1_.refs_2_), channel_id=1, source_target_pairs={{0,2},{1,3},{2,0},{3,1},{4,6},{5,7},{6,4},{7,5},{8,10},{9,11},{10,... | collective-permute-start | bytes 786440 | tf_op jit(solution)/shard_map/ppermute | solution.py:394
  8.5 1.5 %collective-permute-start.2 = (f32[2,128,256]{2,1,0:T(8,128)S(1)}, f32[2,128,256]{2,1,0:T(8,128)S(1)}, u32[]{:S(2)}, u32[]{:S(2)}) collective-permute-start(f32[2,128,256]{2,1,0:T(8,128)S(1)} %pad_maximum_fusion.1.refs_1_.refs_2_), channel_id=1, source_target_pairs={{0,4},{1,5},{2,6},{3,7},{4,0},{5,1},{6,2},{7,3},{8,12},{9,13},{10,... | collective-permute-start | bytes 786440 | tf_op jit(solution)/shard_map/ppermute | solution.py:394
  10.0 3.6 %collective-permute-start.5 = (f32[128,256]{1,0:T(8,128)S(1)}, f32[128,256]{1,0:T(8,128)S(1)}, u32[]{:S(2)}, u32[]{:S(2)}) collective-permute-start(f32[128,256]{1,0:T(8,128)S(1)} %copy-done.1), channel_id=1, source_target_pairs={{0,24},{1,25},{2,26},{3,27},{4,28},{5,29},{6,30},{7,31},{8,16},{9,... | collective-permute-start | bytes 393224 | tf_op jit(solution)/shard_map/ppermute | solution.py:394
  13.6 0.0 collective-permute-start.4
  13.6 1.1 %collective-permute-done.3 = f32[2,128,256]{2,1,0:T(8,128)S(1)} collective-permute-done((f32[2,128,256]{2,1,0:T(8,128)S(1)}, f32[2,128,256]{2,1,0:T(8,128)S(1)}, u32[]{:S(2)}, u32[]{:S(2)}) %collective-permute-start.3) | collective-permute-done | bytes 262176 | tf_op jit(solution)/shard_map/ppermute | solution.py:394
  14.7 1.2 %collective-permute-done.2 = f32[2,128,256]{2,1,0:T(8,128)S(1)} collective-permute-done((f32[2,128,256]{2,1,0:T(8,128)S(1)}, f32[2,128,256]{2,1,0:T(8,128)S(1)}, u32[]{:S(2)}, u32[]{:S(2)}) %collective-permute-start.2) | collective-permute-done | bytes 262176 | tf_op jit(solution)/shard_map/ppermute | solution.py:394
  16.0 0.6 collective-permute-start.7
  16.6 1.1 %collective-permute-done.5 = f32[128,256]{1,0:T(8,128)S(1)} collective-permute-done((f32[128,256]{1,0:T(8,128)S(1)}, f32[128,256]{1,0:T(8,128)S(1)}, u32[]{:S(2)}, u32[]{:S(2)}) %collective-permute-start.5) | collective-permute-done | bytes 131104 | tf_op jit(solution)/shard_map/ppermute | solution.py:394
  17.7 6.0 %collective-permute-done.4 = f32[128,256]{1,0:T(8,128)S(1)} collective-permute-done((f32[128,256]{1,0:T(8,128)S(1)}, f32[128,256]{1,0:T(8,128)S(1)}, u32[]{:S(2)}, u32[]{:S(2)}) %collective-permute-start.4) | collective-permute-done | bytes 131104 | tf_op jit(solution)/shard_map/ppermute | solution.py:394
  23.7 0.6 collective-permute-start.8
  24.3 0.5 collective-permute-start.9
  24.8 0.0 collective-permute-start.1
  24.8 0.1 pad_maximum_fusion.refs_4_
  24.9 0.6 collective-permute-start.6
  25.4 0.0 collective-permute-done.7
  25.5 5.5 %collective-permute-done.8 = f32[2,128,256]{2,1,0:T(8,128)S(1)} collective-permute-done((f32[2,128,256]{2,1,0:T(8,128)S(1)}, f32[2,128,256]{2,1,0:T(8,128)S(1)}, u32[]{:S(2)}, u32[]{:S(2)}) %collective-permute-start.8) | collective-permute-done | bytes 262176 | tf_op jit(solution)/shard_map/ppermute | solution.py:394
  31.0 0.2 collective-permute-done.9
  31.3 0.6 collective-permute-start.11
  31.9 0.0 collective-permute-start.10
  31.9 0.0 collective-permute-done.1.refs_2_.refs_3_
  31.9 3.9 %shard_map.83.refs_1_ = f32[32,128,256]{2,1,0:T(8,128)S(1)} custom-call(s32[16,256]{1,0:T(8,128)S(1)} %get-tuple-element.21.plan, bf16[6,2048,256]{2,1,0:T(8,128)(2,1)S(1)} %get-tuple-element.23.refs_0_, f32[2,128,256]{2,1,0:T(8,128)S(1)} %pad_maximum_fusion.1.refs_1_.refs_2_, f32[2,128,256]{2,1,0:T(8,128)S(1)} %collective-permute-done.1.refs_2_.refs_3_), custom_call_target="tpu_custom_call" | custom-call | flops 4294967296 | bytes 6291456 | tf_op jit(solution)/shard_map/pallas_call | solution.py:370
  35.8 1.9 %collective-permute-done.11.refs_8_ = f32[2,128,256]{2,1,0:T(8,128)S(1)} collective-permute-done((f32[2,128,256]{2,1,0:T(8,128)S(1)}, f32[2,128,256]{2,1,0:T(8,128)S(1)}, u32[]{:S(2)}, u32[]{:S(2)}) %collective-permute-start.11) | collective-permute-done | bytes 262176 | tf_op jit(solution)/shard_map/ppermute | solution.py:394
  37.7 0.1 collective-permute-start.12
  37.8 0.0 collective-permute-done.6.refs_5_
  37.8 6.6 %shard_map.84.refs_1_ = f32[32,128,256]{2,1,0:T(8,128)S(1)} custom-call(s32[16,256]{1,0:T(8,128)S(1)} %get-tuple-element.21.plan, bf16[6,2048,256]{2,1,0:T(8,128)(2,1)S(1)} %get-tuple-element.23.refs_0_, f32[32,128,256]{2,1,0:T(8,128)S(1)} %shard_map.83.refs_1_, f32[2,128,256]{2,1,0:T(8,128)S(1)} %pad_maximum_fusion.1.refs_1_.refs_2_, ...), custom_call_target="tpu_custom_call" | custom-call | flops 4294967296 | bytes 6291456 | tf_op jit(solution)/shard_map/pallas_call | solution.py:370
  44.4 0.0 collective-permute-done.10.refs_7_
  44.4 6.9 %shard_map.85.refs_1_ = f32[32,128,256]{2,1,0:T(8,128)S(1)} custom-call(s32[16,256]{1,0:T(8,128)S(1)} %get-tuple-element.21.plan, bf16[6,2048,256]{2,1,0:T(8,128)(2,1)S(1)} %get-tuple-element.23.refs_0_, f32[32,128,256]{2,1,0:T(8,128)S(1)} %shard_map.84.refs_1_, f32[2,128,256]{2,1,0:T(8,128)S(1)} %pad_maximum_fusion.1.refs_1_.refs_2_, ...), custom_call_target="tpu_custom_call" | custom-call | flops 4294967296 | bytes 6291456 | tf_op jit(solution)/shard_map/pallas_call | solution.py:370
  51.3 0.0 collective-permute-done.12.refs_9_
  51.3 2.9 %shard_map.86 = (f32[32,128,256]{2,1,0:T(8,128)S(1)}, f32[4,128,256]{2,1,0:T(8,128)S(1)}, f32[4,128,256]{2,1,0:T(8,128)S(1)}) custom-call(s32[16,256]{1,0:T(8,128)S(1)} %get-tuple-element.21.plan, bf16[6,2048,256]{2,1,0:T(8,128)(2,1)S(1)} %get-tuple-element.23.refs_0_, f32[32,128,256]{2,1,0:T(8,128)S(1)} %shard_map.85.refs_1_, ...), custom_call_target="tpu_custom_call" | custom-call | flops 4294967296 | bytes 6291456 | tf_op jit(solution)/shard_map/pallas_call | solution.py:370
  54.2 2.8 %collective-permute-start.15 = (f32[4,128,256]{2,1,0:T(8,128)S(1)}, f32[4,128,256]{2,1,0:T(8,128)S(1)}, u32[]{:S(2)}, u32[]{:S(2)}) collective-permute-start(f32[4,128,256]{2,1,0:T(8,128)S(1)} %get-tuple-element.32), channel_id=1, source_target_pairs={{0,1},{1,0},{2,3},{3,2},{4,5},{5,4},{6,7},{7,6},{8,9},{9,8},{10,11... | collective-permute-start | bytes 1572872 | tf_op jit(solution)/shard_map/ppermute | solution.py:394
  57.0 8.7 %shard_map.87 = (f32[4,128,256]{2,1,0:T(8,128)S(1)}, f32[4,128,256]{2,1,0:T(8,128)S(1)}, f32[2,128,256]{2,1,0:T(8,128)S(1)}, f32[2,128,256]{2,1,0:T(8,128)S(1)},...) custom-call(s32[16,256]{1,0:T(8,128)S(1)} %get-tuple-element.21.plan, ...), custom_call_target="tpu_custom_call" | custom-call | flops 4294967296 | bytes 6291456 | tf_op jit(solution)/shard_map/pallas_call | solution.py:370
  65.7 0.1 collective-permute-start.14
  65.7 0.5 collective-permute-start.22
  66.2 0.1 add.58
  66.3 0.1 collective-permute-start.16
  66.4 0.1 collective-permute-start.13
  66.5 1.1 %collective-permute-done.14 = f32[4,128,256]{2,1,0:T(8,128)S(1)} collective-permute-done((f32[4,128,256]{2,1,0:T(8,128)S(1)}, f32[4,128,256]{2,1,0:T(8,128)S(1)}, u32[]{:S(2)}, u32[]{:S(2)}) %collective-permute-start.14) | collective-permute-done | bytes 524320 | tf_op jit(solution)/shard_map/ppermute | solution.py:394
  67.6 0.1 add.57
  67.7 0.7 collective-permute-done.22
  68.4 0.1 add.65
  68.5 7.1 %collective-permute-done.16 = f32[4,128,256]{2,1,0:T(8,128)S(1)} collective-permute-done((f32[4,128,256]{2,1,0:T(8,128)S(1)}, f32[4,128,256]{2,1,0:T(8,128)S(1)}, u32[]{:S(2)}, u32[]{:S(2)}) %collective-permute-start.16) | collective-permute-done | bytes 524320 | tf_op jit(solution)/shard_map/ppermute | solution.py:394
  75.6 0.1 slice_add_fusion.3
  75.7 0.8 collective-permute-start.17
  76.5 2.0 %collective-permute-start.18 = (f32[2,128,256]{2,1,0:T(8,128)S(1)}, f32[2,128,256]{2,1,0:T(8,128)S(1)}, u32[]{:S(2)}, u32[]{:S(2)}) collective-permute-start(f32[2,128,256]{2,1,0:T(8,128)S(1)} %get-tuple-element.38), channel_id=1, source_target_pairs={{0,2},{1,3},{2,0},{3,1},{4,6},{5,7},{6,4},{7,5},{8,10},{9,11},{10,... | collective-permute-start | bytes 786440 | tf_op jit(solution)/shard_map/ppermute | solution.py:394
  78.5 0.0 collective-permute-start.24
  78.6 1.2 %collective-permute-start.23 = (f32[2,128,256]{2,1,0:T(8,128)S(1)}, f32[2,128,256]{2,1,0:T(8,128)S(1)}, u32[]{:S(2)}, u32[]{:S(2)}) collective-permute-start(f32[2,128,256]{2,1,0:T(8,128)S(1)} %get-tuple-element.42), channel_id=1, source_target_pairs={{0,4},{1,5},{2,6},{3,7},{4,0},{5,1},{6,2},{7,3},{8,12},{9,13},{10,... | collective-permute-start | bytes 786440 | tf_op jit(solution)/shard_map/ppermute | solution.py:394
  79.8 4.9 %collective-permute-done.17 = f32[2,128,256]{2,1,0:T(8,128)S(1)} collective-permute-done((f32[2,128,256]{2,1,0:T(8,128)S(1)}, f32[2,128,256]{2,1,0:T(8,128)S(1)}, u32[]{:S(2)}, u32[]{:S(2)}) %collective-permute-start.17) | collective-permute-done | bytes 262176 | tf_op jit(solution)/shard_map/ppermute | solution.py:394
  84.7 1.0 collective-permute-done.18
  85.7 0.1 add_add_fusion.1
  85.8 1.6 %collective-permute-start.20 = (f32[128,256]{1,0:T(8,128)S(1)}, f32[128,256]{1,0:T(8,128)S(1)}, u32[]{:S(2)}, u32[]{:S(2)}) collective-permute-start(f32[128,256]{1,0:T(8,128)S(1)} %get-tuple-element.43), channel_id=1, source_target_pairs={{0,24},{1,25},{2,26},{3,27},{4,28},{5,29},{6,30},{7,31},{8,16},{9,... | collective-permute-start | bytes 393224 | tf_op jit(solution)/shard_map/ppermute | solution.py:394
  87.4 2.6 %collective-permute-start.19 = (f32[128,256]{1,0:T(8,128)S(1)}, f32[128,256]{1,0:T(8,128)S(1)}, u32[]{:S(2)}, u32[]{:S(2)}) collective-permute-start(f32[128,256]{1,0:T(8,128)S(1)} %get-tuple-element.44), channel_id=1, source_target_pairs={{0,16},{1,17},{2,18},{3,19},{4,20},{5,21},{6,22},{7,23},{8,24},{9,... | collective-permute-start | bytes 393224 | tf_op jit(solution)/shard_map/ppermute | solution.py:394
  90.0 0.0 collective-permute-done.21
  90.0 0.0 collective-permute-done.24
  90.0 0.1 add_add_fusion
  90.1 2.0 %collective-permute-start.25 = (f32[128,256]{1,0:T(8,128)S(1)}, f32[128,256]{1,0:T(8,128)S(1)}, u32[]{:S(2)}, u32[]{:S(2)}) collective-permute-start(f32[128,256]{1,0:T(8,128)S(1)} %slice_bitcast_fusion), channel_id=1, source_target_pairs={{0,8},{1,9},{2,10},{3,11},{4,12},{5,13},{6,14},{7,15},{8,0},{9,1},... | collective-permute-start | bytes 393224 | tf_op jit(solution)/shard_map/ppermute | solution.py:394
  92.1 1.7 %collective-permute-done.20 = f32[128,256]{1,0:T(8,128)S(1)} collective-permute-done((f32[128,256]{1,0:T(8,128)S(1)}, f32[128,256]{1,0:T(8,128)S(1)}, u32[]{:S(2)}, u32[]{:S(2)}) %collective-permute-start.20) | collective-permute-done | bytes 131104 | tf_op jit(solution)/shard_map/ppermute | solution.py:394
  93.7 4.1 %collective-permute-done.19 = f32[128,256]{1,0:T(8,128)S(1)} collective-permute-done((f32[128,256]{1,0:T(8,128)S(1)}, f32[128,256]{1,0:T(8,128)S(1)}, u32[]{:S(2)}, u32[]{:S(2)}) %collective-permute-start.19) | collective-permute-done | bytes 131104 | tf_op jit(solution)/shard_map/ppermute | solution.py:394
  97.8 0.0 collective-permute-done.25
  97.8 0.3 fusion
  98.1 0.4 fusion.6
  98.6 0.8 copy.11
  (16 shorter events, 0.2 us)
Async XLA Ops:
  0.0 97.8 %copy-start = (f32[1024,128]{1,0:T(8,128)S(1)}, f32[1024,128]{1,0:T(8,128)}, u32[]{:S(2)}) copy-start(f32[1024,128]{1,0:T(8,128)} %param.10) | copy-start | bytes 1572868
  0.0 6.9 %copy-start.1 = (f32[128,256]{1,0:T(8,128)S(1)}, f32[128,256]{1,0:T(8,128)}, u32[]{:S(2)}) copy-start(f32[128,256]{1,0:T(8,128)} %param.8) | copy-start | bytes 393220
  0.0 6.9 %collective-permute-start = (f32[128,256]{1,0:T(8,128)}, f32[128,256]{1,0:T(8,128)S(1)}, u32[]{:S(2)}, u32[]{:S(2)}) collective-permute-start(f32[128,256]{1,0:T(8,128)} %param.8), channel_id=1, source_target_pairs={{0,8},{1,9},{2,10},{3,11},{4,12},{5,13},{6,14},{7,15},{8,0},{9,1},... | collective-permute-start | bytes 393224 | tf_op jit(solution)/shard_map/ppermute | solution.py:394
  6.9 7.8 %collective-permute-start.3 = (f32[2,128,256]{2,1,0:T(8,128)S(1)}, f32[2,128,256]{2,1,0:T(8,128)S(1)}, u32[]{:S(2)}, u32[]{:S(2)}) collective-permute-start(f32[2,128,256]{2,1,0:T(8,128)S(1)} %pad_maximum_fusion.1.refs_1_.refs_2_), channel_id=1, source_target_pairs={{0,2},{1,3},{2,0},{3,1},{4,6},{5,7},{6,4},{7,5},{8,10},{9,11},{10,... | collective-permute-start | bytes 786440 | tf_op jit(solution)/shard_map/ppermute | solution.py:394
  8.5 7.4 %collective-permute-start.2 = (f32[2,128,256]{2,1,0:T(8,128)S(1)}, f32[2,128,256]{2,1,0:T(8,128)S(1)}, u32[]{:S(2)}, u32[]{:S(2)}) collective-permute-start(f32[2,128,256]{2,1,0:T(8,128)S(1)} %pad_maximum_fusion.1.refs_1_.refs_2_), channel_id=1, source_target_pairs={{0,4},{1,5},{2,6},{3,7},{4,0},{5,1},{6,2},{7,3},{8,12},{9,13},{10,... | collective-permute-start | bytes 786440 | tf_op jit(solution)/shard_map/ppermute | solution.py:394
  10.0 7.6 %collective-permute-start.5 = (f32[128,256]{1,0:T(8,128)S(1)}, f32[128,256]{1,0:T(8,128)S(1)}, u32[]{:S(2)}, u32[]{:S(2)}) collective-permute-start(f32[128,256]{1,0:T(8,128)S(1)} %copy-done.1), channel_id=1, source_target_pairs={{0,24},{1,25},{2,26},{3,27},{4,28},{5,29},{6,30},{7,31},{8,16},{9,... | collective-permute-start | bytes 393224 | tf_op jit(solution)/shard_map/ppermute | solution.py:394
  13.6 10.0 %collective-permute-start.4 = (f32[128,256]{1,0:T(8,128)S(1)}, f32[128,256]{1,0:T(8,128)S(1)}, u32[]{:S(2)}, u32[]{:S(2)}) collective-permute-start(f32[128,256]{1,0:T(8,128)S(1)} %copy-done.1), channel_id=1, source_target_pairs={{0,16},{1,17},{2,18},{3,19},{4,20},{5,21},{6,22},{7,23},{8,24},{9,... | collective-permute-start | bytes 393224 | tf_op jit(solution)/shard_map/ppermute | solution.py:394
  16.0 9.4 %collective-permute-start.7 = (f32[2,128,256]{2,1,0:T(8,128)S(1)}, f32[2,128,256]{2,1,0:T(8,128)S(1)}, u32[]{:S(2)}, u32[]{:S(2)}) collective-permute-start(f32[2,128,256]{2,1,0:T(8,128)S(1)} %broadcast_select_fusion.1), channel_id=1, source_target_pairs={{0,2},{1,5},{2,0},{3,7},{4,6},{5,1},{6,4},{7,3},{8,10},{9,13},{10,... | collective-permute-start | bytes 786440 | tf_op jit(solution)/shard_map/ppermute | solution.py:394
  23.7 7.3 %collective-permute-start.8 = (f32[2,128,256]{2,1,0:T(8,128)S(1)}, f32[2,128,256]{2,1,0:T(8,128)S(1)}, u32[]{:S(2)}, u32[]{:S(2)}) collective-permute-start(f32[2,128,256]{2,1,0:T(8,128)S(1)} %pad_maximum_fusion.2), channel_id=1, source_target_pairs={{0,4},{1,5},{2,6},{3,7},{4,0},{5,1},{6,2},{7,3},{8,12},{9,13},{10,... | collective-permute-start | bytes 786440 | tf_op jit(solution)/shard_map/ppermute | solution.py:394
  24.3 7.0 %collective-permute-start.9 = (f32[2,128,256]{2,1,0:T(8,128)S(1)}, f32[2,128,256]{2,1,0:T(8,128)S(1)}, u32[]{:S(2)}, u32[]{:S(2)}) collective-permute-start(f32[2,128,256]{2,1,0:T(8,128)S(1)} %pad_maximum_fusion.2), channel_id=1, source_target_pairs={{0,2},{1,3},{2,0},{3,1},{4,6},{5,7},{6,4},{7,5},{8,10},{9,11},{10,... | collective-permute-start | bytes 786440 | tf_op jit(solution)/shard_map/ppermute | solution.py:394
  24.8 7.1 %collective-permute-start.1 = (f32[2,128,256]{2,1,0:T(8,128)S(1)}, f32[2,128,256]{2,1,0:T(8,128)S(1)}, u32[]{:S(2)}, u32[]{:S(2)}) collective-permute-start(f32[2,128,256]{2,1,0:T(8,128)S(1)} %pad_maximum_fusion.1.refs_1_.refs_2_), channel_id=1, source_target_pairs={{0,1},{1,0},{2,3},{3,2},{4,5},{5,4},{6,7},{7,6},{8,9},{9,8},{10,11... | collective-permute-start | bytes 786440 | tf_op jit(solution)/shard_map/ppermute | solution.py:394
  24.9 13.0 %collective-permute-start.6 = (f32[6,128,256]{2,1,0:T(8,128)S(1)}, f32[6,128,256]{2,1,0:T(8,128)S(1)}, u32[]{:S(2)}, u32[]{:S(2)}) collective-permute-start(f32[6,128,256]{2,1,0:T(8,128)S(1)} %pad_maximum_fusion.refs_4_), channel_id=1, source_target_pairs={{0,1},{1,0},{2,3},{3,2},{4,5},{5,4},{6,7},{7,6},{8,9},{9,8},{10,11... | collective-permute-start | bytes 2359304 | tf_op jit(solution)/shard_map/ppermute | solution.py:394
  31.3 6.4 %collective-permute-start.11 = (f32[2,128,256]{2,1,0:T(8,128)S(1)}, f32[2,128,256]{2,1,0:T(8,128)S(1)}, u32[]{:S(2)}, u32[]{:S(2)}) collective-permute-start(f32[2,128,256]{2,1,0:T(8,128)S(1)} %get-tuple-element.45), channel_id=1, source_target_pairs={{0,2},{1,5},{2,0},{3,7},{4,6},{5,1},{6,4},{7,3},{8,10},{9,13},{10,... | collective-permute-start | bytes 786440 | tf_op jit(solution)/shard_map/ppermute | solution.py:394
  31.9 12.5 %collective-permute-start.10 = (f32[6,128,256]{2,1,0:T(8,128)S(1)}, f32[6,128,256]{2,1,0:T(8,128)S(1)}, u32[]{:S(2)}, u32[]{:S(2)}) collective-permute-start(f32[6,128,256]{2,1,0:T(8,128)S(1)} %get-tuple-element.46.refs_6_), channel_id=1, source_target_pairs={{0,1},{1,0},{2,3},{3,2},{4,5},{5,4},{6,7},{7,6},{8,9},{9,8},{10,11... | collective-permute-start | bytes 2359304 | tf_op jit(solution)/shard_map/ppermute | solution.py:394
  37.7 13.5 %collective-permute-start.12 = (f32[2,128,256]{2,1,0:T(8,128)S(1)}, f32[2,128,256]{2,1,0:T(8,128)S(1)}, u32[]{:S(2)}, u32[]{:S(2)}) collective-permute-start(f32[2,128,256]{2,1,0:T(8,128)S(1)} %collective-permute-done.11.refs_8_), channel_id=1, source_target_pairs={{0,1},{1,0},{2,3},{3,2},{4,5},{5,4},{6,7},{7,6},{8,9},{9,8},{10,11... | collective-permute-start | bytes 786440 | tf_op jit(solution)/shard_map/ppermute | solution.py:394
  54.2 12.0 %collective-permute-start.15 = (f32[4,128,256]{2,1,0:T(8,128)S(1)}, f32[4,128,256]{2,1,0:T(8,128)S(1)}, u32[]{:S(2)}, u32[]{:S(2)}) collective-permute-start(f32[4,128,256]{2,1,0:T(8,128)S(1)} %get-tuple-element.32), channel_id=1, source_target_pairs={{0,1},{1,0},{2,3},{3,2},{4,5},{5,4},{6,7},{7,6},{8,9},{9,8},{10,11... | collective-permute-start | bytes 1572872 | tf_op jit(solution)/shard_map/ppermute | solution.py:394
  65.7 2.0 %collective-permute-start.14 = (f32[4,128,256]{2,1,0:T(8,128)S(1)}, f32[4,128,256]{2,1,0:T(8,128)S(1)}, u32[]{:S(2)}, u32[]{:S(2)}) collective-permute-start(f32[4,128,256]{2,1,0:T(8,128)S(1)} %get-tuple-element.30), channel_id=1, source_target_pairs={{0,1},{1,0},{2,3},{3,2},{4,5},{5,4},{6,7},{7,6},{8,9},{9,8},{10,11... | collective-permute-start | bytes 1572872 | tf_op jit(solution)/shard_map/ppermute | solution.py:394
  65.7 2.6 %collective-permute-start.22 = (f32[4,128,256]{2,1,0:T(8,128)S(1)}, f32[4,128,256]{2,1,0:T(8,128)S(1)}, u32[]{:S(2)}, u32[]{:S(2)}) collective-permute-start(f32[4,128,256]{2,1,0:T(8,128)S(1)} %get-tuple-element.36), channel_id=1, source_target_pairs={{0,1},{1,0},{2,3},{3,2},{4,5},{5,4},{6,7},{7,6},{8,9},{9,8},{10,11... | collective-permute-start | bytes 1572872 | tf_op jit(solution)/shard_map/ppermute | solution.py:394
  66.3 9.2 %collective-permute-start.16 = (f32[4,128,256]{2,1,0:T(8,128)S(1)}, f32[4,128,256]{2,1,0:T(8,128)S(1)}, u32[]{:S(2)}, u32[]{:S(2)}) collective-permute-start(f32[4,128,256]{2,1,0:T(8,128)S(1)} %add.58), channel_id=1, source_target_pairs={{0,2},{1,5},{2,0},{3,7},{4,6},{5,1},{6,4},{7,3},{8,10},{9,13},{10,... | collective-permute-start | bytes 1572872 | tf_op jit(solution)/shard_map/ppermute | solution.py:394
  66.4 12.2 %collective-permute-start.13 = (f32[2,128,256]{2,1,0:T(8,128)S(1)}, f32[2,128,256]{2,1,0:T(8,128)S(1)}, u32[]{:S(2)}, u32[]{:S(2)}) collective-permute-start(f32[2,128,256]{2,1,0:T(8,128)S(1)} %get-tuple-element.28), channel_id=1, source_target_pairs={{0,1},{1,0},{2,3},{3,2},{4,5},{5,4},{6,7},{7,6},{8,9},{9,8},{10,11... | collective-permute-start | bytes 786440 | tf_op jit(solution)/shard_map/ppermute | solution.py:394
  75.7 9.0 %collective-permute-start.17 = (f32[2,128,256]{2,1,0:T(8,128)S(1)}, f32[2,128,256]{2,1,0:T(8,128)S(1)}, u32[]{:S(2)}, u32[]{:S(2)}) collective-permute-start(f32[2,128,256]{2,1,0:T(8,128)S(1)} %get-tuple-element.37), channel_id=1, source_target_pairs={{0,4},{1,5},{2,6},{3,7},{4,0},{5,1},{6,2},{7,3},{8,12},{9,13},{10,... | collective-permute-start | bytes 786440 | tf_op jit(solution)/shard_map/ppermute | solution.py:394
  76.5 9.2 %collective-permute-start.18 = (f32[2,128,256]{2,1,0:T(8,128)S(1)}, f32[2,128,256]{2,1,0:T(8,128)S(1)}, u32[]{:S(2)}, u32[]{:S(2)}) collective-permute-start(f32[2,128,256]{2,1,0:T(8,128)S(1)} %get-tuple-element.38), channel_id=1, source_target_pairs={{0,2},{1,3},{2,0},{3,1},{4,6},{5,7},{6,4},{7,5},{8,10},{9,11},{10,... | collective-permute-start | bytes 786440 | tf_op jit(solution)/shard_map/ppermute | solution.py:394
  78.5 11.4 %collective-permute-start.21 = (f32[2,128,256]{2,1,0:T(8,128)S(1)}, f32[2,128,256]{2,1,0:T(8,128)S(1)}, u32[]{:S(2)}, u32[]{:S(2)}) collective-permute-start(f32[2,128,256]{2,1,0:T(8,128)S(1)} %get-tuple-element.34), channel_id=1, source_target_pairs={{0,1},{1,0},{2,3},{3,2},{4,5},{5,4},{6,7},{7,6},{8,9},{9,8},{10,11... | collective-permute-start | bytes 786440 | tf_op jit(solution)/shard_map/ppermute | solution.py:394
  78.5 11.4 %collective-permute-start.24 = (f32[2,128,256]{2,1,0:T(8,128)S(1)}, f32[2,128,256]{2,1,0:T(8,128)S(1)}, u32[]{:S(2)}, u32[]{:S(2)}) collective-permute-start(f32[2,128,256]{2,1,0:T(8,128)S(1)} %get-tuple-element.41), channel_id=1, source_target_pairs={{0,2},{1,3},{2,0},{3,1},{4,6},{5,7},{6,4},{7,5},{8,10},{9,11},{10,... | collective-permute-start | bytes 786440 | tf_op jit(solution)/shard_map/ppermute | solution.py:394
  78.6 11.4 %collective-permute-start.23 = (f32[2,128,256]{2,1,0:T(8,128)S(1)}, f32[2,128,256]{2,1,0:T(8,128)S(1)}, u32[]{:S(2)}, u32[]{:S(2)}) collective-permute-start(f32[2,128,256]{2,1,0:T(8,128)S(1)} %get-tuple-element.42), channel_id=1, source_target_pairs={{0,4},{1,5},{2,6},{3,7},{4,0},{5,1},{6,2},{7,3},{8,12},{9,13},{10,... | collective-permute-start | bytes 786440 | tf_op jit(solution)/shard_map/ppermute | solution.py:394
  85.8 7.9 %collective-permute-start.20 = (f32[128,256]{1,0:T(8,128)S(1)}, f32[128,256]{1,0:T(8,128)S(1)}, u32[]{:S(2)}, u32[]{:S(2)}) collective-permute-start(f32[128,256]{1,0:T(8,128)S(1)} %get-tuple-element.43), channel_id=1, source_target_pairs={{0,24},{1,25},{2,26},{3,27},{4,28},{5,29},{6,30},{7,31},{8,16},{9,... | collective-permute-start | bytes 393224 | tf_op jit(solution)/shard_map/ppermute | solution.py:394
  87.4 10.4 %collective-permute-start.19 = (f32[128,256]{1,0:T(8,128)S(1)}, f32[128,256]{1,0:T(8,128)S(1)}, u32[]{:S(2)}, u32[]{:S(2)}) collective-permute-start(f32[128,256]{1,0:T(8,128)S(1)} %get-tuple-element.44), channel_id=1, source_target_pairs={{0,16},{1,17},{2,18},{3,19},{4,20},{5,21},{6,22},{7,23},{8,24},{9,... | collective-permute-start | bytes 393224 | tf_op jit(solution)/shard_map/ppermute | solution.py:394
  90.1 7.8 %collective-permute-start.25 = (f32[128,256]{1,0:T(8,128)S(1)}, f32[128,256]{1,0:T(8,128)S(1)}, u32[]{:S(2)}, u32[]{:S(2)}) collective-permute-start(f32[128,256]{1,0:T(8,128)S(1)} %slice_bitcast_fusion), channel_id=1, source_target_pairs={{0,8},{1,9},{2,10},{3,11},{4,12},{5,13},{6,14},{7,15},{8,0},{9,1},... | collective-permute-start | bytes 393224 | tf_op jit(solution)/shard_map/ppermute | solution.py:394
